TPU v7x, 512 devices: a whole 4x4x16 slice. The times are simulated.
512 devices in a mesh: buyers: 32 (over y, z_lo), goods: 16 (over x, z_hi, core).
Axes of the slice: x: 4, y: 4, z: 16 (z_hi: 2, z_lo: 8; z = z_hi * 8 + z_lo), core: 2. Of those that a mesh axis runs over, the one named last changes fastest.
Arguments:
- buyer_hidden: bfloat16 [40960, 1024], P('buyers', 'goods'), may hold values from -6 to 6
- goods_hidden: bfloat16 [32768, 1024], P('goods', 'buyers'), may hold values from -6 to 6
- buyer_proj: bfloat16 [1024, 128], replicated, may hold values from -0.1875 to 0.1875
- goods_proj: bfloat16 [1024, 128], replicated, may hold values from -0.1875 to 0.1875
- endowment: float32 [40960], P('buyers'), may hold values from 0.5 to 4
Outputs:
- prices: float32 [32768], P('goods')
- utility: float32 [40960], P('buyers')
All inputs are finite; a program needn't handle non-finite values.
Results may differ from a plain program's by a relative error of at most 0.0003.
The roundings to bfloat16 on the way count: a program that leaves them out, or rounds other values in their place, can miss the bound.
Values may be sent and summed in bfloat16 or wider, within the bound.
No kernel may reach another device: no remote copies, remote signals or barrier semaphores. Data moves between devices by JAX's collectives and lax.ppermute only.
A program may use at most 64 MiB of HBM per device.

v0:
```python
import functools

import jax
import jax.numpy as jnp
from jax import lax
from jax.experimental import pallas as pl
from jax.experimental.pallas import tpu as pltpu
from jax.sharding import Mesh, PartitionSpec as P

ITERS = 3
FINE = (("y", 4), ("zl", 8), ("x", 4), ("zh", 2), ("c", 2))
PLANE = ("y", "x", "c")
RING = ("zh", "zl")


E = 128
NBUY = 2560
NGOOD = 1024
LB = NBUY // 128
GT = NGOOD // 128


LOG2E = 1.4426950408889634
LN2 = 0.6931471805599453


def softplus_of(products):
    t = products * (E ** (-0.5) * LOG2E)
    u = jnp.exp2(jnp.minimum(t, 126.0))
    small = u * (LOG2E - (0.5 * LOG2E) * u)
    return jnp.maximum(t, jnp.where(u < 2.0**-8, small, jnp.log2(1.0 + u))) * LN2


def values_kernel(goods_ref, buyers_ref, money_ref, values_ref, out_ref, total, rows):
    step = pl.program_id(0)

    @pl.when(step == 0)
    def _():
        total[...] = jnp.zeros_like(total)

    for b in range(NBUY // 256):
        cols = slice(256 * b, 256 * b + 256)
        scores = lax.dot_general(
            goods_ref[...], buyers_ref[cols, :], (((1,), (1,)), ((), ())), preferred_element_type=jnp.float32
        )
        rounded = softplus_of(scores).astype(jnp.bfloat16)
        values_ref[:, cols] = rounded
        total[:, cols] += jnp.sum(rounded.astype(jnp.float32).reshape(-1, 8, 256), 0)

    @pl.when(step == pl.num_programs(0) - 1)
    def _():
        whole = jnp.sum(total[...], 0, keepdims=True)
        for b in range(LB):
            rows[b : b + 1, :] = whole[:, 128 * b : 128 * b + 128]
        rows[LB : LB + 1, :] = money_ref[...]
        for p in range(out_ref.shape[0]):
            out_ref[p] = rows[0 : LB + 1, :]


def powered(v, k):
    square = v * v if k >= 2 else None
    return {1: lambda: v, 2: lambda: square, 3: lambda: square * v, 4: lambda: square * square}[k]()


def price_kernel(k, got_ref, *refs):
    if k == 1:
        values, out_ref, money_ref, scale, sums = refs
        for y in range(4):
            for i in range(5):
                money_ref[5 * y + i : 5 * y + i + 1, :] = got_ref[8 * y + i, LB : LB + 1, :]
    else:
        money_ref, values, out_ref, scale, sums = refs
    total = got_ref[0, 0:LB, :]
    for p in range(1, got_ref.shape[0]):
        total = total + got_ref[p, 0:LB, :]
    scale[...] = money_ref[...] / total
    for q in range(GT):

        def chunk(i, _, q=q):
            at = pl.multiple_of(128 * q + 16 * i, 16)
            acc = None
            for b in range(LB):
                v = values[pl.ds(at, 16), 128 * b : 128 * b + 128].astype(jnp.float32)
                term = powered(v, k) * scale[b : b + 1, :]
                acc = term if acc is None else acc + term
            sums[pl.ds(pl.multiple_of(16 * i, 16), 16), :] = acc
            return 0

        lax.fori_loop(0, 8, chunk, 0, unroll=2)
        row = jnp.sum(sums[...].T, 0, keepdims=True)
        for p in range(out_ref.shape[0]):
            out_ref[p, q : q + 1, :] = row


def utility_kernel(k, got_ref, *refs):
    last = k == ITERS
    if last:
        before_ref, zh_ref, values, out_ref, prices_ref, inverse, spare = refs
    else:
        values, out_ref, sum_ref, inverse, spare = refs
    total = got_ref[0]
    for p in range(1, got_ref.shape[0]):
        total = total + got_ref[p]
    inverse[...] = 1.0 / total
    if last:
        spare[0:8, :] = total / before_ref[...]
        half = spare[pl.ds(pl.multiple_of(4 * zh_ref[0], 4), 4), :]
        for p in range(prices_ref.shape[0]):
            prices_ref[p] = half
    else:
        sum_ref[...] = total
    accs = tuple(jnp.zeros((8, 128), jnp.float32) for _ in range(LB))
    for q in range(GT):
        spare[...] = jnp.broadcast_to(inverse[q : q + 1, :], (128, 128)).T

        def chunk(i, accs, q=q):
            at = pl.multiple_of(128 * q + 16 * i, 16)
            c = spare[pl.ds(pl.multiple_of(16 * i, 16), 16), :]
            new = []
            for b in range(LB):
                v = values[pl.ds(at, 16), 128 * b : 128 * b + 128].astype(jnp.float32)
                term = powered(v, k + 1) * c
                new.append(accs[b] + (term[0:8] + term[8:16]))
            return tuple(new)

        accs = lax.fori_loop(0, 8, chunk, accs)
    for b in range(LB):
        spare[b : b + 1, :] = jnp.sum(accs[b], 0, keepdims=True)
    for p in range(out_ref.shape[0]):
        out_ref[p] = spare[5 * (p // 8) : 5 * (p // 8) + 5, :] if last else spare[0:LB, :]


VM = pl.BlockSpec(memory_space=pltpu.VMEM)
PARAMS = pltpu.CompilerParams(vmem_limit_bytes=16 << 20)


def values_call(goods_emb, buyer_emb, money_row):
    return pl.pallas_call(
        values_kernel,
        grid=(GT,),
        in_specs=[
            pl.BlockSpec((128, E), lambda i: (i, 0)),
            pl.BlockSpec((NBUY, E), lambda i: (0, 0)),
            pl.BlockSpec((1, 128), lambda i: (0, 0)),
        ],
        out_specs=[
            pl.BlockSpec((128, NBUY), lambda i: (i, 0)),
            pl.BlockSpec((32, LB + 1, 128), lambda i: (0, 0, 0)),
        ],
        out_shape=[
            jax.ShapeDtypeStruct((NGOOD, NBUY), jnp.bfloat16),
            jax.ShapeDtypeStruct((32, LB + 1, 128), jnp.float32),
        ],
        scratch_shapes=[pltpu.VMEM((8, NBUY), jnp.float32), pltpu.VMEM((24, 128), jnp.float32)],
        compiler_params=PARAMS,
    )(goods_emb, buyer_emb, money_row)


def price_call(k, got, values, money=None):
    payload = jax.ShapeDtypeStruct((16, GT, 128), jnp.float32)
    first = k == 1
    return pl.pallas_call(
        functools.partial(price_kernel, k),
        in_specs=[VM] * (2 if first else 3),
        out_specs=[VM, VM] if first else VM,
        out_shape=[payload, jax.ShapeDtypeStruct((LB, 128), jnp.float32)] if first else payload,
        scratch_shapes=[pltpu.VMEM((LB, 128), jnp.float32), pltpu.VMEM((128, 128), jnp.float32)],
        compiler_params=PARAMS,
    )(*((got, values) if first else (got, money, values)))


def utility_call(k, got, values, before=None, zh=None):
    last = k == ITERS
    scratch = [pltpu.VMEM((GT, 128), jnp.float32), pltpu.VMEM((128, 128), jnp.float32)]
    if last:
        return pl.pallas_call(
            functools.partial(utility_kernel, k),
            in_specs=[VM, VM, pl.BlockSpec(memory_space=pltpu.SMEM), VM],
            out_specs=[VM, VM],
            out_shape=[jax.ShapeDtypeStruct((32, 5, 128), jnp.float32), jax.ShapeDtypeStruct((4, 4, 128), jnp.float32)],
            scratch_shapes=scratch,
            compiler_params=PARAMS,
        )(got, before, zh, values)
    return pl.pallas_call(
        functools.partial(utility_kernel, k),
        in_specs=[VM, VM],
        out_specs=[VM, VM],
        out_shape=[jax.ShapeDtypeStruct((32, LB, 128), jnp.float32), jax.ShapeDtypeStruct((GT, 128), jnp.float32)],
        scratch_shapes=scratch,
        compiler_params=PARAMS,
    )(got, values)


def pack_kernel(place_ref, hidden_ref, out_ref):
    x, c = place_ref[0], place_ref[2]
    rows = hidden_ref[...].T
    for q in range(8):
        to_x, to_c = q // 2, q % 2
        at = 80 * (4 * to_x + to_c)
        part = jnp.concatenate([rows[at : at + 80], rows[at + 160 : at + 240]], 1)
        out_ref[(to_c + c) & 1, (to_x + 4 - x) & 3] = part


def half_kernel(place_ref, proj_ref, *refs):
    got, (mine_ref, other_ref, weights, both) = refs[:8], refs[8:]
    x, zh, c = place_ref[0], place_ref[1], place_ref[2]
    weights[...] = jnp.zeros_like(weights)
    total = jnp.zeros((80, 2 * E), jnp.float32)
    for q in range(8):
        dx, dc = q // 2, q % 2
        w = proj_ref[((x + 4 - dx) & 3) * 4 + zh * 2 + ((c + dc) & 1)]
        weights[q, 0:64, 0:E] = w
        weights[q, 64:128, E : 2 * E] = w
        total = total + jnp.dot(got[q][...], weights[q], preferred_element_type=jnp.float32)
    both[0] = total[:, 0:E]
    both[1] = total[:, E : 2 * E]
    mine_ref[...] = both[zh]
    other_ref[...] = both[1 - zh]


def join_kernel(mine_ref, came_ref, out_ref):
    emb = (mine_ref[...] + came_ref[...]).astype(jnp.bfloat16)
    for p in range(out_ref.shape[0]):
        out_ref[p] = emb


def turn_kernel(got_ref, out_ref):
    for s in range(4):
        rows = got_ref[s].T
        for q in range(8):
            out_ref[q, :, 32 * s : 32 * s + 32] = rows[64 * q : 64 * q + 64]


def goods_kernel(got_ref, proj_ref, out_ref):
    total = jnp.dot(got_ref[0], proj_ref[0], preferred_element_type=jnp.float32)
    for q in range(1, 8):
        total = total + jnp.dot(got_ref[q], proj_ref[q], preferred_element_type=jnp.float32)
    emb = total.astype(jnp.bfloat16)
    for p in range(out_ref.shape[0]):
        out_ref[p] = emb


def small_call(kernel, outs, *args, scratch=(), smem=0):
    return pl.pallas_call(
        kernel,
        in_specs=[pl.BlockSpec(memory_space=pltpu.SMEM)] * smem + [VM] * (len(args) - smem),
        out_specs=jax.tree.map(lambda _: VM, outs),
        out_shape=outs,
        scratch_shapes=list(scratch),
        compiler_params=PARAMS,
    )(*args)


def exchange(x, axes):
    return lax.all_to_all(x, axes, 0, 0, tiled=True)


def swap(x, axis):
    return lax.ppermute(x, axis, [(0, 1), (1, 0)])


def embeddings(buyer_hidden, goods_hidden, buyer_proj, goods_proj, place):
    bf16, f32 = jnp.bfloat16, jnp.float32
    shape = jax.ShapeDtypeStruct
    goods_part = exchange(goods_hidden.T.reshape(32, 4, 512).transpose(1, 0, 2), ("y",))
    packed = small_call(pack_kernel, shape((2, 4, 80, 128), bf16), place, buyer_hidden.T, smem=1)
    here, across = packed[0], swap(packed[1], "c")
    parts = [here[0], across[0]]
    for d in range(1, 4):
        two = lax.ppermute(jnp.stack([here[d], across[d]]), "x", [(i, (i + d) % 4) for i in range(4)])
        parts += [two[0], two[1]]
    goods_rows = exchange(small_call(turn_kernel, shape((8, 64, 128), bf16), goods_part), ("zl",))
    mine, other = small_call(
        half_kernel, (shape((80, E), f32),) * 2, place, buyer_proj.reshape(16, 64, E), *parts,
        scratch=(pltpu.VMEM((8, 128, 2 * E), bf16), pltpu.VMEM((2, 80, E), f32)), smem=1,
    )
    came = swap(other, "zh")
    goods_rows, _ = lax.optimization_barrier((goods_rows, other))
    proj = goods_proj.reshape(4, 8, 32, E).transpose(1, 0, 2, 3).reshape(8, 128, E)
    goods_own = small_call(goods_kernel, shape((16, 64, E), bf16), goods_rows, proj)
    goods_emb = exchange(goods_own, RING)
    joined = small_call(join_kernel, shape((32, 80, E), bf16), mine, came)
    joined, goods_emb = lax.optimization_barrier((joined, goods_emb))
    buyer_emb = exchange(joined, PLANE)
    return buyer_emb.reshape(-1, E), goods_emb.reshape(-1, E)


def per_device(buyer_hidden, goods_hidden, buyer_proj, goods_proj, endowment):
    x, y, zh, c = (lax.axis_index(a) for a in ("x", "y", "zh", "c"))
    place = jnp.stack([x, zh, c])
    buyer_emb, goods_emb = embeddings(buyer_hidden, goods_hidden, buyer_proj, goods_proj, place)

    mine = lax.dynamic_index_in_dim(endowment.reshape(4, 2, 160), zh, 1, keepdims=False).reshape(5, 128)
    money_row = lax.dynamic_slice(mine, (jnp.minimum(x * 2 + c, 4), 0), (1, 128))

    values, sent = values_call(goods_emb, buyer_emb, money_row)
    got = exchange(sent, PLANE)
    sent, money = price_call(1, got, values)
    for k in range(1, ITERS):
        sent, before = utility_call(k, exchange(sent, RING), values)
        got = exchange(sent, PLANE)
        sent = price_call(k + 1, got, values, money)
    sent, halves = utility_call(ITERS, exchange(sent, RING), values, before, zh.reshape(1))
    final = exchange(sent, PLANE)
    five = lambda a, axis: lax.dynamic_slice_in_dim(a, 5 * y, 5, axis)
    mine_total = jnp.sum(final, 0) * five(money, 0) / jnp.sum(five(got, 1), 0)
    other = swap(mine_total, "zh")
    prices = exchange(lax.optimization_barrier((halves, mine_total))[0], ("y",)).reshape(-1)
    first = jnp.where(zh == 0, mine_total, other).reshape(4, 160)
    second = jnp.where(zh == 0, other, mine_total).reshape(4, 160)
    utility = jnp.stack([first, second], 1).reshape(-1)
    return (prices, utility)


def solution(mesh):
    fine = Mesh(mesh.devices.reshape([n for _, n in FINE]), [a for a, _ in FINE])
    buyers, goods = ("y", "zl"), ("x", "zh", "c")
    placed = (P(buyers, goods), P(goods, buyers), P(), P(), P(buyers))
    return jax.shard_map(
        per_device, mesh=fine, in_specs=placed, out_specs=(P(goods), P(buyers)), check_vma=False
    )
```

profile of v0, /device:TPU:1, one launch (start us, length us, event | category | flops | bytes accessed | tf_op | source)
XLA Modules:
  0.0 242.4 jit_solution(4111422248437723965)
XLA Ops:
  0.6 0.0 copy-start.2
  0.6 0.1 pad_add_fusion.place_ref
  0.7 0.0 copy-start.1
  0.7 0.9 copy-done.1
  1.6 0.8 shard_map.68
  2.4 8.7 %collective-permute-start = (bf16[4,80,128]{2,1,0:T(8,128)(2,1)S(1)}, bf16[4,80,128]{2,1,0:T(8,128)(2,1)S(1)}, u32[]{:S(2)}, u32[]{:S(2)}) collective-permute-start(bf16[4,80,128]{2,1,0:T(8,128)(2,1)S(1)} %slice_bitcast_fusion), channel_id=1, source_target_pairs={{0,1},{1,0},{2,3},{3,2},{4,5},{5,4},{6,7},{7,6},{8,9},{9,8},{10,11... | collective-permute-start | bytes 245768 | tf_op jit(solution)/shard_map/ppermute | solution.py:259
  11.2 1.6 copy.14
  12.7 3.3 %all-to-all-start = ((bf16[4,32,512]{2,1,0:T(8,128)(2,1)}), bf16[4,32,512]{2,1,0:T(8,128)(2,1)S(1)}, u32[]{:S(2)}, u32[]{:S(2)}) async-start(bf16[4,32,512]{2,1,0:T(8,128)(2,1)} %bitcast.43), calls=%async_computation | async-start | bytes 262144 | tf_op jit(solution)/shard_map/all_to_all | solution.py:255
  16.1 1.0 copy.9
  17.1 0.0 collective-permute-done
  17.1 1.9 collective-permute-start.3
  19.0 1.9 collective-permute-start.2
  21.0 3.4 %collective-permute-start.1 = (bf16[2,80,128]{2,1,0:T(8,128)(2,1)S(1)}, bf16[2,80,128]{2,1,0:T(8,128)(2,1)S(1)}, u32[]{:S(2)}, u32[]{:S(2)}) collective-permute-start(bf16[2,80,128]{2,1,0:T(8,128)(2,1)S(1)} %pad_maximum_fusion), channel_id=1, source_target_pairs={{0,4},{4,8},{8,12},{12,0},{1,5},{5,9},{9,13},{13,1},{2,6},{6,10},{... | collective-permute-start | bytes 122888 | tf_op jit(solution)/shard_map/ppermute | solution.py:270
  24.3 0.0 all-to-all-done.got_ref
  24.4 1.0 shard_map.71
  25.4 9.9 %all-to-all-start.1 = ((bf16[8,64,128]{2,1,0:T(8,128)(2,1)}), bf16[8,64,128]{2,1,0:T(8,128)(2,1)S(1)}, u32[]{:S(2)}, u32[]{:S(2)}) async-start(bf16[8,64,128]{2,1,0:T(8,128)(2,1)} %shard_map.71), calls=%async_computation.1 | async-start | bytes 262144 | tf_op jit(solution)/shard_map/all_to_all | solution.py:255
  35.3 0.0 collective-permute-done.3
  35.3 0.0 collective-permute-done.2
  35.3 0.0 collective-permute-done.1
  35.3 0.0 copy-start
  35.4 0.9 copy-done
  36.3 0.8 shard_map.69
  37.2 8.4 %all-to-all-done.1.got_ref = bf16[8,64,128]{2,1,0:T(8,128)(2,1)S(1)} async-done(((bf16[8,64,128]{2,1,0:T(8,128)(2,1)}), bf16[8,64,128]{2,1,0:T(8,128)(2,1)S(1)}, u32[]{:S(2)}, u32[]{:S(2)}) %all-to-all-start.1) | async-done | bytes 131104 | tf_op jit(solution)/shard_map/all_to_all | solution.py:255
  45.6 0.9 shard_map.72
  46.5 7.4 %all-to-all-start.2 = ((bf16[16,64,128]{2,1,0:T(8,128)(2,1)}), bf16[16,64,128]{2,1,0:T(8,128)(2,1)S(1)}, u32[]{:S(2)}, u32[]{:S(2)}) async-start(bf16[16,64,128]{2,1,0:T(8,128)(2,1)} %shard_map.72), calls=%async_computation.2 | async-start | bytes 524288 | tf_op jit(solution)/shard_map/all_to_all | solution.py:255
  53.9 12.0 %collective-permute-start.4 = (f32[80,128]{1,0:T(8,128)S(1)}, f32[80,128]{1,0:T(8,128)S(1)}, u32[]{:S(2)}, u32[]{:S(2)}) collective-permute-start(f32[80,128]{1,0:T(8,128)S(1)} %get-tuple-element.18), channel_id=1, source_target_pairs={{0,2},{2,0},{1,3},{3,1},{4,6},{6,4},{5,7},{7,5},{8,10},{10,8},{9,1... | collective-permute-start | bytes 122888 | tf_op jit(solution)/shard_map/ppermute | solution.py:259
  65.9 8.2 %collective-permute-done.4.came_ref = f32[80,128]{1,0:T(8,128)S(1)} collective-permute-done((f32[80,128]{1,0:T(8,128)S(1)}, f32[80,128]{1,0:T(8,128)S(1)}, u32[]{:S(2)}, u32[]{:S(2)}) %collective-permute-start.4) | collective-permute-done | bytes 40992 | tf_op jit(solution)/shard_map/ppermute | solution.py:259
  74.1 0.9 shard_map.70
  75.0 0.0 all-to-all-done.2
  75.0 13.0 %all-to-all-start.3 = ((bf16[32,80,128]{2,1,0:T(8,128)(2,1)}), bf16[32,80,128]{2,1,0:T(8,128)(2,1)S(1)}, u32[]{:S(2)}, u32[]{:S(2)}) async-start(bf16[32,80,128]{2,1,0:T(8,128)(2,1)} %shard_map.70), calls=%async_computation.3 | async-start | bytes 1310720 | tf_op jit(solution)/shard_map/all_to_all | solution.py:255
  88.1 0.0 copy-done.2
  88.1 0.1 reshape.47
  88.2 0.1 reshape.48
  88.3 12.6 %all-to-all-done.3 = bf16[32,80,128]{2,1,0:T(8,128)(2,1)S(1)} async-done(((bf16[32,80,128]{2,1,0:T(8,128)(2,1)}), bf16[32,80,128]{2,1,0:T(8,128)(2,1)S(1)}, u32[]{:S(2)}, u32[]{:S(2)}) %all-to-all-start.3) | async-done | bytes 655392 | tf_op jit(solution)/shard_map/all_to_all | solution.py:255
  100.9 7.0 %shard_map.73 = (bf16[1024,2560]{1,0:T(8,128)(2,1)S(1)}, f32[32,21,128]{2,1,0:T(8,128)S(1)}) custom-call(bf16[1024,128]{1,0:T(8,128)(2,1)S(1)} %bitcast.45, bf16[2560,128]{1,0:T(8,128)(2,1)S(1)} %bitcast.44, f32[1,128]{1,0:T(1,128)S(1)} %constant_dynamic-slice_fusion.money_ref), custom_call_target="tpu_custom_call" | custom-call | tf_op jit(solution)/shard_map/pallas_call | solution.py:138
  107.9 13.8 %all_to_all.60.got_ref = f32[32,21,128]{2,1,0:T(8,128)S(1)} all-to-all(f32[32,21,128]{2,1,0:T(8,128)S(1)} %get-tuple-element.22), channel_id=1, replica_groups=mesh['y'=4,'zl'=8,'x'=4,'zh'=2,'c'=2] {'y','x','c'}, dimensions={0} | all-to-all | bytes 688128 | tf_op jit(solution)/shard_map/all_to_all | solution.py:255
  121.7 2.4 shard_map.74
  124.1 14.9 %all_to_all.61.got_ref = f32[16,8,128]{2,1,0:T(8,128)S(1)} all-to-all(f32[16,8,128]{2,1,0:T(8,128)S(1)} %get-tuple-element.24), channel_id=1, replica_groups=mesh['y'=4,'zl'=8,'x'=4,'zh'=2,'c'=2] {'zh','zl'}, dimensions={0} | all-to-all | bytes 131072 | tf_op jit(solution)/shard_map/all_to_all | solution.py:255
  139.0 3.3 %shard_map.75 = (f32[32,20,128]{2,1,0:T(8,128)S(1)}, f32[8,128]{1,0:T(8,128)}) custom-call(f32[16,8,128]{2,1,0:T(8,128)S(1)} %all_to_all.61.got_ref, bf16[1024,2560]{1,0:T(8,128)(2,1)S(1)} %get-tuple-element.23.refs_0_.refs_1_.refs_2_), custom_call_target="tpu_custom_call" | custom-call | tf_op jit(solution)/shard_map/pallas_call | solution.py:184
  142.4 15.4 %all_to_all.62.got_ref = f32[32,20,128]{2,1,0:T(8,128)S(1)} all-to-all(f32[32,20,128]{2,1,0:T(8,128)S(1)} %get-tuple-element.25), channel_id=1, replica_groups=mesh['y'=4,'zl'=8,'x'=4,'zh'=2,'c'=2] {'y','x','c'}, dimensions={0} | all-to-all | bytes 655360 | tf_op jit(solution)/shard_map/all_to_all | solution.py:255
  157.8 2.7 %shard_map.76 = f32[16,8,128]{2,1,0:T(8,128)S(1)} custom-call(f32[32,20,128]{2,1,0:T(8,128)S(1)} %all_to_all.62.got_ref, f32[20,128]{1,0:T(8,128)S(1)} %get-tuple-element.26.refs_0_, bf16[1024,2560]{1,0:T(8,128)(2,1)S(1)} %get-tuple-element.23.refs_0_.refs_1_.refs_2_), custom_call_target="tpu_custom_call" | custom-call | tf_op jit(solution)/shard_map/pallas_call | solution.py:162
  160.5 14.3 %all_to_all.63.got_ref = f32[16,8,128]{2,1,0:T(8,128)S(1)} all-to-all(f32[16,8,128]{2,1,0:T(8,128)S(1)} %shard_map.76), channel_id=1, replica_groups=mesh['y'=4,'zl'=8,'x'=4,'zh'=2,'c'=2] {'zh','zl'}, dimensions={0} | all-to-all | bytes 131072 | tf_op jit(solution)/shard_map/all_to_all | solution.py:255
  174.8 3.1 %shard_map.77 = (f32[32,20,128]{2,1,0:T(8,128)S(1)}, f32[8,128]{1,0:T(8,128)S(1)}) custom-call(f32[16,8,128]{2,1,0:T(8,128)S(1)} %all_to_all.63.got_ref, bf16[1024,2560]{1,0:T(8,128)(2,1)S(1)} %get-tuple-element.23.refs_0_.refs_1_.refs_2_), custom_call_target="tpu_custom_call" | custom-call | tf_op jit(solution)/shard_map/pallas_call | solution.py:184
  177.9 15.4 %all_to_all.64.got_ref = f32[32,20,128]{2,1,0:T(8,128)S(1)} all-to-all(f32[32,20,128]{2,1,0:T(8,128)S(1)} %get-tuple-element.27), channel_id=1, replica_groups=mesh['y'=4,'zl'=8,'x'=4,'zh'=2,'c'=2] {'y','x','c'}, dimensions={0} | all-to-all | bytes 655360 | tf_op jit(solution)/shard_map/all_to_all | solution.py:255
  193.3 3.0 %shard_map.78 = f32[16,8,128]{2,1,0:T(8,128)S(1)} custom-call(f32[32,20,128]{2,1,0:T(8,128)S(1)} %all_to_all.64.got_ref, f32[20,128]{1,0:T(8,128)S(1)} %get-tuple-element.26.refs_0_, bf16[1024,2560]{1,0:T(8,128)(2,1)S(1)} %get-tuple-element.23.refs_0_.refs_1_.refs_2_), custom_call_target="tpu_custom_call" | custom-call | tf_op jit(solution)/shard_map/pallas_call | solution.py:162
  196.4 14.3 %all_to_all.65.got_ref = f32[16,8,128]{2,1,0:T(8,128)S(1)} all-to-all(f32[16,8,128]{2,1,0:T(8,128)S(1)} %shard_map.78), channel_id=1, replica_groups=mesh['y'=4,'zl'=8,'x'=4,'zh'=2,'c'=2] {'zh','zl'}, dimensions={0} | all-to-all | bytes 131072 | tf_op jit(solution)/shard_map/all_to_all | solution.py:255
  210.7 3.8 %shard_map.79 = (f32[32,5,128]{2,1,0:T(8,128)}, f32[4,4,128]{2,1,0:T(4,128)}) custom-call(f32[16,8,128]{2,1,0:T(8,128)S(1)} %all_to_all.65.got_ref, f32[8,128]{1,0:T(8,128)S(1)} %get-tuple-element.28.refs_0_, s32[1]{0:T(128)} %bitcast.1.refs_1_, bf16[1024,2560]{1,0:T(8,128)(2,1)S(1)} %get-tuple-element.23.refs_0_.refs_1_.refs_2_), custom_call_target="tpu_custom_call" | custom-call | tf_op jit(solution)/shard_map/pallas_call | solution.py:176
  214.4 5.6 %all-to-all-start.10 = ((f32[32,5,128]{2,1,0:T(8,128)}), f32[32,5,128]{2,1,0:T(8,128)S(1)}, u32[]{:S(2)}, u32[]{:S(2)}) async-start(f32[32,5,128]{2,1,0:T(8,128)} %get-tuple-element.30), calls=%async_computation.10 | async-start | bytes 262144 | tf_op jit(solution)/shard_map/all_to_all | solution.py:255
  220.1 7.7 %all-to-all-done.10 = f32[32,5,128]{2,1,0:T(8,128)S(1)} async-done(((f32[32,5,128]{2,1,0:T(8,128)}), f32[32,5,128]{2,1,0:T(8,128)S(1)}, u32[]{:S(2)}, u32[]{:S(2)}) %all-to-all-start.10) | async-done | bytes 81952 | tf_op jit(solution)/shard_map/all_to_all | solution.py:255
  227.8 3.2 %collective-permute-start.5 = (f32[5,128]{1,0:T(8,128)S(1)}, f32[5,128]{1,0:T(8,128)S(1)}, u32[]{:S(2)}, u32[]{:S(2)}) collective-permute-start(f32[5,128]{1,0:T(8,128)S(1)} %multiply_divide_fusion), channel_id=1, source_target_pairs={{0,2},{2,0},{1,3},{3,1},{4,6},{6,4},{5,7},{7,5},{8,10},{10,8},{9,1... | collective-permute-start | bytes 7688 | tf_op jit(solution)/shard_map/ppermute | solution.py:259
  231.1 3.3 %all-to-all-start.11 = ((f32[4,4,128]{2,1,0:T(4,128)}), f32[4,4,128]{2,1,0:T(4,128)S(1)}, u32[]{:S(2)}, u32[]{:S(2)}) async-start(f32[4,4,128]{2,1,0:T(4,128)} %get-tuple-element.31), calls=%async_computation.11 | async-start | bytes 16384 | tf_op jit(solution)/shard_map/all_to_all | solution.py:255
  234.3 6.6 %collective-permute-done.5 = f32[5,128]{1,0:T(8,128)S(1)} collective-permute-done((f32[5,128]{1,0:T(8,128)S(1)}, f32[5,128]{1,0:T(8,128)S(1)}, u32[]{:S(2)}, u32[]{:S(2)}) %collective-permute-start.5) | collective-permute-done | bytes 2592 | tf_op jit(solution)/shard_map/ppermute | solution.py:259
  240.9 0.1 stack_reshape.8
  241.0 0.1 stack_reshape.9
  241.1 0.7 reshape.50
  241.8 0.0 all-to-all-done.11
  241.8 0.6 copy.16
  (16 shorter events, 0.2 us)
Async XLA Ops:
  0.6 87.4 %copy-start.2 = (f32[1280]{0:T(1024)S(1)}, f32[1280]{0:T(1024)}, u32[]{:S(2)}) copy-start(f32[1280]{0:T(1024)} %param.9) | copy-start | bytes 15364
  0.7 0.9 copy-start.1
  2.4 14.6 %collective-permute-start = (bf16[4,80,128]{2,1,0:T(8,128)(2,1)S(1)}, bf16[4,80,128]{2,1,0:T(8,128)(2,1)S(1)}, u32[]{:S(2)}, u32[]{:S(2)}) collective-permute-start(bf16[4,80,128]{2,1,0:T(8,128)(2,1)S(1)} %slice_bitcast_fusion), channel_id=1, source_target_pairs={{0,1},{1,0},{2,3},{3,2},{4,5},{5,4},{6,7},{7,6},{8,9},{9,8},{10,11... | collective-permute-start | bytes 245768 | tf_op jit(solution)/shard_map/ppermute | solution.py:259
  12.7 11.6 %all-to-all-start = ((bf16[4,32,512]{2,1,0:T(8,128)(2,1)}), bf16[4,32,512]{2,1,0:T(8,128)(2,1)S(1)}, u32[]{:S(2)}, u32[]{:S(2)}) async-start(bf16[4,32,512]{2,1,0:T(8,128)(2,1)} %bitcast.43), calls=%async_computation | async-start | bytes 262144 | tf_op jit(solution)/shard_map/all_to_all | solution.py:255
  17.1 18.2 %collective-permute-start.3 = (bf16[2,80,128]{2,1,0:T(8,128)(2,1)S(1)}, bf16[2,80,128]{2,1,0:T(8,128)(2,1)S(1)}, u32[]{:S(2)}, u32[]{:S(2)}) collective-permute-start(bf16[2,80,128]{2,1,0:T(8,128)(2,1)S(1)} %pad_maximum_fusion.2), channel_id=1, source_target_pairs={{0,12},{4,0},{8,4},{12,8},{1,13},{5,1},{9,5},{13,9},{2,14},{6,2},{... | collective-permute-start | bytes 122888 | tf_op jit(solution)/shard_map/ppermute | solution.py:270
  19.0 16.3 %collective-permute-start.2 = (bf16[2,80,128]{2,1,0:T(8,128)(2,1)S(1)}, bf16[2,80,128]{2,1,0:T(8,128)(2,1)S(1)}, u32[]{:S(2)}, u32[]{:S(2)}) collective-permute-start(bf16[2,80,128]{2,1,0:T(8,128)(2,1)S(1)} %pad_maximum_fusion.1), channel_id=1, source_target_pairs={{0,8},{4,12},{8,0},{12,4},{1,9},{5,13},{9,1},{13,5},{2,10},{6,14},... | collective-permute-start | bytes 122888 | tf_op jit(solution)/shard_map/ppermute | solution.py:270
  21.0 14.3 %collective-permute-start.1 = (bf16[2,80,128]{2,1,0:T(8,128)(2,1)S(1)}, bf16[2,80,128]{2,1,0:T(8,128)(2,1)S(1)}, u32[]{:S(2)}, u32[]{:S(2)}) collective-permute-start(bf16[2,80,128]{2,1,0:T(8,128)(2,1)S(1)} %pad_maximum_fusion), channel_id=1, source_target_pairs={{0,4},{4,8},{8,12},{12,0},{1,5},{5,9},{9,13},{13,1},{2,6},{6,10},{... | collective-permute-start | bytes 122888 | tf_op jit(solution)/shard_map/ppermute | solution.py:270
  25.4 20.2 %all-to-all-start.1 = ((bf16[8,64,128]{2,1,0:T(8,128)(2,1)}), bf16[8,64,128]{2,1,0:T(8,128)(2,1)S(1)}, u32[]{:S(2)}, u32[]{:S(2)}) async-start(bf16[8,64,128]{2,1,0:T(8,128)(2,1)} %shard_map.71), calls=%async_computation.1 | async-start | bytes 262144 | tf_op jit(solution)/shard_map/all_to_all | solution.py:255
  35.3 1.0 copy-start
  46.5 28.5 %all-to-all-start.2 = ((bf16[16,64,128]{2,1,0:T(8,128)(2,1)}), bf16[16,64,128]{2,1,0:T(8,128)(2,1)S(1)}, u32[]{:S(2)}, u32[]{:S(2)}) async-start(bf16[16,64,128]{2,1,0:T(8,128)(2,1)} %shard_map.72), calls=%async_computation.2 | async-start | bytes 524288 | tf_op jit(solution)/shard_map/all_to_all | solution.py:255
  53.9 20.2 %collective-permute-start.4 = (f32[80,128]{1,0:T(8,128)S(1)}, f32[80,128]{1,0:T(8,128)S(1)}, u32[]{:S(2)}, u32[]{:S(2)}) collective-permute-start(f32[80,128]{1,0:T(8,128)S(1)} %get-tuple-element.18), channel_id=1, source_target_pairs={{0,2},{2,0},{1,3},{3,1},{4,6},{6,4},{5,7},{7,5},{8,10},{10,8},{9,1... | collective-permute-start | bytes 122888 | tf_op jit(solution)/shard_map/ppermute | solution.py:259
  75.0 25.9 %all-to-all-start.3 = ((bf16[32,80,128]{2,1,0:T(8,128)(2,1)}), bf16[32,80,128]{2,1,0:T(8,128)(2,1)S(1)}, u32[]{:S(2)}, u32[]{:S(2)}) async-start(bf16[32,80,128]{2,1,0:T(8,128)(2,1)} %shard_map.70), calls=%async_computation.3 | async-start | bytes 1310720 | tf_op jit(solution)/shard_map/all_to_all | solution.py:255
  214.4 13.3 %all-to-all-start.10 = ((f32[32,5,128]{2,1,0:T(8,128)}), f32[32,5,128]{2,1,0:T(8,128)S(1)}, u32[]{:S(2)}, u32[]{:S(2)}) async-start(f32[32,5,128]{2,1,0:T(8,128)} %get-tuple-element.30), calls=%async_computation.10 | async-start | bytes 262144 | tf_op jit(solution)/shard_map/all_to_all | solution.py:255
  227.8 13.1 %collective-permute-start.5 = (f32[5,128]{1,0:T(8,128)S(1)}, f32[5,128]{1,0:T(8,128)S(1)}, u32[]{:S(2)}, u32[]{:S(2)}) collective-permute-start(f32[5,128]{1,0:T(8,128)S(1)} %multiply_divide_fusion), channel_id=1, source_target_pairs={{0,2},{2,0},{1,3},{3,1},{4,6},{6,4},{5,7},{7,5},{8,10},{10,8},{9,1... | collective-permute-start | bytes 7688 | tf_op jit(solution)/shard_map/ppermute | solution.py:259
  231.1 10.7 %all-to-all-start.11 = ((f32[4,4,128]{2,1,0:T(4,128)}), f32[4,4,128]{2,1,0:T(4,128)S(1)}, u32[]{:S(2)}, u32[]{:S(2)}) async-start(f32[4,4,128]{2,1,0:T(4,128)} %get-tuple-element.31), calls=%async_computation.11 | async-start | bytes 16384 | tf_op jit(solution)/shard_map/all_to_all | solution.py:255
where the time goes:
time: 243 us; the launch traced here: 242 us
  blocking collectives  88.1 us (36%)
  starting transfers between devices  73.6 us (30%)
  waiting for transfers between devices  43.5 us (18%)
  Pallas kernels  29.9 us (12%)
  local copies, waits for them, and re-layouts  6.08 us (3%)
    all_to_all x6, blocking collectives, exchange(): return lax.all_to_all(x, axes, 0, 0, tiled=True)  88.1 us
    all_to_all x6, starting transfers between devices, exchange(): return lax.all_to_all(x, axes, 0, 0, tiled=True)  42.5 us
    all_to_all x6, waiting for transfers between devices, exchange(): return lax.all_to_all(x, axes, 0, 0, tiled=True)  28.7 us
    ppermute x3, starting transfers between devices, swap(): return lax.ppermute(x, axis, [(0, 1), (1, 0)])  23.9 us
    ppermute x3, waiting for transfers between devices, swap(): return lax.ppermute(x, axis, [(0, 1), (1, 0)])  14.8 us
    pallas_call x3, Pallas kernels, price_call(): pl.pallas_call(functools.partial(price_kernel, k), in_specs=[VM] * (2 if...  8.13 us
    ppermute x3, starting transfers between devices, embeddings(): lax.ppermute(jnp.stack([here[d], across[d]]), 'x', [(i, (i + d) % 4) for...  7.2 us
    pallas_call x1, Pallas kernels, values_call(): pl.pallas_call(values_kernel, grid=(GT,), in_specs=[pl.BlockSpec((128, E)...  7.03 us
  transfers between devices with their start and end apart: 12, of which 5 were waited for; matrix products, arithmetic and copies ran while one was open for 2% of the time, Pallas kernels for 1%

commit v1 on v0

--- a/solution.py
+++ b/solution.py
@@ -191,35 +191,47 @@
     )(got, values)
 
 
-def pack_kernel(place_ref, hidden_ref, out_ref):
-    x, c = place_ref[0], place_ref[2]
-    rows = hidden_ref[...].T
+def pack_kernel(place_ref, hidden_ref, keep_ref, go_ref):
+    x, zh, c = place_ref[0], place_ref[1], place_ref[2]
+    rows = hidden_ref[...].astype(jnp.float32).T
+
+    def of(to_x, to_zh, to_c):
+        at = 80 * (4 * to_x + 2 * to_zh + to_c)
+        return rows[at : at + 80]
+
+    for to_x in range(4):
+        for to_zh in range(2):
+            plain = jnp.concatenate([of(to_x, to_zh, 0), of(to_x, to_zh, 1)], 1)
+            turned = jnp.concatenate([of(to_x, to_zh, 1), of(to_x, to_zh, 0)], 1)
+            part = jnp.where(c == 0, plain, turned).astype(jnp.bfloat16)
+            at = (to_x + 4 - x) & 3
+
+            @pl.when(zh == to_zh)
+            def _(at=at, part=part):
+                keep_ref[at] = part
+
+            @pl.when(zh != to_zh)
+            def _(at=at, part=part):
+                go_ref[at] = part
+
+
+def pair_kernel(mine_ref, came_ref, here_ref, across_ref):
+    for d in range(4):
+        mine, came = mine_ref[d].astype(jnp.float32), came_ref[d].astype(jnp.float32)
+        here_ref[d] = jnp.concatenate([mine[:, 0:64], came[:, 0:64]], 1).astype(jnp.bfloat16)
+        across_ref[d] = jnp.concatenate([mine[:, 64:128], came[:, 64:128]], 1).astype(jnp.bfloat16)
+
+
+def buyers_kernel(place_ref, proj_ref, *refs):
+    got, (out_ref, weights) = refs[:8], refs[8:]
+    x, zh, c = place_ref[0], place_ref[1], place_ref[2]
+    total = jnp.zeros((80, E), jnp.float32)
     for q in range(8):
-        to_x, to_c = q // 2, q % 2
-        at = 80 * (4 * to_x + to_c)
-        part = jnp.concatenate([rows[at : at + 80], rows[at + 160 : at + 240]], 1)
-        out_ref[(to_c + c) & 1, (to_x + 4 - x) & 3] = part
-
-
-def half_kernel(place_ref, proj_ref, *refs):
-    got, (mine_ref, other_ref, weights, both) = refs[:8], refs[8:]
-    x, zh, c = place_ref[0], place_ref[1], place_ref[2]
-    weights[...] = jnp.zeros_like(weights)
-    total = jnp.zeros((80, 2 * E), jnp.float32)
-    for q in range(8):
-        dx, dc = q // 2, q % 2
-        w = proj_ref[((x + 4 - dx) & 3) * 4 + zh * 2 + ((c + dc) & 1)]
-        weights[q, 0:64, 0:E] = w
-        weights[q, 64:128, E : 2 * E] = w
+        at = ((x + 4 - q // 2) & 3) * 4 + ((c + q % 2) & 1)
+        weights[q, 0:64] = proj_ref[at + 2 * zh]
+        weights[q, 64:128] = proj_ref[at + 2 - 2 * zh]
         total = total + jnp.dot(got[q][...], weights[q], preferred_element_type=jnp.float32)
-    both[0] = total[:, 0:E]
-    both[1] = total[:, E : 2 * E]
-    mine_ref[...] = both[zh]
-    other_ref[...] = both[1 - zh]
-
-
-def join_kernel(mine_ref, came_ref, out_ref):
-    emb = (mine_ref[...] + came_ref[...]).astype(jnp.bfloat16)
+    emb = total.astype(jnp.bfloat16)
     for p in range(out_ref.shape[0]):
         out_ref[p] = emb
 
@@ -260,28 +272,28 @@
 
 
 def embeddings(buyer_hidden, goods_hidden, buyer_proj, goods_proj, place):
-    bf16, f32 = jnp.bfloat16, jnp.float32
+    bf16 = jnp.bfloat16
     shape = jax.ShapeDtypeStruct
     goods_part = exchange(goods_hidden.T.reshape(32, 4, 512).transpose(1, 0, 2), ("y",))
-    packed = small_call(pack_kernel, shape((2, 4, 80, 128), bf16), place, buyer_hidden.T, smem=1)
-    here, across = packed[0], swap(packed[1], "c")
+    keep, go = small_call(pack_kernel, (shape((4, 80, 128), bf16),) * 2, place, buyer_hidden.T, smem=1)
+    came = swap(go, "zh")
+    here, across = small_call(pair_kernel, (shape((4, 80, 128), bf16),) * 2, keep, came)
+    across = swap(across, "c")
     parts = [here[0], across[0]]
     for d in range(1, 4):
-        two = lax.ppermute(jnp.stack([here[d], across[d]]), "x", [(i, (i + d) % 4) for i in range(4)])
+        two = jnp.stack([here[d], across[d]])
+        two = lax.ppermute(two, "x", [(i, (i + d) % 4) for i in range(4)])
         parts += [two[0], two[1]]
     goods_rows = exchange(small_call(turn_kernel, shape((8, 64, 128), bf16), goods_part), ("zl",))
-    mine, other = small_call(
-        half_kernel, (shape((80, E), f32),) * 2, place, buyer_proj.reshape(16, 64, E), *parts,
-        scratch=(pltpu.VMEM((8, 128, 2 * E), bf16), pltpu.VMEM((2, 80, E), f32)), smem=1,
-    )
-    came = swap(other, "zh")
-    goods_rows, _ = lax.optimization_barrier((goods_rows, other))
     proj = goods_proj.reshape(4, 8, 32, E).transpose(1, 0, 2, 3).reshape(8, 128, E)
     goods_own = small_call(goods_kernel, shape((16, 64, E), bf16), goods_rows, proj)
     goods_emb = exchange(goods_own, RING)
-    joined = small_call(join_kernel, shape((32, 80, E), bf16), mine, came)
-    joined, goods_emb = lax.optimization_barrier((joined, goods_emb))
-    buyer_emb = exchange(joined, PLANE)
+    buyer_own = small_call(
+        buyers_kernel, shape((32, 80, E), bf16), place, buyer_proj.reshape(16, 64, E), *parts,
+        scratch=(pltpu.VMEM((8, 128, E), bf16),), smem=1,
+    )
+    buyer_own, goods_emb = lax.optimization_barrier((buyer_own, goods_emb))
+    buyer_emb = exchange(buyer_own, PLANE)
     return buyer_emb.reshape(-1, E), goods_emb.reshape(-1, E)
 
 

time: 243 us -> 237 us (0.975)
  blocking collectives: 88.1 us -> 95.6 us
  waiting for transfers between devices: 43.5 us -> 36.3 us
  starting transfers between devices: 73.6 us -> 66.7 us
    all_to_all x6, blocking collectives: 88.1 us -> 95.6 us  [exchange(): return lax.all_to_all(x, axes, 0, 0, tiled=True)]
    ppermute x3, waiting for transfers between devices: 14.8 us -> 7.47 us  [swap(): return lax.ppermute(x, axis, [(0, 1), (1, 0)])]
    all_to_all x6, starting transfers between devices: 42.5 us -> 35.3 us  [exchange(): return lax.all_to_all(x, axes, 0, 0, tiled=True)]
    ppermute x3, waiting for transfers between devices: 0.01 us -> 3.7 us  [embeddings(): two = lax.ppermute(two, 'x', [(i, (i + d) % 4) for i in range(4)])]
    all_to_all x6, waiting for transfers between devices: 28.7 us -> 25.1 us  [exchange(): return lax.all_to_all(x, axes, 0, 0, tiled=True)]
  transfers between devices with their start and end apart: 12 -> 12, of which waited for: 5 -> 7; matrix products, arithmetic and copies ran while one was open for 2% -> 1% of each run, Pallas kernels for 1% -> 2%
where the time goes in v1:
time: 237 us; the launch traced here: 236 us
  blocking collectives  95.6 us (40%)
  starting transfers between devices  66.7 us (28%)
  waiting for transfers between devices  36.3 us (15%)
  Pallas kernels  30.5 us (13%)
  local copies, waits for them, and re-layouts  6.07 us (3%)
    all_to_all x6, blocking collectives, exchange(): return lax.all_to_all(x, axes, 0, 0, tiled=True)  95.6 us
    all_to_all x6, starting transfers between devices, exchange(): return lax.all_to_all(x, axes, 0, 0, tiled=True)  35.3 us
    all_to_all x6, waiting for transfers between devices, exchange(): return lax.all_to_all(x, axes, 0, 0, tiled=True)  25.1 us
    ppermute x3, starting transfers between devices, swap(): return lax.ppermute(x, axis, [(0, 1), (1, 0)])  22.1 us
    ppermute x3, starting transfers between devices, embeddings(): two = lax.ppermute(two, 'x', [(i, (i + d) % 4) for i in range(4)])  9.33 us
    pallas_call x3, Pallas kernels, price_call(): pl.pallas_call(functools.partial(price_kernel, k), in_specs=[VM] * (2 if...  8.13 us
    ppermute x3, waiting for transfers between devices, swap(): return lax.ppermute(x, axis, [(0, 1), (1, 0)])  7.47 us
    pallas_call x1, Pallas kernels, values_call(): pl.pallas_call(values_kernel, grid=(GT,), in_specs=[pl.BlockSpec((128, E)...  7.03 us
  transfers between devices with their start and end apart: 12, of which 7 were waited for; matrix products, arithmetic and copies ran while one was open for 1% of the time, Pallas kernels for 2%

profile of v1, /device:TPU:1, one launch (start us, length us, event | category | flops | bytes accessed | tf_op | source)
XLA Modules:
  0.0 236.2 jit_solution(8380349593239728949)
XLA Ops:
  0.6 0.0 copy-start.2
  0.6 1.6 copy.14
  2.2 5.0 %all-to-all-start = ((bf16[4,32,512]{2,1,0:T(8,128)(2,1)}), bf16[4,32,512]{2,1,0:T(8,128)(2,1)S(1)}, u32[]{:S(2)}, u32[]{:S(2)}) async-start(bf16[4,32,512]{2,1,0:T(8,128)(2,1)} %bitcast.35), calls=%async_computation | async-start | bytes 262144 | tf_op jit(solution)/shard_map/all_to_all | solution.py:267
  7.2 0.1 pad_add_fusion.place_ref
  7.3 0.0 copy-start.1
  7.3 0.9 copy-done.1
  8.2 1.3 shard_map.68
  9.5 15.4 %collective-permute-start = (bf16[4,80,128]{2,1,0:T(8,128)(2,1)S(1)}, bf16[4,80,128]{2,1,0:T(8,128)(2,1)S(1)}, u32[]{:S(2)}, u32[]{:S(2)}) collective-permute-start(bf16[4,80,128]{2,1,0:T(8,128)(2,1)S(1)} %get-tuple-element.19), channel_id=1, source_target_pairs={{0,2},{2,0},{1,3},{3,1},{4,6},{6,4},{5,7},{7,5},{8,10},{10,8},{9,1... | collective-permute-start | bytes 245768 | tf_op jit(solution)/shard_map/ppermute | solution.py:271
  25.0 0.0 all-to-all-done.got_ref
  25.0 1.0 shard_map.71
  26.0 4.7 %all-to-all-start.1 = ((bf16[8,64,128]{2,1,0:T(8,128)(2,1)}), bf16[8,64,128]{2,1,0:T(8,128)(2,1)S(1)}, u32[]{:S(2)}, u32[]{:S(2)}) async-start(bf16[8,64,128]{2,1,0:T(8,128)(2,1)} %shard_map.71), calls=%async_computation.1 | async-start | bytes 262144 | tf_op jit(solution)/shard_map/all_to_all | solution.py:267
  30.8 1.0 copy.9
  31.7 0.0 collective-permute-done.came_ref
  31.7 0.1 shard_map.69
  31.9 3.4 %collective-permute-start.1 = (bf16[4,80,128]{2,1,0:T(8,128)(2,1)S(1)}, bf16[4,80,128]{2,1,0:T(8,128)(2,1)S(1)}, u32[]{:S(2)}, u32[]{:S(2)}) collective-permute-start(bf16[4,80,128]{2,1,0:T(8,128)(2,1)S(1)} %get-tuple-element.21), channel_id=1, source_target_pairs={{0,1},{1,0},{2,3},{3,2},{4,5},{5,4},{6,7},{7,6},{8,9},{9,8},{10,11... | collective-permute-start | bytes 245768 | tf_op jit(solution)/shard_map/ppermute | solution.py:271
  35.3 0.9 collective-permute-done.1
  36.2 4.8 %all-to-all-done.1.got_ref = bf16[8,64,128]{2,1,0:T(8,128)(2,1)S(1)} async-done(((bf16[8,64,128]{2,1,0:T(8,128)(2,1)}), bf16[8,64,128]{2,1,0:T(8,128)(2,1)S(1)}, u32[]{:S(2)}, u32[]{:S(2)}) %all-to-all-start.1) | async-done | bytes 131104 | tf_op jit(solution)/shard_map/all_to_all | solution.py:267
  41.0 0.9 shard_map.72
  42.0 6.0 %all-to-all-start.2 = ((bf16[16,64,128]{2,1,0:T(8,128)(2,1)}), bf16[16,64,128]{2,1,0:T(8,128)(2,1)S(1)}, u32[]{:S(2)}, u32[]{:S(2)}) async-start(bf16[16,64,128]{2,1,0:T(8,128)(2,1)} %shard_map.72), calls=%async_computation.2 | async-start | bytes 524288 | tf_op jit(solution)/shard_map/all_to_all | solution.py:267
  48.0 4.4 %collective-permute-start.4 = (bf16[2,80,128]{2,1,0:T(8,128)(2,1)S(1)}, bf16[2,80,128]{2,1,0:T(8,128)(2,1)S(1)}, u32[]{:S(2)}, u32[]{:S(2)}) collective-permute-start(bf16[2,80,128]{2,1,0:T(8,128)(2,1)S(1)} %pad_maximum_fusion.2), channel_id=1, source_target_pairs={{0,12},{4,0},{8,4},{12,8},{1,13},{5,1},{9,5},{13,9},{2,14},{6,2},{... | collective-permute-start | bytes 122888 | tf_op jit(solution)/shard_map/ppermute | solution.py:285
  52.4 2.4 %collective-permute-start.3 = (bf16[2,80,128]{2,1,0:T(8,128)(2,1)S(1)}, bf16[2,80,128]{2,1,0:T(8,128)(2,1)S(1)}, u32[]{:S(2)}, u32[]{:S(2)}) collective-permute-start(bf16[2,80,128]{2,1,0:T(8,128)(2,1)S(1)} %pad_maximum_fusion.1), channel_id=1, source_target_pairs={{0,8},{4,12},{8,0},{12,4},{1,9},{5,13},{9,1},{13,5},{2,10},{6,14},... | collective-permute-start | bytes 122888 | tf_op jit(solution)/shard_map/ppermute | solution.py:285
  54.8 2.5 %collective-permute-start.2 = (bf16[2,80,128]{2,1,0:T(8,128)(2,1)S(1)}, bf16[2,80,128]{2,1,0:T(8,128)(2,1)S(1)}, u32[]{:S(2)}, u32[]{:S(2)}) collective-permute-start(bf16[2,80,128]{2,1,0:T(8,128)(2,1)S(1)} %pad_maximum_fusion), channel_id=1, source_target_pairs={{0,4},{4,8},{8,12},{12,0},{1,5},{5,9},{9,13},{13,1},{2,6},{6,10},{... | collective-permute-start | bytes 122888 | tf_op jit(solution)/shard_map/ppermute | solution.py:285
  57.3 0.0 collective-permute-done.4
  57.4 1.6 collective-permute-done.3
  58.9 2.2 collective-permute-done.2
  61.1 0.0 copy-start
  61.1 0.9 copy-done
  62.0 1.7 shard_map.70
  63.7 0.0 all-to-all-done.2
  63.7 10.7 %all-to-all-start.3 = ((bf16[32,80,128]{2,1,0:T(8,128)(2,1)}), bf16[32,80,128]{2,1,0:T(8,128)(2,1)S(1)}, u32[]{:S(2)}, u32[]{:S(2)}) async-start(bf16[32,80,128]{2,1,0:T(8,128)(2,1)} %shard_map.70), calls=%async_computation.3 | async-start | bytes 1310720 | tf_op jit(solution)/shard_map/all_to_all | solution.py:267
  74.4 0.0 copy-done.2
  74.4 0.1 reshape.42
  74.5 0.1 reshape.43
  74.6 12.6 %all-to-all-done.3 = bf16[32,80,128]{2,1,0:T(8,128)(2,1)S(1)} async-done(((bf16[32,80,128]{2,1,0:T(8,128)(2,1)}), bf16[32,80,128]{2,1,0:T(8,128)(2,1)S(1)}, u32[]{:S(2)}, u32[]{:S(2)}) %all-to-all-start.3) | async-done | bytes 655392 | tf_op jit(solution)/shard_map/all_to_all | solution.py:267
  87.3 7.0 %shard_map.73 = (bf16[1024,2560]{1,0:T(8,128)(2,1)S(1)}, f32[32,21,128]{2,1,0:T(8,128)S(1)}) custom-call(bf16[1024,128]{1,0:T(8,128)(2,1)S(1)} %bitcast.37, bf16[2560,128]{1,0:T(8,128)(2,1)S(1)} %bitcast.36, f32[1,128]{1,0:T(1,128)S(1)} %constant_dynamic-slice_fusion.money_ref), custom_call_target="tpu_custom_call" | custom-call | tf_op jit(solution)/shard_map/pallas_call | solution.py:138
  94.3 13.8 %all_to_all.60.got_ref = f32[32,21,128]{2,1,0:T(8,128)S(1)} all-to-all(f32[32,21,128]{2,1,0:T(8,128)S(1)} %get-tuple-element.24), channel_id=1, replica_groups=mesh['y'=4,'zl'=8,'x'=4,'zh'=2,'c'=2] {'y','x','c'}, dimensions={0} | all-to-all | bytes 688128 | tf_op jit(solution)/shard_map/all_to_all | solution.py:267
  108.0 2.4 %shard_map.74 = (f32[16,8,128]{2,1,0:T(8,128)S(1)}, f32[20,128]{1,0:T(8,128)S(1)}) custom-call(f32[32,21,128]{2,1,0:T(8,128)S(1)} %all_to_all.60.got_ref, bf16[1024,2560]{1,0:T(8,128)(2,1)S(1)} %get-tuple-element.25.refs_0_.refs_1_.refs_2_), custom_call_target="tpu_custom_call" | custom-call | tf_op jit(solution)/shard_map/pallas_call | solution.py:162
  110.5 22.4 %all_to_all.61.got_ref = f32[16,8,128]{2,1,0:T(8,128)S(1)} all-to-all(f32[16,8,128]{2,1,0:T(8,128)S(1)} %get-tuple-element.26), channel_id=1, replica_groups=mesh['y'=4,'zl'=8,'x'=4,'zh'=2,'c'=2] {'zh','zl'}, dimensions={0} | all-to-all | bytes 131072 | tf_op jit(solution)/shard_map/all_to_all | solution.py:267
  132.9 3.3 %shard_map.75 = (f32[32,20,128]{2,1,0:T(8,128)S(1)}, f32[8,128]{1,0:T(8,128)}) custom-call(f32[16,8,128]{2,1,0:T(8,128)S(1)} %all_to_all.61.got_ref, bf16[1024,2560]{1,0:T(8,128)(2,1)S(1)} %get-tuple-element.25.refs_0_.refs_1_.refs_2_), custom_call_target="tpu_custom_call" | custom-call | tf_op jit(solution)/shard_map/pallas_call | solution.py:184
  136.2 15.4 %all_to_all.62.got_ref = f32[32,20,128]{2,1,0:T(8,128)S(1)} all-to-all(f32[32,20,128]{2,1,0:T(8,128)S(1)} %get-tuple-element.27), channel_id=1, replica_groups=mesh['y'=4,'zl'=8,'x'=4,'zh'=2,'c'=2] {'y','x','c'}, dimensions={0} | all-to-all | bytes 655360 | tf_op jit(solution)/shard_map/all_to_all | solution.py:267
  151.6 2.7 %shard_map.76 = f32[16,8,128]{2,1,0:T(8,128)S(1)} custom-call(f32[32,20,128]{2,1,0:T(8,128)S(1)} %all_to_all.62.got_ref, f32[20,128]{1,0:T(8,128)S(1)} %get-tuple-element.28.refs_0_, bf16[1024,2560]{1,0:T(8,128)(2,1)S(1)} %get-tuple-element.25.refs_0_.refs_1_.refs_2_), custom_call_target="tpu_custom_call" | custom-call | tf_op jit(solution)/shard_map/pallas_call | solution.py:162
  154.3 14.3 %all_to_all.63.got_ref = f32[16,8,128]{2,1,0:T(8,128)S(1)} all-to-all(f32[16,8,128]{2,1,0:T(8,128)S(1)} %shard_map.76), channel_id=1, replica_groups=mesh['y'=4,'zl'=8,'x'=4,'zh'=2,'c'=2] {'zh','zl'}, dimensions={0} | all-to-all | bytes 131072 | tf_op jit(solution)/shard_map/all_to_all | solution.py:267
  168.6 3.1 %shard_map.77 = (f32[32,20,128]{2,1,0:T(8,128)S(1)}, f32[8,128]{1,0:T(8,128)S(1)}) custom-call(f32[16,8,128]{2,1,0:T(8,128)S(1)} %all_to_all.63.got_ref, bf16[1024,2560]{1,0:T(8,128)(2,1)S(1)} %get-tuple-element.25.refs_0_.refs_1_.refs_2_), custom_call_target="tpu_custom_call" | custom-call | tf_op jit(solution)/shard_map/pallas_call | solution.py:184
  171.7 15.4 %all_to_all.64.got_ref = f32[32,20,128]{2,1,0:T(8,128)S(1)} all-to-all(f32[32,20,128]{2,1,0:T(8,128)S(1)} %get-tuple-element.29), channel_id=1, replica_groups=mesh['y'=4,'zl'=8,'x'=4,'zh'=2,'c'=2] {'y','x','c'}, dimensions={0} | all-to-all | bytes 655360 | tf_op jit(solution)/shard_map/all_to_all | solution.py:267
  187.1 3.0 %shard_map.78 = f32[16,8,128]{2,1,0:T(8,128)S(1)} custom-call(f32[32,20,128]{2,1,0:T(8,128)S(1)} %all_to_all.64.got_ref, f32[20,128]{1,0:T(8,128)S(1)} %get-tuple-element.28.refs_0_, bf16[1024,2560]{1,0:T(8,128)(2,1)S(1)} %get-tuple-element.25.refs_0_.refs_1_.refs_2_), custom_call_target="tpu_custom_call" | custom-call | tf_op jit(solution)/shard_map/pallas_call | solution.py:162
  190.2 14.3 %all_to_all.65.got_ref = f32[16,8,128]{2,1,0:T(8,128)S(1)} all-to-all(f32[16,8,128]{2,1,0:T(8,128)S(1)} %shard_map.78), channel_id=1, replica_groups=mesh['y'=4,'zl'=8,'x'=4,'zh'=2,'c'=2] {'zh','zl'}, dimensions={0} | all-to-all | bytes 131072 | tf_op jit(solution)/shard_map/all_to_all | solution.py:267
  204.5 3.8 %shard_map.79 = (f32[32,5,128]{2,1,0:T(8,128)}, f32[4,4,128]{2,1,0:T(4,128)}) custom-call(f32[16,8,128]{2,1,0:T(8,128)S(1)} %all_to_all.65.got_ref, f32[8,128]{1,0:T(8,128)S(1)} %get-tuple-element.30.refs_0_, s32[1]{0:T(128)} %bitcast.1.refs_1_, bf16[1024,2560]{1,0:T(8,128)(2,1)S(1)} %get-tuple-element.25.refs_0_.refs_1_.refs_2_), custom_call_target="tpu_custom_call" | custom-call | tf_op jit(solution)/shard_map/pallas_call | solution.py:176
  208.2 5.6 %all-to-all-start.10 = ((f32[32,5,128]{2,1,0:T(8,128)}), f32[32,5,128]{2,1,0:T(8,128)S(1)}, u32[]{:S(2)}, u32[]{:S(2)}) async-start(f32[32,5,128]{2,1,0:T(8,128)} %get-tuple-element.32), calls=%async_computation.10 | async-start | bytes 262144 | tf_op jit(solution)/shard_map/all_to_all | solution.py:267
  213.9 7.7 %all-to-all-done.10 = f32[32,5,128]{2,1,0:T(8,128)S(1)} async-done(((f32[32,5,128]{2,1,0:T(8,128)}), f32[32,5,128]{2,1,0:T(8,128)S(1)}, u32[]{:S(2)}, u32[]{:S(2)}) %all-to-all-start.10) | async-done | bytes 81952 | tf_op jit(solution)/shard_map/all_to_all | solution.py:267
  221.7 3.2 %collective-permute-start.5 = (f32[5,128]{1,0:T(8,128)S(1)}, f32[5,128]{1,0:T(8,128)S(1)}, u32[]{:S(2)}, u32[]{:S(2)}) collective-permute-start(f32[5,128]{1,0:T(8,128)S(1)} %multiply_divide_fusion), channel_id=1, source_target_pairs={{0,2},{2,0},{1,3},{3,1},{4,6},{6,4},{5,7},{7,5},{8,10},{10,8},{9,1... | collective-permute-start | bytes 7688 | tf_op jit(solution)/shard_map/ppermute | solution.py:271
  224.9 3.3 %all-to-all-start.11 = ((f32[4,4,128]{2,1,0:T(4,128)}), f32[4,4,128]{2,1,0:T(4,128)S(1)}, u32[]{:S(2)}, u32[]{:S(2)}) async-start(f32[4,4,128]{2,1,0:T(4,128)} %get-tuple-element.33), calls=%async_computation.11 | async-start | bytes 16384 | tf_op jit(solution)/shard_map/all_to_all | solution.py:267
  228.1 6.6 %collective-permute-done.5 = f32[5,128]{1,0:T(8,128)S(1)} collective-permute-done((f32[5,128]{1,0:T(8,128)S(1)}, f32[5,128]{1,0:T(8,128)S(1)}, u32[]{:S(2)}, u32[]{:S(2)}) %collective-permute-start.5) | collective-permute-done | bytes 2592 | tf_op jit(solution)/shard_map/ppermute | solution.py:271
  234.7 0.1 stack_reshape.8
  234.8 0.1 stack_reshape.9
  234.9 0.7 reshape.45
  235.6 0.0 all-to-all-done.11
  235.6 0.6 copy.16
  (15 shorter events, 0.2 us)
Async XLA Ops:
  0.6 73.8 %copy-start.2 = (f32[1280]{0:T(1024)S(1)}, f32[1280]{0:T(1024)}, u32[]{:S(2)}) copy-start(f32[1280]{0:T(1024)} %param.9) | copy-start | bytes 15364
  2.2 22.8 %all-to-all-start = ((bf16[4,32,512]{2,1,0:T(8,128)(2,1)}), bf16[4,32,512]{2,1,0:T(8,128)(2,1)S(1)}, u32[]{:S(2)}, u32[]{:S(2)}) async-start(bf16[4,32,512]{2,1,0:T(8,128)(2,1)} %bitcast.35), calls=%async_computation | async-start | bytes 262144 | tf_op jit(solution)/shard_map/all_to_all | solution.py:267
  7.3 0.9 copy-start.1
  9.5 22.2 %collective-permute-start = (bf16[4,80,128]{2,1,0:T(8,128)(2,1)S(1)}, bf16[4,80,128]{2,1,0:T(8,128)(2,1)S(1)}, u32[]{:S(2)}, u32[]{:S(2)}) collective-permute-start(bf16[4,80,128]{2,1,0:T(8,128)(2,1)S(1)} %get-tuple-element.19), channel_id=1, source_target_pairs={{0,2},{2,0},{1,3},{3,1},{4,6},{6,4},{5,7},{7,5},{8,10},{10,8},{9,1... | collective-permute-start | bytes 245768 | tf_op jit(solution)/shard_map/ppermute | solution.py:271
  26.0 15.0 %all-to-all-start.1 = ((bf16[8,64,128]{2,1,0:T(8,128)(2,1)}), bf16[8,64,128]{2,1,0:T(8,128)(2,1)S(1)}, u32[]{:S(2)}, u32[]{:S(2)}) async-start(bf16[8,64,128]{2,1,0:T(8,128)(2,1)} %shard_map.71), calls=%async_computation.1 | async-start | bytes 262144 | tf_op jit(solution)/shard_map/all_to_all | solution.py:267
  31.9 4.3 %collective-permute-start.1 = (bf16[4,80,128]{2,1,0:T(8,128)(2,1)S(1)}, bf16[4,80,128]{2,1,0:T(8,128)(2,1)S(1)}, u32[]{:S(2)}, u32[]{:S(2)}) collective-permute-start(bf16[4,80,128]{2,1,0:T(8,128)(2,1)S(1)} %get-tuple-element.21), channel_id=1, source_target_pairs={{0,1},{1,0},{2,3},{3,2},{4,5},{5,4},{6,7},{7,6},{8,9},{9,8},{10,11... | collective-permute-start | bytes 245768 | tf_op jit(solution)/shard_map/ppermute | solution.py:271
  42.0 21.7 %all-to-all-start.2 = ((bf16[16,64,128]{2,1,0:T(8,128)(2,1)}), bf16[16,64,128]{2,1,0:T(8,128)(2,1)S(1)}, u32[]{:S(2)}, u32[]{:S(2)}) async-start(bf16[16,64,128]{2,1,0:T(8,128)(2,1)} %shard_map.72), calls=%async_computation.2 | async-start | bytes 524288 | tf_op jit(solution)/shard_map/all_to_all | solution.py:267
  48.0 9.4 %collective-permute-start.4 = (bf16[2,80,128]{2,1,0:T(8,128)(2,1)S(1)}, bf16[2,80,128]{2,1,0:T(8,128)(2,1)S(1)}, u32[]{:S(2)}, u32[]{:S(2)}) collective-permute-start(bf16[2,80,128]{2,1,0:T(8,128)(2,1)S(1)} %pad_maximum_fusion.2), channel_id=1, source_target_pairs={{0,12},{4,0},{8,4},{12,8},{1,13},{5,1},{9,5},{13,9},{2,14},{6,2},{... | collective-permute-start | bytes 122888 | tf_op jit(solution)/shard_map/ppermute | solution.py:285
  52.4 6.5 %collective-permute-start.3 = (bf16[2,80,128]{2,1,0:T(8,128)(2,1)S(1)}, bf16[2,80,128]{2,1,0:T(8,128)(2,1)S(1)}, u32[]{:S(2)}, u32[]{:S(2)}) collective-permute-start(bf16[2,80,128]{2,1,0:T(8,128)(2,1)S(1)} %pad_maximum_fusion.1), channel_id=1, source_target_pairs={{0,8},{4,12},{8,0},{12,4},{1,9},{5,13},{9,1},{13,5},{2,10},{6,14},... | collective-permute-start | bytes 122888 | tf_op jit(solution)/shard_map/ppermute | solution.py:285
  54.8 6.3 %collective-permute-start.2 = (bf16[2,80,128]{2,1,0:T(8,128)(2,1)S(1)}, bf16[2,80,128]{2,1,0:T(8,128)(2,1)S(1)}, u32[]{:S(2)}, u32[]{:S(2)}) collective-permute-start(bf16[2,80,128]{2,1,0:T(8,128)(2,1)S(1)} %pad_maximum_fusion), channel_id=1, source_target_pairs={{0,4},{4,8},{8,12},{12,0},{1,5},{5,9},{9,13},{13,1},{2,6},{6,10},{... | collective-permute-start | bytes 122888 | tf_op jit(solution)/shard_map/ppermute | solution.py:285
  61.1 1.0 copy-start
  63.7 23.5 %all-to-all-start.3 = ((bf16[32,80,128]{2,1,0:T(8,128)(2,1)}), bf16[32,80,128]{2,1,0:T(8,128)(2,1)S(1)}, u32[]{:S(2)}, u32[]{:S(2)}) async-start(bf16[32,80,128]{2,1,0:T(8,128)(2,1)} %shard_map.70), calls=%async_computation.3 | async-start | bytes 1310720 | tf_op jit(solution)/shard_map/all_to_all | solution.py:267
  208.2 13.4 %all-to-all-start.10 = ((f32[32,5,128]{2,1,0:T(8,128)}), f32[32,5,128]{2,1,0:T(8,128)S(1)}, u32[]{:S(2)}, u32[]{:S(2)}) async-start(f32[32,5,128]{2,1,0:T(8,128)} %get-tuple-element.32), calls=%async_computation.10 | async-start | bytes 262144 | tf_op jit(solution)/shard_map/all_to_all | solution.py:267
  221.7 13.1 %collective-permute-start.5 = (f32[5,128]{1,0:T(8,128)S(1)}, f32[5,128]{1,0:T(8,128)S(1)}, u32[]{:S(2)}, u32[]{:S(2)}) collective-permute-start(f32[5,128]{1,0:T(8,128)S(1)} %multiply_divide_fusion), channel_id=1, source_target_pairs={{0,2},{2,0},{1,3},{3,1},{4,6},{6,4},{5,7},{7,5},{8,10},{10,8},{9,1... | collective-permute-start | bytes 7688 | tf_op jit(solution)/shard_map/ppermute | solution.py:271
  224.9 10.7 %all-to-all-start.11 = ((f32[4,4,128]{2,1,0:T(4,128)}), f32[4,4,128]{2,1,0:T(4,128)S(1)}, u32[]{:S(2)}, u32[]{:S(2)}) async-start(f32[4,4,128]{2,1,0:T(4,128)} %get-tuple-element.33), calls=%async_computation.11 | async-start | bytes 16384 | tf_op jit(solution)/shard_map/all_to_all | solution.py:267

commit v2 on v1

--- a/solution.py
+++ b/solution.py
@@ -57,77 +57,100 @@
             out_ref[p] = rows[0 : LB + 1, :]
 
 
-def powered(v, k):
-    square = v * v if k >= 2 else None
-    return {1: lambda: v, 2: lambda: square, 3: lambda: square * v, 4: lambda: square * square}[k]()
+def three_parts(x, lhs):
+    lhs[...] = jnp.zeros_like(lhs)
+    for i in range(3):
+        part = x.astype(jnp.bfloat16).astype(jnp.float32)
+        x = x - part
+        for b in range(part.shape[0]):
+            lhs[i : i + 1, 128 * b : 128 * b + 128] = part[b : b + 1, :]
 
 
 def price_kernel(k, got_ref, *refs):
     if k == 1:
-        values, out_ref, money_ref, scale, sums = refs
+        values, out_ref, money_ref, lhs = refs
         for y in range(4):
             for i in range(5):
                 money_ref[5 * y + i : 5 * y + i + 1, :] = got_ref[8 * y + i, LB : LB + 1, :]
     else:
-        money_ref, values, out_ref, scale, sums = refs
+        money_ref, power, out_ref, scale, sums = refs
     total = got_ref[0, 0:LB, :]
     for p in range(1, got_ref.shape[0]):
         total = total + got_ref[p, 0:LB, :]
-    scale[...] = money_ref[...] / total
+    if k == 1:
+        three_parts(money_ref[...] / total, lhs)
+        products = lax.dot_general(
+            lhs[...].astype(jnp.bfloat16), values[...], (((1,), (1,)), ((), ())), preferred_element_type=jnp.float32
+        )
+        whole = jnp.sum(products, 0, keepdims=True)
+        rows = [whole[:, 128 * q : 128 * q + 128] for q in range(GT)]
+    else:
+        scale[...] = money_ref[...] / total
+
+        def chunk(i, _):
+            at = pl.ds(pl.multiple_of(16 * i, 16), 16)
+            even = power[at, 0:128] * scale[0:1, :]
+            odd = power[at, 128:256] * scale[1:2, :]
+            for b in range(2, LB, 2):
+                even = even + power[at, 128 * b : 128 * b + 128] * scale[b : b + 1, :]
+                odd = odd + power[at, 128 * b + 128 : 128 * b + 256] * scale[b + 1 : b + 2, :]
+            sums[at, :] = even + odd
+            return 0
+
+        lax.fori_loop(0, NGOOD // 16, chunk, 0, unroll=4)
+        rows = [jnp.sum(sums[128 * q : 128 * q + 128, :].T, 0, keepdims=True) for q in range(GT)]
     for q in range(GT):
-
-        def chunk(i, _, q=q):
-            at = pl.multiple_of(128 * q + 16 * i, 16)
-            acc = None
-            for b in range(LB):
-                v = values[pl.ds(at, 16), 128 * b : 128 * b + 128].astype(jnp.float32)
-                term = powered(v, k) * scale[b : b + 1, :]
-                acc = term if acc is None else acc + term
-            sums[pl.ds(pl.multiple_of(16 * i, 16), 16), :] = acc
-            return 0
-
-        lax.fori_loop(0, 8, chunk, 0, unroll=2)
-        row = jnp.sum(sums[...].T, 0, keepdims=True)
         for p in range(out_ref.shape[0]):
-            out_ref[p, q : q + 1, :] = row
+            out_ref[p, q : q + 1, :] = rows[q]
 
 
 def utility_kernel(k, got_ref, *refs):
-    last = k == ITERS
-    if last:
-        before_ref, zh_ref, values, out_ref, prices_ref, inverse, spare = refs
-    else:
-        values, out_ref, sum_ref, inverse, spare = refs
+    if k == 1:
+        values, out_ref, sum_ref, power, inverse, rows = refs
+    elif k == 2:
+        values, square, out_ref, sum_ref, power, inverse, rows = refs
+    else:
+        before_ref, zh_ref, square, out_ref, prices_ref, inverse, rows = refs
     total = got_ref[0]
     for p in range(1, got_ref.shape[0]):
         total = total + got_ref[p]
-    inverse[...] = 1.0 / total
-    if last:
-        spare[0:8, :] = total / before_ref[...]
-        half = spare[pl.ds(pl.multiple_of(4 * zh_ref[0], 4), 4), :]
+    if k == ITERS:
+        rows[0:8, :] = total / before_ref[...]
+        half = rows[pl.ds(pl.multiple_of(4 * zh_ref[0], 4), 4), :]
         for p in range(prices_ref.shape[0]):
             prices_ref[p] = half
     else:
         sum_ref[...] = total
+    ratio = 1.0 / total
+    for q in range(GT):
+        inverse[128 * q : 128 * q + 128, :] = jnp.broadcast_to(ratio[q : q + 1, :], (128, 128)).T
+
+    def chunk(i, accs):
+        at = pl.ds(pl.multiple_of(16 * i, 16), 16)
+        c = inverse[at, :]
+        new = []
+        for b in range(LB):
+            cols = slice(128 * b, 128 * b + 128)
+            if k == 1:
+                v = values[at, cols].astype(jnp.float32)
+                raised = v * v
+            elif k == 2:
+                raised = square[at, cols] * values[at, cols].astype(jnp.float32)
+            else:
+                v = square[at, cols]
+                raised = v * v
+            if k < ITERS:
+                power[at, cols] = raised
+            term = raised * c
+            new.append(accs[b] + (term[0:8] + term[8:16]))
+        return tuple(new)
+
     accs = tuple(jnp.zeros((8, 128), jnp.float32) for _ in range(LB))
-    for q in range(GT):
-        spare[...] = jnp.broadcast_to(inverse[q : q + 1, :], (128, 128)).T
-
-        def chunk(i, accs, q=q):
-            at = pl.multiple_of(128 * q + 16 * i, 16)
-            c = spare[pl.ds(pl.multiple_of(16 * i, 16), 16), :]
-            new = []
-            for b in range(LB):
-                v = values[pl.ds(at, 16), 128 * b : 128 * b + 128].astype(jnp.float32)
-                term = powered(v, k + 1) * c
-                new.append(accs[b] + (term[0:8] + term[8:16]))
-            return tuple(new)
-
-        accs = lax.fori_loop(0, 8, chunk, accs)
+    accs = lax.fori_loop(0, NGOOD // 16, chunk, accs, unroll=2)
     for b in range(LB):
-        spare[b : b + 1, :] = jnp.sum(accs[b], 0, keepdims=True)
+        rows[b : b + 1, :] = jnp.sum(accs[b], 0, keepdims=True)
     for p in range(out_ref.shape[0]):
-        out_ref[p] = spare[5 * (p // 8) : 5 * (p // 8) + 5, :] if last else spare[0:LB, :]
+        out_ref[p] = rows[5 * (p // 8) : 5 * (p // 8) + 5, :] if k == ITERS else rows[0:LB, :]
 
 
 VM = pl.BlockSpec(memory_space=pltpu.VMEM)
@@ -156,39 +179,33 @@
     )(goods_emb, buyer_emb, money_row)
 
 
-def price_call(k, got, values, money=None):
+def price_call(k, got, power, money=None):
     payload = jax.ShapeDtypeStruct((16, GT, 128), jnp.float32)
     first = k == 1
+    scratch = [(8, NBUY)] if first else [(LB, 128), (NGOOD, 128)]
     return pl.pallas_call(
         functools.partial(price_kernel, k),
         in_specs=[VM] * (2 if first else 3),
         out_specs=[VM, VM] if first else VM,
         out_shape=[payload, jax.ShapeDtypeStruct((LB, 128), jnp.float32)] if first else payload,
-        scratch_shapes=[pltpu.VMEM((LB, 128), jnp.float32), pltpu.VMEM((128, 128), jnp.float32)],
+        scratch_shapes=[pltpu.VMEM(x, jnp.float32) for x in scratch],
         compiler_params=PARAMS,
-    )(*((got, values) if first else (got, money, values)))
-
-
-def utility_call(k, got, values, before=None, zh=None):
-    last = k == ITERS
-    scratch = [pltpu.VMEM((GT, 128), jnp.float32), pltpu.VMEM((128, 128), jnp.float32)]
-    if last:
-        return pl.pallas_call(
-            functools.partial(utility_kernel, k),
-            in_specs=[VM, VM, pl.BlockSpec(memory_space=pltpu.SMEM), VM],
-            out_specs=[VM, VM],
-            out_shape=[jax.ShapeDtypeStruct((32, 5, 128), jnp.float32), jax.ShapeDtypeStruct((4, 4, 128), jnp.float32)],
-            scratch_shapes=scratch,
-            compiler_params=PARAMS,
-        )(got, before, zh, values)
+    )(*((got, power) if first else (got, money, power)))
+
+
+def utility_call(k, got, *blocks):
+    if k == ITERS:
+        outs, specs = [(32, 5, 128), (4, 4, 128)], [VM, VM, pl.BlockSpec(memory_space=pltpu.SMEM), VM]
+    else:
+        outs, specs = [(32, LB, 128), (GT, 128), (NGOOD, NBUY)], [VM] * (1 + len(blocks))
     return pl.pallas_call(
         functools.partial(utility_kernel, k),
-        in_specs=[VM, VM],
-        out_specs=[VM, VM],
-        out_shape=[jax.ShapeDtypeStruct((32, LB, 128), jnp.float32), jax.ShapeDtypeStruct((GT, 128), jnp.float32)],
-        scratch_shapes=scratch,
+        in_specs=specs,
+        out_specs=[VM] * len(outs),
+        out_shape=[jax.ShapeDtypeStruct(o, jnp.float32) for o in outs],
+        scratch_shapes=[pltpu.VMEM((NGOOD, 128), jnp.float32), pltpu.VMEM((24, 128), jnp.float32)],
         compiler_params=PARAMS,
-    )(got, values)
+    )(got, *blocks)
 
 
 def pack_kernel(place_ref, hidden_ref, keep_ref, go_ref):
@@ -308,11 +325,12 @@
     values, sent = values_call(goods_emb, buyer_emb, money_row)
     got = exchange(sent, PLANE)
     sent, money = price_call(1, got, values)
-    for k in range(1, ITERS):
-        sent, before = utility_call(k, exchange(sent, RING), values)
-        got = exchange(sent, PLANE)
-        sent = price_call(k + 1, got, values, money)
-    sent, halves = utility_call(ITERS, exchange(sent, RING), values, before, zh.reshape(1))
+    sent, _, square = utility_call(1, exchange(sent, RING), values)
+    sent = price_call(2, exchange(sent, PLANE), square, money)
+    sent, before, cube = utility_call(2, exchange(sent, RING), values, square)
+    got = exchange(sent, PLANE)
+    sent = price_call(3, got, cube, money)
+    sent, halves = utility_call(3, exchange(sent, RING), before, zh.reshape(1), square)
     final = exchange(sent, PLANE)
     five = lambda a, axis: lax.dynamic_slice_in_dim(a, 5 * y, 5, axis)
     mine_total = jnp.sum(final, 0) * five(money, 0) / jnp.sum(five(got, 1), 0)

time: 237 us -> 229 us (0.966)
  Pallas kernels: 30.5 us -> 22.6 us
    pallas_call x3, Pallas kernels: 8.13 us -> 3.69 us  [price_call(): pl.pallas_call(functools.partial(price_kernel, k), in_specs=[VM] * (2 if...]
    pallas_call x3, Pallas kernels: 10.2 us -> 6.84 us  [utility_call(): pl.pallas_call(functools.partial(utility_kernel, k), in_specs=specs, out_...]
where the time goes in v2:
time: 229 us; the launch traced here: 228 us
  blocking collectives  95.6 us (42%)
  starting transfers between devices  66.7 us (29%)
  waiting for transfers between devices  35.6 us (16%)
  Pallas kernels  22.6 us (10%)
  local copies, waits for them, and re-layouts  6.76 us (3%)
    all_to_all x6, blocking collectives, exchange(): return lax.all_to_all(x, axes, 0, 0, tiled=True)  95.6 us
    all_to_all x6, starting transfers between devices, exchange(): return lax.all_to_all(x, axes, 0, 0, tiled=True)  35.3 us
    all_to_all x6, waiting for transfers between devices, exchange(): return lax.all_to_all(x, axes, 0, 0, tiled=True)  24.4 us
    ppermute x3, starting transfers between devices, swap(): return lax.ppermute(x, axis, [(0, 1), (1, 0)])  22.1 us
    ppermute x3, starting transfers between devices, embeddings(): two = lax.ppermute(two, 'x', [(i, (i + d) % 4) for i in range(4)])  9.33 us
    ppermute x3, waiting for transfers between devices, swap(): return lax.ppermute(x, axis, [(0, 1), (1, 0)])  7.47 us
    pallas_call x1, Pallas kernels, values_call(): pl.pallas_call(values_kernel, grid=(GT,), in_specs=[pl.BlockSpec((128, E)...  7.02 us
    pallas_call x3, Pallas kernels, utility_call(): pl.pallas_call(functools.partial(utility_kernel, k), in_specs=specs, out_...  6.84 us
  transfers between devices with their start and end apart: 12, of which 7 were waited for; matrix products, arithmetic and copies ran while one was open for 1% of the time, Pallas kernels for 2%

profile of v2, /device:TPU:1, one launch (start us, length us, event | category | flops | bytes accessed | tf_op | source)
XLA Modules:
  0.0 228.4 jit_solution(14044859803204222048)
XLA Ops:
  0.6 1.6 copy.14
  2.2 5.0 %all-to-all-start = ((bf16[4,32,512]{2,1,0:T(8,128)(2,1)}), bf16[4,32,512]{2,1,0:T(8,128)(2,1)S(1)}, u32[]{:S(2)}, u32[]{:S(2)}) async-start(bf16[4,32,512]{2,1,0:T(8,128)(2,1)} %bitcast.35), calls=%async_computation | async-start | bytes 262144 | tf_op jit(solution)/shard_map/all_to_all | solution.py:284
  7.2 0.1 pad_add_fusion.place_ref
  7.3 0.0 copy-start.1
  7.3 0.9 copy-done.1
  8.2 1.3 shard_map.68
  9.5 15.4 %collective-permute-start = (bf16[4,80,128]{2,1,0:T(8,128)(2,1)S(1)}, bf16[4,80,128]{2,1,0:T(8,128)(2,1)S(1)}, u32[]{:S(2)}, u32[]{:S(2)}) collective-permute-start(bf16[4,80,128]{2,1,0:T(8,128)(2,1)S(1)} %get-tuple-element.21), channel_id=1, source_target_pairs={{0,2},{2,0},{1,3},{3,1},{4,6},{6,4},{5,7},{7,5},{8,10},{10,8},{9,1... | collective-permute-start | bytes 245768 | tf_op jit(solution)/shard_map/ppermute | solution.py:288
  25.0 0.0 all-to-all-done.got_ref
  25.0 1.0 shard_map.71
  26.0 4.7 %all-to-all-start.1 = ((bf16[8,64,128]{2,1,0:T(8,128)(2,1)}), bf16[8,64,128]{2,1,0:T(8,128)(2,1)S(1)}, u32[]{:S(2)}, u32[]{:S(2)}) async-start(bf16[8,64,128]{2,1,0:T(8,128)(2,1)} %shard_map.71), calls=%async_computation.1 | async-start | bytes 262144 | tf_op jit(solution)/shard_map/all_to_all | solution.py:284
  30.8 1.0 copy.9
  31.7 0.0 collective-permute-done.came_ref
  31.7 0.1 shard_map.69
  31.9 3.4 %collective-permute-start.1 = (bf16[4,80,128]{2,1,0:T(8,128)(2,1)S(1)}, bf16[4,80,128]{2,1,0:T(8,128)(2,1)S(1)}, u32[]{:S(2)}, u32[]{:S(2)}) collective-permute-start(bf16[4,80,128]{2,1,0:T(8,128)(2,1)S(1)} %get-tuple-element.23), channel_id=1, source_target_pairs={{0,1},{1,0},{2,3},{3,2},{4,5},{5,4},{6,7},{7,6},{8,9},{9,8},{10,11... | collective-permute-start | bytes 245768 | tf_op jit(solution)/shard_map/ppermute | solution.py:288
  35.3 0.9 collective-permute-done.1
  36.2 4.8 %all-to-all-done.1.got_ref = bf16[8,64,128]{2,1,0:T(8,128)(2,1)S(1)} async-done(((bf16[8,64,128]{2,1,0:T(8,128)(2,1)}), bf16[8,64,128]{2,1,0:T(8,128)(2,1)S(1)}, u32[]{:S(2)}, u32[]{:S(2)}) %all-to-all-start.1) | async-done | bytes 131104 | tf_op jit(solution)/shard_map/all_to_all | solution.py:284
  41.0 0.9 shard_map.72
  42.0 6.0 %all-to-all-start.2 = ((bf16[16,64,128]{2,1,0:T(8,128)(2,1)}), bf16[16,64,128]{2,1,0:T(8,128)(2,1)S(1)}, u32[]{:S(2)}, u32[]{:S(2)}) async-start(bf16[16,64,128]{2,1,0:T(8,128)(2,1)} %shard_map.72), calls=%async_computation.2 | async-start | bytes 524288 | tf_op jit(solution)/shard_map/all_to_all | solution.py:284
  47.9 4.4 %collective-permute-start.4 = (bf16[2,80,128]{2,1,0:T(8,128)(2,1)S(1)}, bf16[2,80,128]{2,1,0:T(8,128)(2,1)S(1)}, u32[]{:S(2)}, u32[]{:S(2)}) collective-permute-start(bf16[2,80,128]{2,1,0:T(8,128)(2,1)S(1)} %pad_maximum_fusion.2), channel_id=1, source_target_pairs={{0,12},{4,0},{8,4},{12,8},{1,13},{5,1},{9,5},{13,9},{2,14},{6,2},{... | collective-permute-start | bytes 122888 | tf_op jit(solution)/shard_map/ppermute | solution.py:302
  52.4 2.4 %collective-permute-start.3 = (bf16[2,80,128]{2,1,0:T(8,128)(2,1)S(1)}, bf16[2,80,128]{2,1,0:T(8,128)(2,1)S(1)}, u32[]{:S(2)}, u32[]{:S(2)}) collective-permute-start(bf16[2,80,128]{2,1,0:T(8,128)(2,1)S(1)} %pad_maximum_fusion.1), channel_id=1, source_target_pairs={{0,8},{4,12},{8,0},{12,4},{1,9},{5,13},{9,1},{13,5},{2,10},{6,14},... | collective-permute-start | bytes 122888 | tf_op jit(solution)/shard_map/ppermute | solution.py:302
  54.8 2.5 %collective-permute-start.2 = (bf16[2,80,128]{2,1,0:T(8,128)(2,1)S(1)}, bf16[2,80,128]{2,1,0:T(8,128)(2,1)S(1)}, u32[]{:S(2)}, u32[]{:S(2)}) collective-permute-start(bf16[2,80,128]{2,1,0:T(8,128)(2,1)S(1)} %pad_maximum_fusion), channel_id=1, source_target_pairs={{0,4},{4,8},{8,12},{12,0},{1,5},{5,9},{9,13},{13,1},{2,6},{6,10},{... | collective-permute-start | bytes 122888 | tf_op jit(solution)/shard_map/ppermute | solution.py:302
  57.3 0.0 collective-permute-done.4
  57.3 1.5 collective-permute-done.3
  58.9 2.2 collective-permute-done.2
  61.1 0.0 copy-start
  61.1 0.9 copy-done
  62.0 1.7 shard_map.70
  63.7 0.0 all-to-all-done.2
  63.7 10.7 %all-to-all-start.3 = ((bf16[32,80,128]{2,1,0:T(8,128)(2,1)}), bf16[32,80,128]{2,1,0:T(8,128)(2,1)S(1)}, u32[]{:S(2)}, u32[]{:S(2)}) async-start(bf16[32,80,128]{2,1,0:T(8,128)(2,1)} %shard_map.70), calls=%async_computation.3 | async-start | bytes 1310720 | tf_op jit(solution)/shard_map/all_to_all | solution.py:284
  74.4 0.8 reshape.42
  75.2 0.1 reshape.43
  75.3 11.9 %all-to-all-done.3 = bf16[32,80,128]{2,1,0:T(8,128)(2,1)S(1)} async-done(((bf16[32,80,128]{2,1,0:T(8,128)(2,1)}), bf16[32,80,128]{2,1,0:T(8,128)(2,1)S(1)}, u32[]{:S(2)}, u32[]{:S(2)}) %all-to-all-start.3) | async-done | bytes 655392 | tf_op jit(solution)/shard_map/all_to_all | solution.py:284
  87.2 7.0 %shard_map.73 = (bf16[1024,2560]{1,0:T(8,128)(2,1)S(1)}, f32[32,21,128]{2,1,0:T(8,128)S(1)}) custom-call(bf16[1024,128]{1,0:T(8,128)(2,1)S(1)} %bitcast.37, bf16[2560,128]{1,0:T(8,128)(2,1)S(1)} %bitcast.36, f32[1,128]{1,0:T(1,128)S(1)} %constant_dynamic-slice_fusion.money_ref), custom_call_target="tpu_custom_call" | custom-call | tf_op jit(solution)/shard_map/pallas_call | solution.py:161
  94.3 13.8 %all_to_all.60.got_ref = f32[32,21,128]{2,1,0:T(8,128)S(1)} all-to-all(f32[32,21,128]{2,1,0:T(8,128)S(1)} %get-tuple-element.26), channel_id=1, replica_groups=mesh['y'=4,'zl'=8,'x'=4,'zh'=2,'c'=2] {'y','x','c'}, dimensions={0} | all-to-all | bytes 688128 | tf_op jit(solution)/shard_map/all_to_all | solution.py:284
  108.0 1.5 shard_map.74
  109.5 22.4 %all_to_all.61.got_ref = f32[16,8,128]{2,1,0:T(8,128)S(1)} all-to-all(f32[16,8,128]{2,1,0:T(8,128)S(1)} %get-tuple-element.28), channel_id=1, replica_groups=mesh['y'=4,'zl'=8,'x'=4,'zh'=2,'c'=2] {'zh','zl'}, dimensions={0} | all-to-all | bytes 131072 | tf_op jit(solution)/shard_map/all_to_all | solution.py:284
  131.9 2.6 %shard_map.75 = (f32[32,20,128]{2,1,0:T(8,128)S(1)}, f32[8,128]{1,0:T(8,128)}, f32[1024,2560]{1,0:T(8,128)S(1)}) custom-call(f32[16,8,128]{2,1,0:T(8,128)S(1)} %all_to_all.61.got_ref, bf16[1024,2560]{1,0:T(8,128)(2,1)S(1)} %get-tuple-element.27.refs_0_), custom_call_target="tpu_custom_call" | custom-call | tf_op jit(solution)/shard_map/pallas_call | solution.py:201
  134.5 15.4 %all_to_all.62.got_ref = f32[32,20,128]{2,1,0:T(8,128)S(1)} all-to-all(f32[32,20,128]{2,1,0:T(8,128)S(1)} %get-tuple-element.29), channel_id=1, replica_groups=mesh['y'=4,'zl'=8,'x'=4,'zh'=2,'c'=2] {'y','x','c'}, dimensions={0} | all-to-all | bytes 655360 | tf_op jit(solution)/shard_map/all_to_all | solution.py:284
  149.9 1.1 shard_map.76
  151.0 14.3 %all_to_all.63.got_ref = f32[16,8,128]{2,1,0:T(8,128)S(1)} all-to-all(f32[16,8,128]{2,1,0:T(8,128)S(1)} %shard_map.76), channel_id=1, replica_groups=mesh['y'=4,'zl'=8,'x'=4,'zh'=2,'c'=2] {'zh','zl'}, dimensions={0} | all-to-all | bytes 131072 | tf_op jit(solution)/shard_map/all_to_all | solution.py:284
  165.3 2.1 shard_map.77
  167.4 15.4 %all_to_all.64.got_ref = f32[32,20,128]{2,1,0:T(8,128)S(1)} all-to-all(f32[32,20,128]{2,1,0:T(8,128)S(1)} %get-tuple-element.32), channel_id=1, replica_groups=mesh['y'=4,'zl'=8,'x'=4,'zh'=2,'c'=2] {'y','x','c'}, dimensions={0} | all-to-all | bytes 655360 | tf_op jit(solution)/shard_map/all_to_all | solution.py:284
  182.9 1.1 shard_map.78
  183.9 14.3 %all_to_all.65.got_ref = f32[16,8,128]{2,1,0:T(8,128)S(1)} all-to-all(f32[16,8,128]{2,1,0:T(8,128)S(1)} %shard_map.78), channel_id=1, replica_groups=mesh['y'=4,'zl'=8,'x'=4,'zh'=2,'c'=2] {'zh','zl'}, dimensions={0} | all-to-all | bytes 131072 | tf_op jit(solution)/shard_map/all_to_all | solution.py:284
  198.2 2.2 shard_map.79
  200.4 5.6 %all-to-all-start.10 = ((f32[32,5,128]{2,1,0:T(8,128)}), f32[32,5,128]{2,1,0:T(8,128)S(1)}, u32[]{:S(2)}, u32[]{:S(2)}) async-start(f32[32,5,128]{2,1,0:T(8,128)} %get-tuple-element.36), calls=%async_computation.10 | async-start | bytes 262144 | tf_op jit(solution)/shard_map/all_to_all | solution.py:284
  206.1 7.7 %all-to-all-done.10 = f32[32,5,128]{2,1,0:T(8,128)S(1)} async-done(((f32[32,5,128]{2,1,0:T(8,128)}), f32[32,5,128]{2,1,0:T(8,128)S(1)}, u32[]{:S(2)}, u32[]{:S(2)}) %all-to-all-start.10) | async-done | bytes 81952 | tf_op jit(solution)/shard_map/all_to_all | solution.py:284
  213.8 3.2 %collective-permute-start.5 = (f32[5,128]{1,0:T(8,128)S(1)}, f32[5,128]{1,0:T(8,128)S(1)}, u32[]{:S(2)}, u32[]{:S(2)}) collective-permute-start(f32[5,128]{1,0:T(8,128)S(1)} %multiply_divide_fusion), channel_id=1, source_target_pairs={{0,2},{2,0},{1,3},{3,1},{4,6},{6,4},{5,7},{7,5},{8,10},{10,8},{9,1... | collective-permute-start | bytes 7688 | tf_op jit(solution)/shard_map/ppermute | solution.py:288
  217.0 3.3 %all-to-all-start.11 = ((f32[4,4,128]{2,1,0:T(4,128)}), f32[4,4,128]{2,1,0:T(4,128)S(1)}, u32[]{:S(2)}, u32[]{:S(2)}) async-start(f32[4,4,128]{2,1,0:T(4,128)} %get-tuple-element.37), calls=%async_computation.11 | async-start | bytes 16384 | tf_op jit(solution)/shard_map/all_to_all | solution.py:284
  220.3 6.6 %collective-permute-done.5 = f32[5,128]{1,0:T(8,128)S(1)} collective-permute-done((f32[5,128]{1,0:T(8,128)S(1)}, f32[5,128]{1,0:T(8,128)S(1)}, u32[]{:S(2)}, u32[]{:S(2)}) %collective-permute-start.5) | collective-permute-done | bytes 2592 | tf_op jit(solution)/shard_map/ppermute | solution.py:288
  226.9 0.1 stack_reshape.8
  227.0 0.1 stack_reshape.9
  227.1 0.7 reshape.45
  227.7 0.0 all-to-all-done.11
  227.8 0.6 copy.16
  (15 shorter events, 0.2 us)
Async XLA Ops:
  2.2 22.8 %all-to-all-start = ((bf16[4,32,512]{2,1,0:T(8,128)(2,1)}), bf16[4,32,512]{2,1,0:T(8,128)(2,1)S(1)}, u32[]{:S(2)}, u32[]{:S(2)}) async-start(bf16[4,32,512]{2,1,0:T(8,128)(2,1)} %bitcast.35), calls=%async_computation | async-start | bytes 262144 | tf_op jit(solution)/shard_map/all_to_all | solution.py:284
  7.3 0.9 copy-start.1
  9.5 22.2 %collective-permute-start = (bf16[4,80,128]{2,1,0:T(8,128)(2,1)S(1)}, bf16[4,80,128]{2,1,0:T(8,128)(2,1)S(1)}, u32[]{:S(2)}, u32[]{:S(2)}) collective-permute-start(bf16[4,80,128]{2,1,0:T(8,128)(2,1)S(1)} %get-tuple-element.21), channel_id=1, source_target_pairs={{0,2},{2,0},{1,3},{3,1},{4,6},{6,4},{5,7},{7,5},{8,10},{10,8},{9,1... | collective-permute-start | bytes 245768 | tf_op jit(solution)/shard_map/ppermute | solution.py:288
  26.0 15.0 %all-to-all-start.1 = ((bf16[8,64,128]{2,1,0:T(8,128)(2,1)}), bf16[8,64,128]{2,1,0:T(8,128)(2,1)S(1)}, u32[]{:S(2)}, u32[]{:S(2)}) async-start(bf16[8,64,128]{2,1,0:T(8,128)(2,1)} %shard_map.71), calls=%async_computation.1 | async-start | bytes 262144 | tf_op jit(solution)/shard_map/all_to_all | solution.py:284
  31.9 4.3 %collective-permute-start.1 = (bf16[4,80,128]{2,1,0:T(8,128)(2,1)S(1)}, bf16[4,80,128]{2,1,0:T(8,128)(2,1)S(1)}, u32[]{:S(2)}, u32[]{:S(2)}) collective-permute-start(bf16[4,80,128]{2,1,0:T(8,128)(2,1)S(1)} %get-tuple-element.23), channel_id=1, source_target_pairs={{0,1},{1,0},{2,3},{3,2},{4,5},{5,4},{6,7},{7,6},{8,9},{9,8},{10,11... | collective-permute-start | bytes 245768 | tf_op jit(solution)/shard_map/ppermute | solution.py:288
  42.0 21.7 %all-to-all-start.2 = ((bf16[16,64,128]{2,1,0:T(8,128)(2,1)}), bf16[16,64,128]{2,1,0:T(8,128)(2,1)S(1)}, u32[]{:S(2)}, u32[]{:S(2)}) async-start(bf16[16,64,128]{2,1,0:T(8,128)(2,1)} %shard_map.72), calls=%async_computation.2 | async-start | bytes 524288 | tf_op jit(solution)/shard_map/all_to_all | solution.py:284
  47.9 9.4 %collective-permute-start.4 = (bf16[2,80,128]{2,1,0:T(8,128)(2,1)S(1)}, bf16[2,80,128]{2,1,0:T(8,128)(2,1)S(1)}, u32[]{:S(2)}, u32[]{:S(2)}) collective-permute-start(bf16[2,80,128]{2,1,0:T(8,128)(2,1)S(1)} %pad_maximum_fusion.2), channel_id=1, source_target_pairs={{0,12},{4,0},{8,4},{12,8},{1,13},{5,1},{9,5},{13,9},{2,14},{6,2},{... | collective-permute-start | bytes 122888 | tf_op jit(solution)/shard_map/ppermute | solution.py:302
  52.4 6.5 %collective-permute-start.3 = (bf16[2,80,128]{2,1,0:T(8,128)(2,1)S(1)}, bf16[2,80,128]{2,1,0:T(8,128)(2,1)S(1)}, u32[]{:S(2)}, u32[]{:S(2)}) collective-permute-start(bf16[2,80,128]{2,1,0:T(8,128)(2,1)S(1)} %pad_maximum_fusion.1), channel_id=1, source_target_pairs={{0,8},{4,12},{8,0},{12,4},{1,9},{5,13},{9,1},{13,5},{2,10},{6,14},... | collective-permute-start | bytes 122888 | tf_op jit(solution)/shard_map/ppermute | solution.py:302
  54.8 6.3 %collective-permute-start.2 = (bf16[2,80,128]{2,1,0:T(8,128)(2,1)S(1)}, bf16[2,80,128]{2,1,0:T(8,128)(2,1)S(1)}, u32[]{:S(2)}, u32[]{:S(2)}) collective-permute-start(bf16[2,80,128]{2,1,0:T(8,128)(2,1)S(1)} %pad_maximum_fusion), channel_id=1, source_target_pairs={{0,4},{4,8},{8,12},{12,0},{1,5},{5,9},{9,13},{13,1},{2,6},{6,10},{... | collective-permute-start | bytes 122888 | tf_op jit(solution)/shard_map/ppermute | solution.py:302
  61.1 1.0 copy-start
  63.7 23.5 %all-to-all-start.3 = ((bf16[32,80,128]{2,1,0:T(8,128)(2,1)}), bf16[32,80,128]{2,1,0:T(8,128)(2,1)S(1)}, u32[]{:S(2)}, u32[]{:S(2)}) async-start(bf16[32,80,128]{2,1,0:T(8,128)(2,1)} %shard_map.70), calls=%async_computation.3 | async-start | bytes 1310720 | tf_op jit(solution)/shard_map/all_to_all | solution.py:284
  200.4 13.3 %all-to-all-start.10 = ((f32[32,5,128]{2,1,0:T(8,128)}), f32[32,5,128]{2,1,0:T(8,128)S(1)}, u32[]{:S(2)}, u32[]{:S(2)}) async-start(f32[32,5,128]{2,1,0:T(8,128)} %get-tuple-element.36), calls=%async_computation.10 | async-start | bytes 262144 | tf_op jit(solution)/shard_map/all_to_all | solution.py:284
  213.8 13.1 %collective-permute-start.5 = (f32[5,128]{1,0:T(8,128)S(1)}, f32[5,128]{1,0:T(8,128)S(1)}, u32[]{:S(2)}, u32[]{:S(2)}) collective-permute-start(f32[5,128]{1,0:T(8,128)S(1)} %multiply_divide_fusion), channel_id=1, source_target_pairs={{0,2},{2,0},{1,3},{3,1},{4,6},{6,4},{5,7},{7,5},{8,10},{10,8},{9,1... | collective-permute-start | bytes 7688 | tf_op jit(solution)/shard_map/ppermute | solution.py:288
  217.0 10.7 %all-to-all-start.11 = ((f32[4,4,128]{2,1,0:T(4,128)}), f32[4,4,128]{2,1,0:T(4,128)S(1)}, u32[]{:S(2)}, u32[]{:S(2)}) async-start(f32[4,4,128]{2,1,0:T(4,128)} %get-tuple-element.37), calls=%async_computation.11 | async-start | bytes 16384 | tf_op jit(solution)/shard_map/all_to_all | solution.py:284

commit v3 on v2

--- a/solution.py
+++ b/solution.py
@@ -253,18 +253,21 @@
         out_ref[p] = emb
 
 
-def turn_kernel(got_ref, out_ref):
-    for s in range(4):
-        rows = got_ref[s].T
-        for q in range(8):
-            out_ref[q, :, 32 * s : 32 * s + 32] = rows[64 * q : 64 * q + 64]
+def tiles_kernel(hidden_ref, out_ref):
+    for t in range(16):
+        top = hidden_ref[0:16, 128 * t : 128 * t + 128].astype(jnp.float32)
+        low = hidden_ref[16:32, 128 * t : 128 * t + 128].astype(jnp.float32)
+        out_ref[2 * t] = jnp.concatenate([top[:, 0:64], low[:, 0:64]], 1).astype(jnp.bfloat16)
+        out_ref[2 * t + 1] = jnp.concatenate([top[:, 64:128], low[:, 64:128]], 1).astype(jnp.bfloat16)
 
 
 def goods_kernel(got_ref, proj_ref, out_ref):
-    total = jnp.dot(got_ref[0], proj_ref[0], preferred_element_type=jnp.float32)
-    for q in range(1, 8):
-        total = total + jnp.dot(got_ref[q], proj_ref[q], preferred_element_type=jnp.float32)
-    emb = total.astype(jnp.bfloat16)
+    hidden = got_ref[...].reshape(512, 128).astype(jnp.float32).T.astype(jnp.bfloat16)
+    halves = [
+        jnp.dot(hidden[64 * h : 64 * h + 64], proj_ref[:, h].reshape(512, E), preferred_element_type=jnp.float32)
+        for h in range(2)
+    ]
+    emb = (halves[0] + halves[1]).astype(jnp.bfloat16)
     for p in range(out_ref.shape[0]):
         out_ref[p] = emb
 
@@ -291,7 +294,6 @@
 def embeddings(buyer_hidden, goods_hidden, buyer_proj, goods_proj, place):
     bf16 = jnp.bfloat16
     shape = jax.ShapeDtypeStruct
-    goods_part = exchange(goods_hidden.T.reshape(32, 4, 512).transpose(1, 0, 2), ("y",))
     keep, go = small_call(pack_kernel, (shape((4, 80, 128), bf16),) * 2, place, buyer_hidden.T, smem=1)
     came = swap(go, "zh")
     here, across = small_call(pair_kernel, (shape((4, 80, 128), bf16),) * 2, keep, came)
@@ -301,9 +303,9 @@
         two = jnp.stack([here[d], across[d]])
         two = lax.ppermute(two, "x", [(i, (i + d) % 4) for i in range(4)])
         parts += [two[0], two[1]]
-    goods_rows = exchange(small_call(turn_kernel, shape((8, 64, 128), bf16), goods_part), ("zl",))
-    proj = goods_proj.reshape(4, 8, 32, E).transpose(1, 0, 2, 3).reshape(8, 128, E)
-    goods_own = small_call(goods_kernel, shape((16, 64, E), bf16), goods_rows, proj)
+    tiles = small_call(tiles_kernel, shape((32, 16, 128), bf16), goods_hidden.T)
+    tiles = exchange(tiles, ("y", "zl"))
+    goods_own = small_call(goods_kernel, shape((16, 64, E), bf16), tiles, goods_proj.reshape(32, 2, 16, E))
     goods_emb = exchange(goods_own, RING)
     buyer_own = small_call(
         buyers_kernel, shape((32, 80, E), bf16), place, buyer_proj.reshape(16, 64, E), *parts,

time: 229 us -> 228 us (level)
  starting transfers between devices: 66.7 us -> 63.6 us
  waiting for transfers between devices: 35.6 us -> 38.4 us
    all_to_all x6 -> x5, starting transfers between devices: 35.3 us -> 31.7 us  [exchange(): return lax.all_to_all(x, axes, 0, 0, tiled=True)]
    all_to_all x6 -> x5, waiting for transfers between devices: 24.4 us -> 27.2 us  [exchange(): return lax.all_to_all(x, axes, 0, 0, tiled=True)]
    reshape x2 -> x0, local copies, waits for them, and re-layouts: 2.52 us -> none  [the longest x1 1.55 us: embeddings(): goods_hidden.T.reshape(32, 4, 512).transpose(1, 0, 2)]
  transfers between devices with their start and end apart: 12 -> 11, of which waited for: 7 -> 7; matrix products, arithmetic and copies ran while one was open for 1% -> 1% of each run, Pallas kernels for 2% -> 1%
where the time goes in v3:
time: 228 us; the launch traced here: 227 us
  blocking collectives  95.7 us (42%)
  starting transfers between devices  63.6 us (28%)
  waiting for transfers between devices  38.4 us (17%)
  Pallas kernels  22.4 us (10%)
  local copies, waits for them, and re-layouts  6.09 us (3%)
    all_to_all x6, blocking collectives, exchange(): return lax.all_to_all(x, axes, 0, 0, tiled=True)  95.7 us
    all_to_all x5, starting transfers between devices, exchange(): return lax.all_to_all(x, axes, 0, 0, tiled=True)  31.7 us
    all_to_all x5, waiting for transfers between devices, exchange(): return lax.all_to_all(x, axes, 0, 0, tiled=True)  27.2 us
    ppermute x3, starting transfers between devices, swap(): return lax.ppermute(x, axis, [(0, 1), (1, 0)])  22.6 us
    ppermute x3, starting transfers between devices, embeddings(): two = lax.ppermute(two, 'x', [(i, (i + d) % 4) for i in range(4)])  9.33 us
    ppermute x3, waiting for transfers between devices, swap(): return lax.ppermute(x, axis, [(0, 1), (1, 0)])  7.47 us
    pallas_call x1, Pallas kernels, values_call(): pl.pallas_call(values_kernel, grid=(GT,), in_specs=[pl.BlockSpec((128, E)...  7.02 us
    pallas_call x3, Pallas kernels, utility_call(): pl.pallas_call(functools.partial(utility_kernel, k), in_specs=specs, out_...  6.84 us
  transfers between devices with their start and end apart: 11, of which 7 were waited for; matrix products, arithmetic and copies ran while one was open for 1% of the time, Pallas kernels for 1%

profile of v3, /device:TPU:1, one launch (start us, length us, event | category | flops | bytes accessed | tf_op | source)
XLA Modules:
  0.0 227.3 jit_solution(16346136627769035957)
XLA Ops:
  0.6 0.1 pad_add_fusion.place_ref
  0.7 0.0 copy-start.2
  0.7 0.9 copy-done.2
  1.6 1.3 shard_map.68
  2.9 16.3 %collective-permute-start = (bf16[4,80,128]{2,1,0:T(8,128)(2,1)S(1)}, bf16[4,80,128]{2,1,0:T(8,128)(2,1)S(1)}, u32[]{:S(2)}, u32[]{:S(2)}) collective-permute-start(bf16[4,80,128]{2,1,0:T(8,128)(2,1)S(1)} %get-tuple-element.21), channel_id=1, source_target_pairs={{0,2},{2,0},{1,3},{3,1},{4,6},{6,4},{5,7},{7,5},{8,10},{10,8},{9,1... | collective-permute-start | bytes 245768 | tf_op jit(solution)/shard_map/ppermute | solution.py:291
  19.2 0.0 copy-start.3
  19.2 0.9 copy-done.3
  20.1 0.7 shard_map.71
  20.9 7.8 %all-to-all-start = ((bf16[32,16,128]{2,1,0:T(8,128)(2,1)}), bf16[32,16,128]{2,1,0:T(8,128)(2,1)S(1)}, u32[]{:S(2)}, u32[]{:S(2)}) async-start(bf16[32,16,128]{2,1,0:T(8,128)(2,1)} %shard_map.71), calls=%async_computation | async-start | bytes 262144 | tf_op jit(solution)/shard_map/all_to_all | solution.py:287
  28.6 0.0 collective-permute-done.came_ref
  28.7 0.1 shard_map.69
  28.8 3.1 %collective-permute-start.1 = (bf16[4,80,128]{2,1,0:T(8,128)(2,1)S(1)}, bf16[4,80,128]{2,1,0:T(8,128)(2,1)S(1)}, u32[]{:S(2)}, u32[]{:S(2)}) collective-permute-start(bf16[4,80,128]{2,1,0:T(8,128)(2,1)S(1)} %get-tuple-element.23), channel_id=1, source_target_pairs={{0,1},{1,0},{2,3},{3,2},{4,5},{5,4},{6,7},{7,6},{8,9},{9,8},{10,11... | collective-permute-start | bytes 245768 | tf_op jit(solution)/shard_map/ppermute | solution.py:291
  31.9 0.9 collective-permute-done.1
  32.8 7.6 %all-to-all-done.got_ref = bf16[32,16,128]{2,1,0:T(8,128)(2,1)S(1)} async-done(((bf16[32,16,128]{2,1,0:T(8,128)(2,1)}), bf16[32,16,128]{2,1,0:T(8,128)(2,1)S(1)}, u32[]{:S(2)}, u32[]{:S(2)}) %all-to-all-start) | async-done | bytes 131104 | tf_op jit(solution)/shard_map/all_to_all | solution.py:287
  40.4 0.0 copy-start
  40.4 0.9 copy-done
  41.4 1.0 shard_map.72
  42.4 6.0 %all-to-all-start.1 = ((bf16[16,64,128]{2,1,0:T(8,128)(2,1)}), bf16[16,64,128]{2,1,0:T(8,128)(2,1)S(1)}, u32[]{:S(2)}, u32[]{:S(2)}) async-start(bf16[16,64,128]{2,1,0:T(8,128)(2,1)} %shard_map.72), calls=%async_computation.1 | async-start | bytes 524288 | tf_op jit(solution)/shard_map/all_to_all | solution.py:287
  48.4 4.4 %collective-permute-start.4 = (bf16[2,80,128]{2,1,0:T(8,128)(2,1)S(1)}, bf16[2,80,128]{2,1,0:T(8,128)(2,1)S(1)}, u32[]{:S(2)}, u32[]{:S(2)}) collective-permute-start(bf16[2,80,128]{2,1,0:T(8,128)(2,1)S(1)} %pad_maximum_fusion.2), channel_id=1, source_target_pairs={{0,12},{4,0},{8,4},{12,8},{1,13},{5,1},{9,5},{13,9},{2,14},{6,2},{... | collective-permute-start | bytes 122888 | tf_op jit(solution)/shard_map/ppermute | solution.py:304
  52.8 2.4 %collective-permute-start.3 = (bf16[2,80,128]{2,1,0:T(8,128)(2,1)S(1)}, bf16[2,80,128]{2,1,0:T(8,128)(2,1)S(1)}, u32[]{:S(2)}, u32[]{:S(2)}) collective-permute-start(bf16[2,80,128]{2,1,0:T(8,128)(2,1)S(1)} %pad_maximum_fusion.1), channel_id=1, source_target_pairs={{0,8},{4,12},{8,0},{12,4},{1,9},{5,13},{9,1},{13,5},{2,10},{6,14},... | collective-permute-start | bytes 122888 | tf_op jit(solution)/shard_map/ppermute | solution.py:304
  55.2 2.5 %collective-permute-start.2 = (bf16[2,80,128]{2,1,0:T(8,128)(2,1)S(1)}, bf16[2,80,128]{2,1,0:T(8,128)(2,1)S(1)}, u32[]{:S(2)}, u32[]{:S(2)}) collective-permute-start(bf16[2,80,128]{2,1,0:T(8,128)(2,1)S(1)} %pad_maximum_fusion), channel_id=1, source_target_pairs={{0,4},{4,8},{8,12},{12,0},{1,5},{5,9},{9,13},{13,1},{2,6},{6,10},{... | collective-permute-start | bytes 122888 | tf_op jit(solution)/shard_map/ppermute | solution.py:304
  57.8 0.0 collective-permute-done.4
  57.8 1.5 collective-permute-done.3
  59.3 2.2 collective-permute-done.2
  61.5 0.0 copy-start.1
  61.5 0.9 copy-done.1
  62.4 1.7 shard_map.70
  64.1 0.0 all-to-all-done.1
  64.1 9.0 %all-to-all-start.2 = ((bf16[32,80,128]{2,1,0:T(8,128)(2,1)}), bf16[32,80,128]{2,1,0:T(8,128)(2,1)S(1)}, u32[]{:S(2)}, u32[]{:S(2)}) async-start(bf16[32,80,128]{2,1,0:T(8,128)(2,1)} %shard_map.70), calls=%async_computation.2 | async-start | bytes 1310720 | tf_op jit(solution)/shard_map/all_to_all | solution.py:287
  73.2 0.8 reshape.34
  74.0 0.1 reshape.35
  74.1 11.9 %all-to-all-done.2 = bf16[32,80,128]{2,1,0:T(8,128)(2,1)S(1)} async-done(((bf16[32,80,128]{2,1,0:T(8,128)(2,1)}), bf16[32,80,128]{2,1,0:T(8,128)(2,1)S(1)}, u32[]{:S(2)}, u32[]{:S(2)}) %all-to-all-start.2) | async-done | bytes 655392 | tf_op jit(solution)/shard_map/all_to_all | solution.py:287
  86.0 7.0 %shard_map.73 = (bf16[1024,2560]{1,0:T(8,128)(2,1)S(1)}, f32[32,21,128]{2,1,0:T(8,128)S(1)}) custom-call(bf16[1024,128]{1,0:T(8,128)(2,1)S(1)} %bitcast.27, bf16[2560,128]{1,0:T(8,128)(2,1)S(1)} %bitcast.26, f32[1,128]{1,0:T(1,128)S(1)} %constant_dynamic-slice_fusion.money_ref), custom_call_target="tpu_custom_call" | custom-call | tf_op jit(solution)/shard_map/pallas_call | solution.py:161
  93.0 13.8 %all_to_all.55.got_ref = f32[32,21,128]{2,1,0:T(8,128)S(1)} all-to-all(f32[32,21,128]{2,1,0:T(8,128)S(1)} %get-tuple-element.26), channel_id=1, replica_groups=mesh['y'=4,'zl'=8,'x'=4,'zh'=2,'c'=2] {'y','x','c'}, dimensions={0} | all-to-all | bytes 688128 | tf_op jit(solution)/shard_map/all_to_all | solution.py:287
  106.8 1.5 shard_map.74
  108.3 22.5 %all_to_all.56.got_ref = f32[16,8,128]{2,1,0:T(8,128)S(1)} all-to-all(f32[16,8,128]{2,1,0:T(8,128)S(1)} %get-tuple-element.28), channel_id=1, replica_groups=mesh['y'=4,'zl'=8,'x'=4,'zh'=2,'c'=2] {'zh','zl'}, dimensions={0} | all-to-all | bytes 131072 | tf_op jit(solution)/shard_map/all_to_all | solution.py:287
  130.8 2.6 %shard_map.75 = (f32[32,20,128]{2,1,0:T(8,128)S(1)}, f32[8,128]{1,0:T(8,128)}, f32[1024,2560]{1,0:T(8,128)S(1)}) custom-call(f32[16,8,128]{2,1,0:T(8,128)S(1)} %all_to_all.56.got_ref, bf16[1024,2560]{1,0:T(8,128)(2,1)S(1)} %get-tuple-element.27.refs_0_), custom_call_target="tpu_custom_call" | custom-call | tf_op jit(solution)/shard_map/pallas_call | solution.py:201
  133.4 15.4 %all_to_all.57.got_ref = f32[32,20,128]{2,1,0:T(8,128)S(1)} all-to-all(f32[32,20,128]{2,1,0:T(8,128)S(1)} %get-tuple-element.29), channel_id=1, replica_groups=mesh['y'=4,'zl'=8,'x'=4,'zh'=2,'c'=2] {'y','x','c'}, dimensions={0} | all-to-all | bytes 655360 | tf_op jit(solution)/shard_map/all_to_all | solution.py:287
  148.8 1.1 shard_map.76
  149.9 14.3 %all_to_all.58.got_ref = f32[16,8,128]{2,1,0:T(8,128)S(1)} all-to-all(f32[16,8,128]{2,1,0:T(8,128)S(1)} %shard_map.76), channel_id=1, replica_groups=mesh['y'=4,'zl'=8,'x'=4,'zh'=2,'c'=2] {'zh','zl'}, dimensions={0} | all-to-all | bytes 131072 | tf_op jit(solution)/shard_map/all_to_all | solution.py:287
  164.2 2.1 shard_map.77
  166.4 15.4 %all_to_all.59.got_ref = f32[32,20,128]{2,1,0:T(8,128)S(1)} all-to-all(f32[32,20,128]{2,1,0:T(8,128)S(1)} %get-tuple-element.32), channel_id=1, replica_groups=mesh['y'=4,'zl'=8,'x'=4,'zh'=2,'c'=2] {'y','x','c'}, dimensions={0} | all-to-all | bytes 655360 | tf_op jit(solution)/shard_map/all_to_all | solution.py:287
  181.8 1.1 shard_map.78
  182.9 14.3 %all_to_all.60.got_ref = f32[16,8,128]{2,1,0:T(8,128)S(1)} all-to-all(f32[16,8,128]{2,1,0:T(8,128)S(1)} %shard_map.78), channel_id=1, replica_groups=mesh['y'=4,'zl'=8,'x'=4,'zh'=2,'c'=2] {'zh','zl'}, dimensions={0} | all-to-all | bytes 131072 | tf_op jit(solution)/shard_map/all_to_all | solution.py:287
  197.2 2.2 shard_map.79
  199.3 5.6 %all-to-all-start.9 = ((f32[32,5,128]{2,1,0:T(8,128)}), f32[32,5,128]{2,1,0:T(8,128)S(1)}, u32[]{:S(2)}, u32[]{:S(2)}) async-start(f32[32,5,128]{2,1,0:T(8,128)} %get-tuple-element.36), calls=%async_computation.9 | async-start | bytes 262144 | tf_op jit(solution)/shard_map/all_to_all | solution.py:287
  205.0 7.7 %all-to-all-done.9 = f32[32,5,128]{2,1,0:T(8,128)S(1)} async-done(((f32[32,5,128]{2,1,0:T(8,128)}), f32[32,5,128]{2,1,0:T(8,128)S(1)}, u32[]{:S(2)}, u32[]{:S(2)}) %all-to-all-start.9) | async-done | bytes 81952 | tf_op jit(solution)/shard_map/all_to_all | solution.py:287
  212.7 3.2 %collective-permute-start.5 = (f32[5,128]{1,0:T(8,128)S(1)}, f32[5,128]{1,0:T(8,128)S(1)}, u32[]{:S(2)}, u32[]{:S(2)}) collective-permute-start(f32[5,128]{1,0:T(8,128)S(1)} %multiply_divide_fusion), channel_id=1, source_target_pairs={{0,2},{2,0},{1,3},{3,1},{4,6},{6,4},{5,7},{7,5},{8,10},{10,8},{9,1... | collective-permute-start | bytes 7688 | tf_op jit(solution)/shard_map/ppermute | solution.py:291
  215.9 3.3 %all-to-all-start.10 = ((f32[4,4,128]{2,1,0:T(4,128)}), f32[4,4,128]{2,1,0:T(4,128)S(1)}, u32[]{:S(2)}, u32[]{:S(2)}) async-start(f32[4,4,128]{2,1,0:T(4,128)} %get-tuple-element.37), calls=%async_computation.10 | async-start | bytes 16384 | tf_op jit(solution)/shard_map/all_to_all | solution.py:287
  219.2 6.6 %collective-permute-done.5 = f32[5,128]{1,0:T(8,128)S(1)} collective-permute-done((f32[5,128]{1,0:T(8,128)S(1)}, f32[5,128]{1,0:T(8,128)S(1)}, u32[]{:S(2)}, u32[]{:S(2)}) %collective-permute-start.5) | collective-permute-done | bytes 2592 | tf_op jit(solution)/shard_map/ppermute | solution.py:291
  225.8 0.1 stack_reshape.8
  225.9 0.1 stack_reshape.9
  226.0 0.7 reshape.37
  226.7 0.0 all-to-all-done.10
  226.7 0.6 copy.10
  (15 shorter events, 0.2 us)
Async XLA Ops:
  0.7 0.9 copy-start.2
  2.9 25.7 %collective-permute-start = (bf16[4,80,128]{2,1,0:T(8,128)(2,1)S(1)}, bf16[4,80,128]{2,1,0:T(8,128)(2,1)S(1)}, u32[]{:S(2)}, u32[]{:S(2)}) collective-permute-start(bf16[4,80,128]{2,1,0:T(8,128)(2,1)S(1)} %get-tuple-element.21), channel_id=1, source_target_pairs={{0,2},{2,0},{1,3},{3,1},{4,6},{6,4},{5,7},{7,5},{8,10},{10,8},{9,1... | collective-permute-start | bytes 245768 | tf_op jit(solution)/shard_map/ppermute | solution.py:291
  19.2 0.9 copy-start.3
  20.9 19.6 %all-to-all-start = ((bf16[32,16,128]{2,1,0:T(8,128)(2,1)}), bf16[32,16,128]{2,1,0:T(8,128)(2,1)S(1)}, u32[]{:S(2)}, u32[]{:S(2)}) async-start(bf16[32,16,128]{2,1,0:T(8,128)(2,1)} %shard_map.71), calls=%async_computation | async-start | bytes 262144 | tf_op jit(solution)/shard_map/all_to_all | solution.py:287
  28.8 4.1 %collective-permute-start.1 = (bf16[4,80,128]{2,1,0:T(8,128)(2,1)S(1)}, bf16[4,80,128]{2,1,0:T(8,128)(2,1)S(1)}, u32[]{:S(2)}, u32[]{:S(2)}) collective-permute-start(bf16[4,80,128]{2,1,0:T(8,128)(2,1)S(1)} %get-tuple-element.23), channel_id=1, source_target_pairs={{0,1},{1,0},{2,3},{3,2},{4,5},{5,4},{6,7},{7,6},{8,9},{9,8},{10,11... | collective-permute-start | bytes 245768 | tf_op jit(solution)/shard_map/ppermute | solution.py:291
  40.4 1.0 copy-start
  42.4 21.8 %all-to-all-start.1 = ((bf16[16,64,128]{2,1,0:T(8,128)(2,1)}), bf16[16,64,128]{2,1,0:T(8,128)(2,1)S(1)}, u32[]{:S(2)}, u32[]{:S(2)}) async-start(bf16[16,64,128]{2,1,0:T(8,128)(2,1)} %shard_map.72), calls=%async_computation.1 | async-start | bytes 524288 | tf_op jit(solution)/shard_map/all_to_all | solution.py:287
  48.4 9.4 %collective-permute-start.4 = (bf16[2,80,128]{2,1,0:T(8,128)(2,1)S(1)}, bf16[2,80,128]{2,1,0:T(8,128)(2,1)S(1)}, u32[]{:S(2)}, u32[]{:S(2)}) collective-permute-start(bf16[2,80,128]{2,1,0:T(8,128)(2,1)S(1)} %pad_maximum_fusion.2), channel_id=1, source_target_pairs={{0,12},{4,0},{8,4},{12,8},{1,13},{5,1},{9,5},{13,9},{2,14},{6,2},{... | collective-permute-start | bytes 122888 | tf_op jit(solution)/shard_map/ppermute | solution.py:304
  52.8 6.5 %collective-permute-start.3 = (bf16[2,80,128]{2,1,0:T(8,128)(2,1)S(1)}, bf16[2,80,128]{2,1,0:T(8,128)(2,1)S(1)}, u32[]{:S(2)}, u32[]{:S(2)}) collective-permute-start(bf16[2,80,128]{2,1,0:T(8,128)(2,1)S(1)} %pad_maximum_fusion.1), channel_id=1, source_target_pairs={{0,8},{4,12},{8,0},{12,4},{1,9},{5,13},{9,1},{13,5},{2,10},{6,14},... | collective-permute-start | bytes 122888 | tf_op jit(solution)/shard_map/ppermute | solution.py:304
  55.2 6.3 %collective-permute-start.2 = (bf16[2,80,128]{2,1,0:T(8,128)(2,1)S(1)}, bf16[2,80,128]{2,1,0:T(8,128)(2,1)S(1)}, u32[]{:S(2)}, u32[]{:S(2)}) collective-permute-start(bf16[2,80,128]{2,1,0:T(8,128)(2,1)S(1)} %pad_maximum_fusion), channel_id=1, source_target_pairs={{0,4},{4,8},{8,12},{12,0},{1,5},{5,9},{9,13},{13,1},{2,6},{6,10},{... | collective-permute-start | bytes 122888 | tf_op jit(solution)/shard_map/ppermute | solution.py:304
  61.5 1.0 copy-start.1
  64.1 21.9 %all-to-all-start.2 = ((bf16[32,80,128]{2,1,0:T(8,128)(2,1)}), bf16[32,80,128]{2,1,0:T(8,128)(2,1)S(1)}, u32[]{:S(2)}, u32[]{:S(2)}) async-start(bf16[32,80,128]{2,1,0:T(8,128)(2,1)} %shard_map.70), calls=%async_computation.2 | async-start | bytes 1310720 | tf_op jit(solution)/shard_map/all_to_all | solution.py:287
  199.3 13.3 %all-to-all-start.9 = ((f32[32,5,128]{2,1,0:T(8,128)}), f32[32,5,128]{2,1,0:T(8,128)S(1)}, u32[]{:S(2)}, u32[]{:S(2)}) async-start(f32[32,5,128]{2,1,0:T(8,128)} %get-tuple-element.36), calls=%async_computation.9 | async-start | bytes 262144 | tf_op jit(solution)/shard_map/all_to_all | solution.py:287
  212.7 13.1 %collective-permute-start.5 = (f32[5,128]{1,0:T(8,128)S(1)}, f32[5,128]{1,0:T(8,128)S(1)}, u32[]{:S(2)}, u32[]{:S(2)}) collective-permute-start(f32[5,128]{1,0:T(8,128)S(1)} %multiply_divide_fusion), channel_id=1, source_target_pairs={{0,2},{2,0},{1,3},{3,1},{4,6},{6,4},{5,7},{7,5},{8,10},{10,8},{9,1... | collective-permute-start | bytes 7688 | tf_op jit(solution)/shard_map/ppermute | solution.py:291
  215.9 10.7 %all-to-all-start.10 = ((f32[4,4,128]{2,1,0:T(4,128)}), f32[4,4,128]{2,1,0:T(4,128)S(1)}, u32[]{:S(2)}, u32[]{:S(2)}) async-start(f32[4,4,128]{2,1,0:T(4,128)} %get-tuple-element.37), calls=%async_computation.10 | async-start | bytes 16384 | tf_op jit(solution)/shard_map/all_to_all | solution.py:287

commit v4 on v3

--- a/solution.py
+++ b/solution.py
@@ -68,33 +68,35 @@
 
 def price_kernel(k, got_ref, *refs):
     if k == 1:
-        values, out_ref, money_ref, lhs = refs
-        for y in range(4):
-            for i in range(5):
-                money_ref[5 * y + i : 5 * y + i + 1, :] = got_ref[8 * y + i, LB : LB + 1, :]
-    else:
-        money_ref, power, out_ref, scale, sums = refs
-    total = got_ref[0, 0:LB, :]
-    for p in range(1, got_ref.shape[0]):
-        total = total + got_ref[p, 0:LB, :]
-    if k == 1:
-        three_parts(money_ref[...] / total, lhs)
+        values, out_ref, money_ref, lhs, money = refs
+        for b in range(LB):
+            row = got_ref[8 * (b // 5) + b % 5, LB : LB + 1, :]
+            money[b : b + 1, :] = row
+            money_ref[b // 5 : b // 5 + 1, 128 * (b % 5) : 128 * (b % 5) + 128] = row
+        total = got_ref[0, 0:LB, :]
+        for p in range(1, got_ref.shape[0]):
+            total = total + got_ref[p, 0:LB, :]
+        three_parts(money[...] / total, lhs)
         products = lax.dot_general(
             lhs[...].astype(jnp.bfloat16), values[...], (((1,), (1,)), ((), ())), preferred_element_type=jnp.float32
         )
         whole = jnp.sum(products, 0, keepdims=True)
         rows = [whole[:, 128 * q : 128 * q + 128] for q in range(GT)]
     else:
+        money_ref, power, out_ref, scale, sums = refs
+        total = got_ref[0]
+        for p in range(1, got_ref.shape[0]):
+            total = total + got_ref[p]
         scale[...] = money_ref[...] / total
 
         def chunk(i, _):
             at = pl.ds(pl.multiple_of(16 * i, 16), 16)
-            even = power[at, 0:128] * scale[0:1, :]
-            odd = power[at, 128:256] * scale[1:2, :]
-            for b in range(2, LB, 2):
-                even = even + power[at, 128 * b : 128 * b + 128] * scale[b : b + 1, :]
-                odd = odd + power[at, 128 * b + 128 : 128 * b + 256] * scale[b + 1 : b + 2, :]
-            sums[at, :] = even + odd
+            two = [None, None]
+            for b in range(LB):
+                part = scale[b // 5 : b // 5 + 1, 128 * (b % 5) : 128 * (b % 5) + 128]
+                term = power[at, 128 * b : 128 * b + 128] * part
+                two[b % 2] = term if two[b % 2] is None else two[b % 2] + term
+            sums[at, :] = two[0] + two[1]
             return 0
 
         lax.fori_loop(0, NGOOD // 16, chunk, 0, unroll=4)
@@ -148,9 +150,13 @@
     accs = tuple(jnp.zeros((8, 128), jnp.float32) for _ in range(LB))
     accs = lax.fori_loop(0, NGOOD // 16, chunk, accs, unroll=2)
     for b in range(LB):
-        rows[b : b + 1, :] = jnp.sum(accs[b], 0, keepdims=True)
+        row = jnp.sum(accs[b], 0, keepdims=True)
+        if k == ITERS:
+            rows[b : b + 1, :] = row
+        else:
+            rows[b // 5 : b // 5 + 1, 128 * (b % 5) : 128 * (b % 5) + 128] = row
     for p in range(out_ref.shape[0]):
-        out_ref[p] = rows[5 * (p // 8) : 5 * (p // 8) + 5, :] if k == ITERS else rows[0:LB, :]
+        out_ref[p] = rows[5 * (p // 8) : 5 * (p // 8) + 5, :] if k == ITERS else rows[0:4, :]
 
 
 VM = pl.BlockSpec(memory_space=pltpu.VMEM)
@@ -182,12 +188,12 @@
 def price_call(k, got, power, money=None):
     payload = jax.ShapeDtypeStruct((16, GT, 128), jnp.float32)
     first = k == 1
-    scratch = [(8, NBUY)] if first else [(LB, 128), (NGOOD, 128)]
+    scratch = [(8, NBUY), (LB, 128)] if first else [(4, 640), (NGOOD, 128)]
     return pl.pallas_call(
         functools.partial(price_kernel, k),
         in_specs=[VM] * (2 if first else 3),
         out_specs=[VM, VM] if first else VM,
-        out_shape=[payload, jax.ShapeDtypeStruct((LB, 128), jnp.float32)] if first else payload,
+        out_shape=[payload, jax.ShapeDtypeStruct((4, 640), jnp.float32)] if first else payload,
         scratch_shapes=[pltpu.VMEM(x, jnp.float32) for x in scratch],
         compiler_params=PARAMS,
     )(*((got, power) if first else (got, money, power)))
@@ -197,13 +203,16 @@
     if k == ITERS:
         outs, specs = [(32, 5, 128), (4, 4, 128)], [VM, VM, pl.BlockSpec(memory_space=pltpu.SMEM), VM]
     else:
-        outs, specs = [(32, LB, 128), (GT, 128), (NGOOD, NBUY)], [VM] * (1 + len(blocks))
+        outs, specs = [(32, 4, 640), (GT, 128), (NGOOD, NBUY)], [VM] * (1 + len(blocks))
     return pl.pallas_call(
         functools.partial(utility_kernel, k),
         in_specs=specs,
         out_specs=[VM] * len(outs),
         out_shape=[jax.ShapeDtypeStruct(o, jnp.float32) for o in outs],
-        scratch_shapes=[pltpu.VMEM((NGOOD, 128), jnp.float32), pltpu.VMEM((24, 128), jnp.float32)],
+        scratch_shapes=[
+            pltpu.VMEM((NGOOD, 128), jnp.float32),
+            pltpu.VMEM((24, 128) if k == ITERS else (8, 640), jnp.float32),
+        ],
         compiler_params=PARAMS,
     )(got, *blocks)
 
@@ -334,8 +343,9 @@
     sent = price_call(3, got, cube, money)
     sent, halves = utility_call(3, exchange(sent, RING), before, zh.reshape(1), square)
     final = exchange(sent, PLANE)
-    five = lambda a, axis: lax.dynamic_slice_in_dim(a, 5 * y, 5, axis)
-    mine_total = jnp.sum(final, 0) * five(money, 0) / jnp.sum(five(got, 1), 0)
+    own = lambda a, axis: lax.dynamic_index_in_dim(a, y, axis, keepdims=False)
+    before = (own(money, 0) / jnp.sum(own(got, 1), 0)).reshape(5, 128)
+    mine_total = jnp.sum(final, 0) * before
     other = swap(mine_total, "zh")
     prices = exchange(lax.optimization_barrier((halves, mine_total))[0], ("y",)).reshape(-1)
     first = jnp.where(zh == 0, mine_total, other).reshape(4, 160)

time: 228 us -> 227 us (level)
  no operation moved by 1% of the time
where the time goes in v4:
time: 227 us; the launch traced here: 226 us
  blocking collectives  94.4 us (42%)
  starting transfers between devices  63.6 us (28%)
  waiting for transfers between devices  38.3 us (17%)
  Pallas kernels  22.4 us (10%)
  local copies, waits for them, and re-layouts  6.1 us (3%)
    all_to_all x6, blocking collectives, exchange(): return lax.all_to_all(x, axes, 0, 0, tiled=True)  94.4 us
    all_to_all x5, starting transfers between devices, exchange(): return lax.all_to_all(x, axes, 0, 0, tiled=True)  31.7 us
    all_to_all x5, waiting for transfers between devices, exchange(): return lax.all_to_all(x, axes, 0, 0, tiled=True)  27.1 us
    ppermute x3, starting transfers between devices, swap(): return lax.ppermute(x, axis, [(0, 1), (1, 0)])  22.6 us
    ppermute x3, starting transfers between devices, embeddings(): two = lax.ppermute(two, 'x', [(i, (i + d) % 4) for i in range(4)])  9.33 us
    ppermute x3, waiting for transfers between devices, swap(): return lax.ppermute(x, axis, [(0, 1), (1, 0)])  7.47 us
    pallas_call x1, Pallas kernels, values_call(): pl.pallas_call(values_kernel, grid=(GT,), in_specs=[pl.BlockSpec((128, E)...  7.02 us
    pallas_call x3, Pallas kernels, utility_call(): pl.pallas_call(functools.partial(utility_kernel, k), in_specs=specs, out_...  6.83 us
  transfers between devices with their start and end apart: 11, of which 7 were waited for; matrix products, arithmetic and copies ran while one was open for 1% of the time, Pallas kernels for 1%

profile of v4, /device:TPU:1, one launch (start us, length us, event | category | flops | bytes accessed | tf_op | source)
XLA Modules:
  0.0 225.9 jit_solution(2801490312728294130)
XLA Ops:
  0.6 0.1 pad_add_fusion.place_ref
  0.7 0.0 copy-start.2
  0.7 0.9 copy-done.2
  1.6 1.3 shard_map.68
  2.9 16.3 %collective-permute-start = (bf16[4,80,128]{2,1,0:T(8,128)(2,1)S(1)}, bf16[4,80,128]{2,1,0:T(8,128)(2,1)S(1)}, u32[]{:S(2)}, u32[]{:S(2)}) collective-permute-start(bf16[4,80,128]{2,1,0:T(8,128)(2,1)S(1)} %get-tuple-element.21), channel_id=1, source_target_pairs={{0,2},{2,0},{1,3},{3,1},{4,6},{6,4},{5,7},{7,5},{8,10},{10,8},{9,1... | collective-permute-start | bytes 245768 | tf_op jit(solution)/shard_map/ppermute | solution.py:300
  19.2 0.0 copy-start.3
  19.2 0.9 copy-done.3
  20.1 0.7 shard_map.71
  20.9 7.8 %all-to-all-start = ((bf16[32,16,128]{2,1,0:T(8,128)(2,1)}), bf16[32,16,128]{2,1,0:T(8,128)(2,1)S(1)}, u32[]{:S(2)}, u32[]{:S(2)}) async-start(bf16[32,16,128]{2,1,0:T(8,128)(2,1)} %shard_map.71), calls=%async_computation | async-start | bytes 262144 | tf_op jit(solution)/shard_map/all_to_all | solution.py:296
  28.6 0.0 collective-permute-done.came_ref
  28.7 0.1 shard_map.69
  28.8 3.1 %collective-permute-start.1 = (bf16[4,80,128]{2,1,0:T(8,128)(2,1)S(1)}, bf16[4,80,128]{2,1,0:T(8,128)(2,1)S(1)}, u32[]{:S(2)}, u32[]{:S(2)}) collective-permute-start(bf16[4,80,128]{2,1,0:T(8,128)(2,1)S(1)} %get-tuple-element.23), channel_id=1, source_target_pairs={{0,1},{1,0},{2,3},{3,2},{4,5},{5,4},{6,7},{7,6},{8,9},{9,8},{10,11... | collective-permute-start | bytes 245768 | tf_op jit(solution)/shard_map/ppermute | solution.py:300
  31.9 0.9 collective-permute-done.1
  32.8 7.6 %all-to-all-done.got_ref = bf16[32,16,128]{2,1,0:T(8,128)(2,1)S(1)} async-done(((bf16[32,16,128]{2,1,0:T(8,128)(2,1)}), bf16[32,16,128]{2,1,0:T(8,128)(2,1)S(1)}, u32[]{:S(2)}, u32[]{:S(2)}) %all-to-all-start) | async-done | bytes 131104 | tf_op jit(solution)/shard_map/all_to_all | solution.py:296
  40.4 0.0 copy-start
  40.4 0.9 copy-done
  41.4 1.0 shard_map.72
  42.4 6.0 %all-to-all-start.1 = ((bf16[16,64,128]{2,1,0:T(8,128)(2,1)}), bf16[16,64,128]{2,1,0:T(8,128)(2,1)S(1)}, u32[]{:S(2)}, u32[]{:S(2)}) async-start(bf16[16,64,128]{2,1,0:T(8,128)(2,1)} %shard_map.72), calls=%async_computation.1 | async-start | bytes 524288 | tf_op jit(solution)/shard_map/all_to_all | solution.py:296
  48.4 4.4 %collective-permute-start.4 = (bf16[2,80,128]{2,1,0:T(8,128)(2,1)S(1)}, bf16[2,80,128]{2,1,0:T(8,128)(2,1)S(1)}, u32[]{:S(2)}, u32[]{:S(2)}) collective-permute-start(bf16[2,80,128]{2,1,0:T(8,128)(2,1)S(1)} %pad_maximum_fusion.2), channel_id=1, source_target_pairs={{0,12},{4,0},{8,4},{12,8},{1,13},{5,1},{9,5},{13,9},{2,14},{6,2},{... | collective-permute-start | bytes 122888 | tf_op jit(solution)/shard_map/ppermute | solution.py:313
  52.8 2.4 %collective-permute-start.3 = (bf16[2,80,128]{2,1,0:T(8,128)(2,1)S(1)}, bf16[2,80,128]{2,1,0:T(8,128)(2,1)S(1)}, u32[]{:S(2)}, u32[]{:S(2)}) collective-permute-start(bf16[2,80,128]{2,1,0:T(8,128)(2,1)S(1)} %pad_maximum_fusion.1), channel_id=1, source_target_pairs={{0,8},{4,12},{8,0},{12,4},{1,9},{5,13},{9,1},{13,5},{2,10},{6,14},... | collective-permute-start | bytes 122888 | tf_op jit(solution)/shard_map/ppermute | solution.py:313
  55.2 2.5 %collective-permute-start.2 = (bf16[2,80,128]{2,1,0:T(8,128)(2,1)S(1)}, bf16[2,80,128]{2,1,0:T(8,128)(2,1)S(1)}, u32[]{:S(2)}, u32[]{:S(2)}) collective-permute-start(bf16[2,80,128]{2,1,0:T(8,128)(2,1)S(1)} %pad_maximum_fusion), channel_id=1, source_target_pairs={{0,4},{4,8},{8,12},{12,0},{1,5},{5,9},{9,13},{13,1},{2,6},{6,10},{... | collective-permute-start | bytes 122888 | tf_op jit(solution)/shard_map/ppermute | solution.py:313
  57.8 0.0 collective-permute-done.4
  57.8 1.5 collective-permute-done.3
  59.3 2.2 collective-permute-done.2
  61.5 0.0 copy-start.1
  61.5 0.9 copy-done.1
  62.5 1.7 shard_map.70
  64.1 0.0 all-to-all-done.1
  64.1 9.0 %all-to-all-start.2 = ((bf16[32,80,128]{2,1,0:T(8,128)(2,1)}), bf16[32,80,128]{2,1,0:T(8,128)(2,1)S(1)}, u32[]{:S(2)}, u32[]{:S(2)}) async-start(bf16[32,80,128]{2,1,0:T(8,128)(2,1)} %shard_map.70), calls=%async_computation.2 | async-start | bytes 1310720 | tf_op jit(solution)/shard_map/all_to_all | solution.py:296
  73.2 0.8 reshape.37
  74.0 0.1 reshape.38
  74.1 11.9 %all-to-all-done.2 = bf16[32,80,128]{2,1,0:T(8,128)(2,1)S(1)} async-done(((bf16[32,80,128]{2,1,0:T(8,128)(2,1)}), bf16[32,80,128]{2,1,0:T(8,128)(2,1)S(1)}, u32[]{:S(2)}, u32[]{:S(2)}) %all-to-all-start.2) | async-done | bytes 655392 | tf_op jit(solution)/shard_map/all_to_all | solution.py:296
  86.0 7.0 %shard_map.73 = (bf16[1024,2560]{1,0:T(8,128)(2,1)S(1)}, f32[32,21,128]{2,1,0:T(8,128)S(1)}) custom-call(bf16[1024,128]{1,0:T(8,128)(2,1)S(1)} %bitcast.37, bf16[2560,128]{1,0:T(8,128)(2,1)S(1)} %bitcast.36, f32[1,128]{1,0:T(1,128)S(1)} %constant_dynamic-slice_fusion.money_ref), custom_call_target="tpu_custom_call" | custom-call | tf_op jit(solution)/shard_map/pallas_call | solution.py:167
  93.1 13.8 %all_to_all.55.got_ref = f32[32,21,128]{2,1,0:T(8,128)S(1)} all-to-all(f32[32,21,128]{2,1,0:T(8,128)S(1)} %get-tuple-element.26), channel_id=1, replica_groups=mesh['y'=4,'zl'=8,'x'=4,'zh'=2,'c'=2] {'y','x','c'}, dimensions={0} | all-to-all | bytes 688128 | tf_op jit(solution)/shard_map/all_to_all | solution.py:296
  106.8 1.5 shard_map.74
  108.3 22.5 %all_to_all.56.got_ref = f32[16,8,128]{2,1,0:T(8,128)S(1)} all-to-all(f32[16,8,128]{2,1,0:T(8,128)S(1)} %get-tuple-element.28), channel_id=1, replica_groups=mesh['y'=4,'zl'=8,'x'=4,'zh'=2,'c'=2] {'zh','zl'}, dimensions={0} | all-to-all | bytes 131072 | tf_op jit(solution)/shard_map/all_to_all | solution.py:296
  130.9 2.6 %shard_map.75 = (f32[32,4,640]{2,1,0:T(4,128)S(1)}, f32[8,128]{1,0:T(8,128)}, f32[1024,2560]{1,0:T(8,128)S(1)}) custom-call(f32[16,8,128]{2,1,0:T(8,128)S(1)} %all_to_all.56.got_ref, bf16[1024,2560]{1,0:T(8,128)(2,1)S(1)} %get-tuple-element.27.refs_0_), custom_call_target="tpu_custom_call" | custom-call | tf_op jit(solution)/shard_map/pallas_call | solution.py:207
  133.4 14.8 %all_to_all.57.got_ref = f32[32,4,640]{2,1,0:T(4,128)S(1)} all-to-all(f32[32,4,640]{2,1,0:T(4,128)S(1)} %get-tuple-element.29), channel_id=1, replica_groups=mesh['y'=4,'zl'=8,'x'=4,'zh'=2,'c'=2] {'y','x','c'}, dimensions={0} | all-to-all | bytes 655360 | tf_op jit(solution)/shard_map/all_to_all | solution.py:296
  148.2 1.1 shard_map.76
  149.3 14.3 %all_to_all.58.got_ref = f32[16,8,128]{2,1,0:T(8,128)S(1)} all-to-all(f32[16,8,128]{2,1,0:T(8,128)S(1)} %shard_map.76), channel_id=1, replica_groups=mesh['y'=4,'zl'=8,'x'=4,'zh'=2,'c'=2] {'zh','zl'}, dimensions={0} | all-to-all | bytes 131072 | tf_op jit(solution)/shard_map/all_to_all | solution.py:296
  163.6 2.1 shard_map.77
  165.7 14.7 %all_to_all.59.got_ref = f32[32,4,640]{2,1,0:T(4,128)S(1)} all-to-all(f32[32,4,640]{2,1,0:T(4,128)S(1)} %get-tuple-element.32), channel_id=1, replica_groups=mesh['y'=4,'zl'=8,'x'=4,'zh'=2,'c'=2] {'y','x','c'}, dimensions={0} | all-to-all | bytes 655360 | tf_op jit(solution)/shard_map/all_to_all | solution.py:296
  180.4 1.1 shard_map.78
  181.5 14.3 %all_to_all.60.got_ref = f32[16,8,128]{2,1,0:T(8,128)S(1)} all-to-all(f32[16,8,128]{2,1,0:T(8,128)S(1)} %shard_map.78), channel_id=1, replica_groups=mesh['y'=4,'zl'=8,'x'=4,'zh'=2,'c'=2] {'zh','zl'}, dimensions={0} | all-to-all | bytes 131072 | tf_op jit(solution)/shard_map/all_to_all | solution.py:296
  195.8 2.2 shard_map.79
  198.0 5.6 %all-to-all-start.9 = ((f32[32,5,128]{2,1,0:T(8,128)}), f32[32,5,128]{2,1,0:T(8,128)S(1)}, u32[]{:S(2)}, u32[]{:S(2)}) async-start(f32[32,5,128]{2,1,0:T(8,128)} %get-tuple-element.36), calls=%async_computation.9 | async-start | bytes 262144 | tf_op jit(solution)/shard_map/all_to_all | solution.py:296
  203.6 0.1 dynamic-slice_reduce_fusion
  203.7 7.6 %all-to-all-done.9 = f32[32,5,128]{2,1,0:T(8,128)S(1)} async-done(((f32[32,5,128]{2,1,0:T(8,128)}), f32[32,5,128]{2,1,0:T(8,128)S(1)}, u32[]{:S(2)}, u32[]{:S(2)}) %all-to-all-start.9) | async-done | bytes 81952 | tf_op jit(solution)/shard_map/all_to_all | solution.py:296
  211.4 3.2 %collective-permute-start.5 = (f32[5,128]{1,0:T(8,128)S(1)}, f32[5,128]{1,0:T(8,128)S(1)}, u32[]{:S(2)}, u32[]{:S(2)}) collective-permute-start(f32[5,128]{1,0:T(8,128)S(1)} %fusion), channel_id=1, source_target_pairs={{0,2},{2,0},{1,3},{3,1},{4,6},{6,4},{5,7},{7,5},{8,10},{10,8},{9,1... | collective-permute-start | bytes 7688 | tf_op jit(solution)/shard_map/ppermute | solution.py:300
  214.6 3.3 %all-to-all-start.10 = ((f32[4,4,128]{2,1,0:T(4,128)}), f32[4,4,128]{2,1,0:T(4,128)S(1)}, u32[]{:S(2)}, u32[]{:S(2)}) async-start(f32[4,4,128]{2,1,0:T(4,128)} %get-tuple-element.37), calls=%async_computation.10 | async-start | bytes 16384 | tf_op jit(solution)/shard_map/all_to_all | solution.py:296
  217.9 6.6 %collective-permute-done.5 = f32[5,128]{1,0:T(8,128)S(1)} collective-permute-done((f32[5,128]{1,0:T(8,128)S(1)}, f32[5,128]{1,0:T(8,128)S(1)}, u32[]{:S(2)}, u32[]{:S(2)}) %collective-permute-start.5) | collective-permute-done | bytes 2592 | tf_op jit(solution)/shard_map/ppermute | solution.py:300
  224.4 0.1 stack_reshape.6
  224.5 0.1 stack_reshape.7
  224.6 0.7 reshape.40
  225.3 0.0 all-to-all-done.10
  225.3 0.6 copy.8
  (15 shorter events, 0.2 us)
Async XLA Ops:
  0.7 0.9 copy-start.2
  2.9 25.7 %collective-permute-start = (bf16[4,80,128]{2,1,0:T(8,128)(2,1)S(1)}, bf16[4,80,128]{2,1,0:T(8,128)(2,1)S(1)}, u32[]{:S(2)}, u32[]{:S(2)}) collective-permute-start(bf16[4,80,128]{2,1,0:T(8,128)(2,1)S(1)} %get-tuple-element.21), channel_id=1, source_target_pairs={{0,2},{2,0},{1,3},{3,1},{4,6},{6,4},{5,7},{7,5},{8,10},{10,8},{9,1... | collective-permute-start | bytes 245768 | tf_op jit(solution)/shard_map/ppermute | solution.py:300
  19.2 0.9 copy-start.3
  20.9 19.6 %all-to-all-start = ((bf16[32,16,128]{2,1,0:T(8,128)(2,1)}), bf16[32,16,128]{2,1,0:T(8,128)(2,1)S(1)}, u32[]{:S(2)}, u32[]{:S(2)}) async-start(bf16[32,16,128]{2,1,0:T(8,128)(2,1)} %shard_map.71), calls=%async_computation | async-start | bytes 262144 | tf_op jit(solution)/shard_map/all_to_all | solution.py:296
  28.8 4.1 %collective-permute-start.1 = (bf16[4,80,128]{2,1,0:T(8,128)(2,1)S(1)}, bf16[4,80,128]{2,1,0:T(8,128)(2,1)S(1)}, u32[]{:S(2)}, u32[]{:S(2)}) collective-permute-start(bf16[4,80,128]{2,1,0:T(8,128)(2,1)S(1)} %get-tuple-element.23), channel_id=1, source_target_pairs={{0,1},{1,0},{2,3},{3,2},{4,5},{5,4},{6,7},{7,6},{8,9},{9,8},{10,11... | collective-permute-start | bytes 245768 | tf_op jit(solution)/shard_map/ppermute | solution.py:300
  40.4 1.0 copy-start
  42.4 21.8 %all-to-all-start.1 = ((bf16[16,64,128]{2,1,0:T(8,128)(2,1)}), bf16[16,64,128]{2,1,0:T(8,128)(2,1)S(1)}, u32[]{:S(2)}, u32[]{:S(2)}) async-start(bf16[16,64,128]{2,1,0:T(8,128)(2,1)} %shard_map.72), calls=%async_computation.1 | async-start | bytes 524288 | tf_op jit(solution)/shard_map/all_to_all | solution.py:296
  48.4 9.4 %collective-permute-start.4 = (bf16[2,80,128]{2,1,0:T(8,128)(2,1)S(1)}, bf16[2,80,128]{2,1,0:T(8,128)(2,1)S(1)}, u32[]{:S(2)}, u32[]{:S(2)}) collective-permute-start(bf16[2,80,128]{2,1,0:T(8,128)(2,1)S(1)} %pad_maximum_fusion.2), channel_id=1, source_target_pairs={{0,12},{4,0},{8,4},{12,8},{1,13},{5,1},{9,5},{13,9},{2,14},{6,2},{... | collective-permute-start | bytes 122888 | tf_op jit(solution)/shard_map/ppermute | solution.py:313
  52.8 6.5 %collective-permute-start.3 = (bf16[2,80,128]{2,1,0:T(8,128)(2,1)S(1)}, bf16[2,80,128]{2,1,0:T(8,128)(2,1)S(1)}, u32[]{:S(2)}, u32[]{:S(2)}) collective-permute-start(bf16[2,80,128]{2,1,0:T(8,128)(2,1)S(1)} %pad_maximum_fusion.1), channel_id=1, source_target_pairs={{0,8},{4,12},{8,0},{12,4},{1,9},{5,13},{9,1},{13,5},{2,10},{6,14},... | collective-permute-start | bytes 122888 | tf_op jit(solution)/shard_map/ppermute | solution.py:313
  55.2 6.3 %collective-permute-start.2 = (bf16[2,80,128]{2,1,0:T(8,128)(2,1)S(1)}, bf16[2,80,128]{2,1,0:T(8,128)(2,1)S(1)}, u32[]{:S(2)}, u32[]{:S(2)}) collective-permute-start(bf16[2,80,128]{2,1,0:T(8,128)(2,1)S(1)} %pad_maximum_fusion), channel_id=1, source_target_pairs={{0,4},{4,8},{8,12},{12,0},{1,5},{5,9},{9,13},{13,1},{2,6},{6,10},{... | collective-permute-start | bytes 122888 | tf_op jit(solution)/shard_map/ppermute | solution.py:313
  61.5 1.0 copy-start.1
  64.1 21.9 %all-to-all-start.2 = ((bf16[32,80,128]{2,1,0:T(8,128)(2,1)}), bf16[32,80,128]{2,1,0:T(8,128)(2,1)S(1)}, u32[]{:S(2)}, u32[]{:S(2)}) async-start(bf16[32,80,128]{2,1,0:T(8,128)(2,1)} %shard_map.70), calls=%async_computation.2 | async-start | bytes 1310720 | tf_op jit(solution)/shard_map/all_to_all | solution.py:296
  198.0 13.3 %all-to-all-start.9 = ((f32[32,5,128]{2,1,0:T(8,128)}), f32[32,5,128]{2,1,0:T(8,128)S(1)}, u32[]{:S(2)}, u32[]{:S(2)}) async-start(f32[32,5,128]{2,1,0:T(8,128)} %get-tuple-element.36), calls=%async_computation.9 | async-start | bytes 262144 | tf_op jit(solution)/shard_map/all_to_all | solution.py:296
  211.4 13.1 %collective-permute-start.5 = (f32[5,128]{1,0:T(8,128)S(1)}, f32[5,128]{1,0:T(8,128)S(1)}, u32[]{:S(2)}, u32[]{:S(2)}) collective-permute-start(f32[5,128]{1,0:T(8,128)S(1)} %fusion), channel_id=1, source_target_pairs={{0,2},{2,0},{1,3},{3,1},{4,6},{6,4},{5,7},{7,5},{8,10},{10,8},{9,1... | collective-permute-start | bytes 7688 | tf_op jit(solution)/shard_map/ppermute | solution.py:300
  214.6 10.7 %all-to-all-start.10 = ((f32[4,4,128]{2,1,0:T(4,128)}), f32[4,4,128]{2,1,0:T(4,128)S(1)}, u32[]{:S(2)}, u32[]{:S(2)}) async-start(f32[4,4,128]{2,1,0:T(4,128)} %get-tuple-element.37), calls=%async_computation.10 | async-start | bytes 16384 | tf_op jit(solution)/shard_map/all_to_all | solution.py:296

commit v5 on v4

--- a/solution.py
+++ b/solution.py
@@ -217,7 +217,7 @@
     )(got, *blocks)
 
 
-def pack_kernel(place_ref, hidden_ref, keep_ref, go_ref):
+def pack_kernel(place_ref, hidden_ref, goods_ref, keep_ref, go_ref, tiles_ref):
     x, zh, c = place_ref[0], place_ref[1], place_ref[2]
     rows = hidden_ref[...].astype(jnp.float32).T
 
@@ -240,6 +240,12 @@
             def _(at=at, part=part):
                 go_ref[at] = part
 
+    for t in range(16):
+        top = goods_ref[0:16, 128 * t : 128 * t + 128].astype(jnp.float32)
+        low = goods_ref[16:32, 128 * t : 128 * t + 128].astype(jnp.float32)
+        tiles_ref[2 * t] = jnp.concatenate([top[:, 0:64], low[:, 0:64]], 1).astype(jnp.bfloat16)
+        tiles_ref[2 * t + 1] = jnp.concatenate([top[:, 64:128], low[:, 64:128]], 1).astype(jnp.bfloat16)
+
 
 def pair_kernel(mine_ref, came_ref, here_ref, across_ref):
     for d in range(4):
@@ -249,31 +255,21 @@
 
 
 def buyers_kernel(place_ref, proj_ref, *refs):
-    got, (out_ref, weights) = refs[:8], refs[8:]
-    x, zh, c = place_ref[0], place_ref[1], place_ref[2]
+    got, out_ref = refs[:8], refs[8]
+    x, c = place_ref[0], place_ref[2]
     total = jnp.zeros((80, E), jnp.float32)
     for q in range(8):
-        at = ((x + 4 - q // 2) & 3) * 4 + ((c + q % 2) & 1)
-        weights[q, 0:64] = proj_ref[at + 2 * zh]
-        weights[q, 64:128] = proj_ref[at + 2 - 2 * zh]
-        total = total + jnp.dot(got[q][...], weights[q], preferred_element_type=jnp.float32)
+        at = ((x + 4 - q // 2) & 3) * 2 + ((c + q % 2) & 1)
+        total = total + jnp.dot(got[q][...], proj_ref[at], preferred_element_type=jnp.float32)
     emb = total.astype(jnp.bfloat16)
     for p in range(out_ref.shape[0]):
         out_ref[p] = emb
 
 
-def tiles_kernel(hidden_ref, out_ref):
-    for t in range(16):
-        top = hidden_ref[0:16, 128 * t : 128 * t + 128].astype(jnp.float32)
-        low = hidden_ref[16:32, 128 * t : 128 * t + 128].astype(jnp.float32)
-        out_ref[2 * t] = jnp.concatenate([top[:, 0:64], low[:, 0:64]], 1).astype(jnp.bfloat16)
-        out_ref[2 * t + 1] = jnp.concatenate([top[:, 64:128], low[:, 64:128]], 1).astype(jnp.bfloat16)
-
-
 def goods_kernel(got_ref, proj_ref, out_ref):
     hidden = got_ref[...].reshape(512, 128).astype(jnp.float32).T.astype(jnp.bfloat16)
     halves = [
-        jnp.dot(hidden[64 * h : 64 * h + 64], proj_ref[:, h].reshape(512, E), preferred_element_type=jnp.float32)
+        jnp.dot(hidden[64 * h : 64 * h + 64], proj_ref[h].reshape(512, E), preferred_element_type=jnp.float32)
         for h in range(2)
     ]
     emb = (halves[0] + halves[1]).astype(jnp.bfloat16)
@@ -303,7 +299,8 @@
 def embeddings(buyer_hidden, goods_hidden, buyer_proj, goods_proj, place):
     bf16 = jnp.bfloat16
     shape = jax.ShapeDtypeStruct
-    keep, go = small_call(pack_kernel, (shape((4, 80, 128), bf16),) * 2, place, buyer_hidden.T, smem=1)
+    outs = (shape((4, 80, 128), bf16), shape((4, 80, 128), bf16), shape((32, 16, 128), bf16))
+    keep, go, tiles = small_call(pack_kernel, outs, place, buyer_hidden.T, goods_hidden.T, smem=1)
     came = swap(go, "zh")
     here, across = small_call(pair_kernel, (shape((4, 80, 128), bf16),) * 2, keep, came)
     across = swap(across, "c")
@@ -312,14 +309,12 @@
         two = jnp.stack([here[d], across[d]])
         two = lax.ppermute(two, "x", [(i, (i + d) % 4) for i in range(4)])
         parts += [two[0], two[1]]
-    tiles = small_call(tiles_kernel, shape((32, 16, 128), bf16), goods_hidden.T)
     tiles = exchange(tiles, ("y", "zl"))
-    goods_own = small_call(goods_kernel, shape((16, 64, E), bf16), tiles, goods_proj.reshape(32, 2, 16, E))
+    goods_own = small_call(goods_kernel, shape((16, 64, E), bf16), tiles, goods_proj.reshape(32, 2, 16, E).transpose(1, 0, 2, 3))
     goods_emb = exchange(goods_own, RING)
-    buyer_own = small_call(
-        buyers_kernel, shape((32, 80, E), bf16), place, buyer_proj.reshape(16, 64, E), *parts,
-        scratch=(pltpu.VMEM((8, 128, E), bf16),), smem=1,
-    )
+    proj = buyer_proj.reshape(4, 2, 2, 64, E)
+    proj = jnp.where(place[1] == 0, proj, proj[:, ::-1]).transpose(0, 2, 1, 3, 4).reshape(8, 128, E)
+    buyer_own = small_call(buyers_kernel, shape((32, 80, E), bf16), place, proj, *parts, smem=1)
     buyer_own, goods_emb = lax.optimization_barrier((buyer_own, goods_emb))
     buyer_emb = exchange(buyer_own, PLANE)
     return buyer_emb.reshape(-1, E), goods_emb.reshape(-1, E)

time: 227 us -> 225 us (level)
    pallas_call x5 -> x4, Pallas kernels: 4.83 us -> 4.81 us  [small_call(): pl.pallas_call(kernel, in_specs=[pl.BlockSpec(memory_space=pltpu.SMEM)] *...]
  transfers between devices with their start and end apart: 11 -> 11, of which waited for: 7 -> 7; matrix products, arithmetic and copies ran while one was open for 1% -> 2% of each run, Pallas kernels for 1% -> 1%
where the time goes in v5:
time: 225 us; the launch traced here: 224 us
  blocking collectives  93.5 us (42%)
  starting transfers between devices  64.5 us (29%)
  waiting for transfers between devices  36.2 us (16%)
  Pallas kernels  22.4 us (10%)
  local copies, waits for them, and re-layouts  6.15 us (3%)
    all_to_all x6, blocking collectives, exchange(): return lax.all_to_all(x, axes, 0, 0, tiled=True)  93.5 us
    all_to_all x5, starting transfers between devices, exchange(): return lax.all_to_all(x, axes, 0, 0, tiled=True)  32.6 us
    all_to_all x5, waiting for transfers between devices, exchange(): return lax.all_to_all(x, axes, 0, 0, tiled=True)  25.1 us
    ppermute x3, starting transfers between devices, swap(): return lax.ppermute(x, axis, [(0, 1), (1, 0)])  22.6 us
    ppermute x3, starting transfers between devices, embeddings(): two = lax.ppermute(two, 'x', [(i, (i + d) % 4) for i in range(4)])  9.33 us
    ppermute x3, waiting for transfers between devices, swap(): return lax.ppermute(x, axis, [(0, 1), (1, 0)])  7.47 us
    pallas_call x1, Pallas kernels, values_call(): pl.pallas_call(values_kernel, grid=(GT,), in_specs=[pl.BlockSpec((128, E)...  7.03 us
    pallas_call x3, Pallas kernels, utility_call(): pl.pallas_call(functools.partial(utility_kernel, k), in_specs=specs, out_...  6.84 us
  transfers between devices with their start and end apart: 11, of which 7 were waited for; matrix products, arithmetic and copies ran while one was open for 2% of the time, Pallas kernels for 1%

profile of v5, /device:TPU:1, one launch (start us, length us, event | category | flops | bytes accessed | tf_op | source)
XLA Modules:
  0.0 224.0 jit_solution(12220628659528455198)
XLA Ops:
  0.6 0.1 pad_add_fusion.place_ref
  0.7 0.0 copy-start
  0.7 0.9 copy-done
  1.6 0.0 copy-start.1
  1.6 0.9 copy-done.1
  2.5 2.1 shard_map.68
  4.6 16.2 %collective-permute-start = (bf16[4,80,128]{2,1,0:T(8,128)(2,1)S(1)}, bf16[4,80,128]{2,1,0:T(8,128)(2,1)S(1)}, u32[]{:S(2)}, u32[]{:S(2)}) collective-permute-start(bf16[4,80,128]{2,1,0:T(8,128)(2,1)S(1)} %get-tuple-element.22), channel_id=1, source_target_pairs={{0,2},{2,0},{1,3},{3,1},{4,6},{6,4},{5,7},{7,5},{8,10},{10,8},{9,1... | collective-permute-start | bytes 245768 | tf_op jit(solution)/shard_map/ppermute | solution.py:296
  20.9 7.8 %all-to-all-start = ((bf16[32,16,128]{2,1,0:T(8,128)(2,1)}), bf16[32,16,128]{2,1,0:T(8,128)(2,1)S(1)}, u32[]{:S(2)}, u32[]{:S(2)}) async-start(bf16[32,16,128]{2,1,0:T(8,128)(2,1)} %get-tuple-element.25), calls=%async_computation | async-start | bytes 262144 | tf_op jit(solution)/shard_map/all_to_all | solution.py:292
  28.7 1.0 copy.10
  29.6 0.1 reverse_select_fusion
  29.7 1.0 copy.13
  30.7 0.0 collective-permute-done.came_ref
  30.7 0.1 shard_map.69
  30.8 3.1 %collective-permute-start.1 = (bf16[4,80,128]{2,1,0:T(8,128)(2,1)S(1)}, bf16[4,80,128]{2,1,0:T(8,128)(2,1)S(1)}, u32[]{:S(2)}, u32[]{:S(2)}) collective-permute-start(bf16[4,80,128]{2,1,0:T(8,128)(2,1)S(1)} %get-tuple-element.24), channel_id=1, source_target_pairs={{0,1},{1,0},{2,3},{3,2},{4,5},{5,4},{6,7},{7,6},{8,9},{9,8},{10,11... | collective-permute-start | bytes 245768 | tf_op jit(solution)/shard_map/ppermute | solution.py:296
  34.0 0.9 collective-permute-done.1
  34.9 5.6 %all-to-all-done.got_ref = bf16[32,16,128]{2,1,0:T(8,128)(2,1)S(1)} async-done(((bf16[32,16,128]{2,1,0:T(8,128)(2,1)}), bf16[32,16,128]{2,1,0:T(8,128)(2,1)S(1)}, u32[]{:S(2)}, u32[]{:S(2)}) %all-to-all-start) | async-done | bytes 131104 | tf_op jit(solution)/shard_map/all_to_all | solution.py:292
  40.4 1.0 shard_map.71
  41.4 6.0 %all-to-all-start.1 = ((bf16[16,64,128]{2,1,0:T(8,128)(2,1)}), bf16[16,64,128]{2,1,0:T(8,128)(2,1)S(1)}, u32[]{:S(2)}, u32[]{:S(2)}) async-start(bf16[16,64,128]{2,1,0:T(8,128)(2,1)} %shard_map.71), calls=%async_computation.1 | async-start | bytes 524288 | tf_op jit(solution)/shard_map/all_to_all | solution.py:292
  47.4 4.4 %collective-permute-start.4 = (bf16[2,80,128]{2,1,0:T(8,128)(2,1)S(1)}, bf16[2,80,128]{2,1,0:T(8,128)(2,1)S(1)}, u32[]{:S(2)}, u32[]{:S(2)}) collective-permute-start(bf16[2,80,128]{2,1,0:T(8,128)(2,1)S(1)} %pad_maximum_fusion.2), channel_id=1, source_target_pairs={{0,12},{4,0},{8,4},{12,8},{1,13},{5,1},{9,5},{13,9},{2,14},{6,2},{... | collective-permute-start | bytes 122888 | tf_op jit(solution)/shard_map/ppermute | solution.py:310
  51.8 2.4 %collective-permute-start.3 = (bf16[2,80,128]{2,1,0:T(8,128)(2,1)S(1)}, bf16[2,80,128]{2,1,0:T(8,128)(2,1)S(1)}, u32[]{:S(2)}, u32[]{:S(2)}) collective-permute-start(bf16[2,80,128]{2,1,0:T(8,128)(2,1)S(1)} %pad_maximum_fusion.1), channel_id=1, source_target_pairs={{0,8},{4,12},{8,0},{12,4},{1,9},{5,13},{9,1},{13,5},{2,10},{6,14},... | collective-permute-start | bytes 122888 | tf_op jit(solution)/shard_map/ppermute | solution.py:310
  54.3 2.5 %collective-permute-start.2 = (bf16[2,80,128]{2,1,0:T(8,128)(2,1)S(1)}, bf16[2,80,128]{2,1,0:T(8,128)(2,1)S(1)}, u32[]{:S(2)}, u32[]{:S(2)}) collective-permute-start(bf16[2,80,128]{2,1,0:T(8,128)(2,1)S(1)} %pad_maximum_fusion), channel_id=1, source_target_pairs={{0,4},{4,8},{8,12},{12,0},{1,5},{5,9},{9,13},{13,1},{2,6},{6,10},{... | collective-permute-start | bytes 122888 | tf_op jit(solution)/shard_map/ppermute | solution.py:310
  56.8 0.0 collective-permute-done.4
  56.8 1.5 collective-permute-done.3
  58.4 2.2 collective-permute-done.2
  60.5 1.7 shard_map.70
  62.2 0.0 all-to-all-done.1
  62.2 9.9 %all-to-all-start.2 = ((bf16[32,80,128]{2,1,0:T(8,128)(2,1)}), bf16[32,80,128]{2,1,0:T(8,128)(2,1)S(1)}, u32[]{:S(2)}, u32[]{:S(2)}) async-start(bf16[32,80,128]{2,1,0:T(8,128)(2,1)} %shard_map.70), calls=%async_computation.2 | async-start | bytes 1310720 | tf_op jit(solution)/shard_map/all_to_all | solution.py:292
  72.1 0.8 reshape.41
  72.9 0.1 reshape.42
  73.0 11.9 %all-to-all-done.2 = bf16[32,80,128]{2,1,0:T(8,128)(2,1)S(1)} async-done(((bf16[32,80,128]{2,1,0:T(8,128)(2,1)}), bf16[32,80,128]{2,1,0:T(8,128)(2,1)S(1)}, u32[]{:S(2)}, u32[]{:S(2)}) %all-to-all-start.2) | async-done | bytes 655392 | tf_op jit(solution)/shard_map/all_to_all | solution.py:292
  85.0 7.0 %shard_map.72 = (bf16[1024,2560]{1,0:T(8,128)(2,1)S(1)}, f32[32,21,128]{2,1,0:T(8,128)S(1)}) custom-call(bf16[1024,128]{1,0:T(8,128)(2,1)S(1)} %bitcast.43, bf16[2560,128]{1,0:T(8,128)(2,1)S(1)} %bitcast.42, f32[1,128]{1,0:T(1,128)S(1)} %constant_dynamic-slice_fusion.money_ref), custom_call_target="tpu_custom_call" | custom-call | tf_op jit(solution)/shard_map/pallas_call | solution.py:167
  92.0 13.8 %all_to_all.55.got_ref = f32[32,21,128]{2,1,0:T(8,128)S(1)} all-to-all(f32[32,21,128]{2,1,0:T(8,128)S(1)} %get-tuple-element.28), channel_id=1, replica_groups=mesh['y'=4,'zl'=8,'x'=4,'zh'=2,'c'=2] {'y','x','c'}, dimensions={0} | all-to-all | bytes 688128 | tf_op jit(solution)/shard_map/all_to_all | solution.py:292
  105.8 1.5 shard_map.73
  107.3 21.7 %all_to_all.56.got_ref = f32[16,8,128]{2,1,0:T(8,128)S(1)} all-to-all(f32[16,8,128]{2,1,0:T(8,128)S(1)} %get-tuple-element.30), channel_id=1, replica_groups=mesh['y'=4,'zl'=8,'x'=4,'zh'=2,'c'=2] {'zh','zl'}, dimensions={0} | all-to-all | bytes 131072 | tf_op jit(solution)/shard_map/all_to_all | solution.py:292
  128.9 2.6 %shard_map.74 = (f32[32,4,640]{2,1,0:T(4,128)S(1)}, f32[8,128]{1,0:T(8,128)}, f32[1024,2560]{1,0:T(8,128)S(1)}) custom-call(f32[16,8,128]{2,1,0:T(8,128)S(1)} %all_to_all.56.got_ref, bf16[1024,2560]{1,0:T(8,128)(2,1)S(1)} %get-tuple-element.29.refs_0_), custom_call_target="tpu_custom_call" | custom-call | tf_op jit(solution)/shard_map/pallas_call | solution.py:207
  131.5 14.8 %all_to_all.57.got_ref = f32[32,4,640]{2,1,0:T(4,128)S(1)} all-to-all(f32[32,4,640]{2,1,0:T(4,128)S(1)} %get-tuple-element.31), channel_id=1, replica_groups=mesh['y'=4,'zl'=8,'x'=4,'zh'=2,'c'=2] {'y','x','c'}, dimensions={0} | all-to-all | bytes 655360 | tf_op jit(solution)/shard_map/all_to_all | solution.py:292
  146.3 1.1 shard_map.75
  147.4 14.3 %all_to_all.58.got_ref = f32[16,8,128]{2,1,0:T(8,128)S(1)} all-to-all(f32[16,8,128]{2,1,0:T(8,128)S(1)} %shard_map.75), channel_id=1, replica_groups=mesh['y'=4,'zl'=8,'x'=4,'zh'=2,'c'=2] {'zh','zl'}, dimensions={0} | all-to-all | bytes 131072 | tf_op jit(solution)/shard_map/all_to_all | solution.py:292
  161.7 2.1 shard_map.76
  163.8 14.7 %all_to_all.59.got_ref = f32[32,4,640]{2,1,0:T(4,128)S(1)} all-to-all(f32[32,4,640]{2,1,0:T(4,128)S(1)} %get-tuple-element.34), channel_id=1, replica_groups=mesh['y'=4,'zl'=8,'x'=4,'zh'=2,'c'=2] {'y','x','c'}, dimensions={0} | all-to-all | bytes 655360 | tf_op jit(solution)/shard_map/all_to_all | solution.py:292
  178.5 1.1 shard_map.77
  179.6 14.3 %all_to_all.60.got_ref = f32[16,8,128]{2,1,0:T(8,128)S(1)} all-to-all(f32[16,8,128]{2,1,0:T(8,128)S(1)} %shard_map.77), channel_id=1, replica_groups=mesh['y'=4,'zl'=8,'x'=4,'zh'=2,'c'=2] {'zh','zl'}, dimensions={0} | all-to-all | bytes 131072 | tf_op jit(solution)/shard_map/all_to_all | solution.py:292
  193.9 2.2 shard_map.78
  196.1 5.6 %all-to-all-start.9 = ((f32[32,5,128]{2,1,0:T(8,128)}), f32[32,5,128]{2,1,0:T(8,128)S(1)}, u32[]{:S(2)}, u32[]{:S(2)}) async-start(f32[32,5,128]{2,1,0:T(8,128)} %get-tuple-element.38), calls=%async_computation.9 | async-start | bytes 262144 | tf_op jit(solution)/shard_map/all_to_all | solution.py:292
  201.7 0.1 dynamic-slice_reduce_fusion
  201.8 7.6 %all-to-all-done.9 = f32[32,5,128]{2,1,0:T(8,128)S(1)} async-done(((f32[32,5,128]{2,1,0:T(8,128)}), f32[32,5,128]{2,1,0:T(8,128)S(1)}, u32[]{:S(2)}, u32[]{:S(2)}) %all-to-all-start.9) | async-done | bytes 81952 | tf_op jit(solution)/shard_map/all_to_all | solution.py:292
  209.5 3.2 %collective-permute-start.5 = (f32[5,128]{1,0:T(8,128)S(1)}, f32[5,128]{1,0:T(8,128)S(1)}, u32[]{:S(2)}, u32[]{:S(2)}) collective-permute-start(f32[5,128]{1,0:T(8,128)S(1)} %fusion), channel_id=1, source_target_pairs={{0,2},{2,0},{1,3},{3,1},{4,6},{6,4},{5,7},{7,5},{8,10},{10,8},{9,1... | collective-permute-start | bytes 7688 | tf_op jit(solution)/shard_map/ppermute | solution.py:296
  212.7 3.3 %all-to-all-start.10 = ((f32[4,4,128]{2,1,0:T(4,128)}), f32[4,4,128]{2,1,0:T(4,128)S(1)}, u32[]{:S(2)}, u32[]{:S(2)}) async-start(f32[4,4,128]{2,1,0:T(4,128)} %get-tuple-element.39), calls=%async_computation.10 | async-start | bytes 16384 | tf_op jit(solution)/shard_map/all_to_all | solution.py:292
  215.9 6.6 %collective-permute-done.5 = f32[5,128]{1,0:T(8,128)S(1)} collective-permute-done((f32[5,128]{1,0:T(8,128)S(1)}, f32[5,128]{1,0:T(8,128)S(1)}, u32[]{:S(2)}, u32[]{:S(2)}) %collective-permute-start.5) | collective-permute-done | bytes 2592 | tf_op jit(solution)/shard_map/ppermute | solution.py:296
  222.5 0.1 stack_reshape.6
  222.6 0.1 stack_reshape.7
  222.7 0.7 reshape.44
  223.4 0.0 all-to-all-done.10
  223.4 0.6 copy.15
  (15 shorter events, 0.2 us)
Async XLA Ops:
  0.7 0.9 copy-start
  1.6 0.9 copy-start.1
  4.6 26.1 %collective-permute-start = (bf16[4,80,128]{2,1,0:T(8,128)(2,1)S(1)}, bf16[4,80,128]{2,1,0:T(8,128)(2,1)S(1)}, u32[]{:S(2)}, u32[]{:S(2)}) collective-permute-start(bf16[4,80,128]{2,1,0:T(8,128)(2,1)S(1)} %get-tuple-element.22), channel_id=1, source_target_pairs={{0,2},{2,0},{1,3},{3,1},{4,6},{6,4},{5,7},{7,5},{8,10},{10,8},{9,1... | collective-permute-start | bytes 245768 | tf_op jit(solution)/shard_map/ppermute | solution.py:296
  20.9 19.6 %all-to-all-start = ((bf16[32,16,128]{2,1,0:T(8,128)(2,1)}), bf16[32,16,128]{2,1,0:T(8,128)(2,1)S(1)}, u32[]{:S(2)}, u32[]{:S(2)}) async-start(bf16[32,16,128]{2,1,0:T(8,128)(2,1)} %get-tuple-element.25), calls=%async_computation | async-start | bytes 262144 | tf_op jit(solution)/shard_map/all_to_all | solution.py:292
  30.8 4.1 %collective-permute-start.1 = (bf16[4,80,128]{2,1,0:T(8,128)(2,1)S(1)}, bf16[4,80,128]{2,1,0:T(8,128)(2,1)S(1)}, u32[]{:S(2)}, u32[]{:S(2)}) collective-permute-start(bf16[4,80,128]{2,1,0:T(8,128)(2,1)S(1)} %get-tuple-element.24), channel_id=1, source_target_pairs={{0,1},{1,0},{2,3},{3,2},{4,5},{5,4},{6,7},{7,6},{8,9},{9,8},{10,11... | collective-permute-start | bytes 245768 | tf_op jit(solution)/shard_map/ppermute | solution.py:296
  41.4 20.8 %all-to-all-start.1 = ((bf16[16,64,128]{2,1,0:T(8,128)(2,1)}), bf16[16,64,128]{2,1,0:T(8,128)(2,1)S(1)}, u32[]{:S(2)}, u32[]{:S(2)}) async-start(bf16[16,64,128]{2,1,0:T(8,128)(2,1)} %shard_map.71), calls=%async_computation.1 | async-start | bytes 524288 | tf_op jit(solution)/shard_map/all_to_all | solution.py:292
  47.4 9.4 %collective-permute-start.4 = (bf16[2,80,128]{2,1,0:T(8,128)(2,1)S(1)}, bf16[2,80,128]{2,1,0:T(8,128)(2,1)S(1)}, u32[]{:S(2)}, u32[]{:S(2)}) collective-permute-start(bf16[2,80,128]{2,1,0:T(8,128)(2,1)S(1)} %pad_maximum_fusion.2), channel_id=1, source_target_pairs={{0,12},{4,0},{8,4},{12,8},{1,13},{5,1},{9,5},{13,9},{2,14},{6,2},{... | collective-permute-start | bytes 122888 | tf_op jit(solution)/shard_map/ppermute | solution.py:310
  51.8 6.5 %collective-permute-start.3 = (bf16[2,80,128]{2,1,0:T(8,128)(2,1)S(1)}, bf16[2,80,128]{2,1,0:T(8,128)(2,1)S(1)}, u32[]{:S(2)}, u32[]{:S(2)}) collective-permute-start(bf16[2,80,128]{2,1,0:T(8,128)(2,1)S(1)} %pad_maximum_fusion.1), channel_id=1, source_target_pairs={{0,8},{4,12},{8,0},{12,4},{1,9},{5,13},{9,1},{13,5},{2,10},{6,14},... | collective-permute-start | bytes 122888 | tf_op jit(solution)/shard_map/ppermute | solution.py:310
  54.3 6.3 %collective-permute-start.2 = (bf16[2,80,128]{2,1,0:T(8,128)(2,1)S(1)}, bf16[2,80,128]{2,1,0:T(8,128)(2,1)S(1)}, u32[]{:S(2)}, u32[]{:S(2)}) collective-permute-start(bf16[2,80,128]{2,1,0:T(8,128)(2,1)S(1)} %pad_maximum_fusion), channel_id=1, source_target_pairs={{0,4},{4,8},{8,12},{12,0},{1,5},{5,9},{9,13},{13,1},{2,6},{6,10},{... | collective-permute-start | bytes 122888 | tf_op jit(solution)/shard_map/ppermute | solution.py:310
  62.2 22.8 %all-to-all-start.2 = ((bf16[32,80,128]{2,1,0:T(8,128)(2,1)}), bf16[32,80,128]{2,1,0:T(8,128)(2,1)S(1)}, u32[]{:S(2)}, u32[]{:S(2)}) async-start(bf16[32,80,128]{2,1,0:T(8,128)(2,1)} %shard_map.70), calls=%async_computation.2 | async-start | bytes 1310720 | tf_op jit(solution)/shard_map/all_to_all | solution.py:292
  196.1 13.4 %all-to-all-start.9 = ((f32[32,5,128]{2,1,0:T(8,128)}), f32[32,5,128]{2,1,0:T(8,128)S(1)}, u32[]{:S(2)}, u32[]{:S(2)}) async-start(f32[32,5,128]{2,1,0:T(8,128)} %get-tuple-element.38), calls=%async_computation.9 | async-start | bytes 262144 | tf_op jit(solution)/shard_map/all_to_all | solution.py:292
  209.5 13.1 %collective-permute-start.5 = (f32[5,128]{1,0:T(8,128)S(1)}, f32[5,128]{1,0:T(8,128)S(1)}, u32[]{:S(2)}, u32[]{:S(2)}) collective-permute-start(f32[5,128]{1,0:T(8,128)S(1)} %fusion), channel_id=1, source_target_pairs={{0,2},{2,0},{1,3},{3,1},{4,6},{6,4},{5,7},{7,5},{8,10},{10,8},{9,1... | collective-permute-start | bytes 7688 | tf_op jit(solution)/shard_map/ppermute | solution.py:296
  212.7 10.7 %all-to-all-start.10 = ((f32[4,4,128]{2,1,0:T(4,128)}), f32[4,4,128]{2,1,0:T(4,128)S(1)}, u32[]{:S(2)}, u32[]{:S(2)}) async-start(f32[4,4,128]{2,1,0:T(4,128)} %get-tuple-element.39), calls=%async_computation.10 | async-start | bytes 16384 | tf_op jit(solution)/shard_map/all_to_all | solution.py:292

commit v6 on v5

--- a/solution.py
+++ b/solution.py
@@ -166,14 +166,14 @@
 def values_call(goods_emb, buyer_emb, money_row):
     return pl.pallas_call(
         values_kernel,
-        grid=(GT,),
+        grid=(NGOOD // 256,),
         in_specs=[
-            pl.BlockSpec((128, E), lambda i: (i, 0)),
+            pl.BlockSpec((256, E), lambda i: (i, 0)),
             pl.BlockSpec((NBUY, E), lambda i: (0, 0)),
             pl.BlockSpec((1, 128), lambda i: (0, 0)),
         ],
         out_specs=[
-            pl.BlockSpec((128, NBUY), lambda i: (i, 0)),
+            pl.BlockSpec((256, NBUY), lambda i: (i, 0)),
             pl.BlockSpec((32, LB + 1, 128), lambda i: (0, 0, 0)),
         ],
         out_shape=[

time: 225 us -> 224 us (level)
  no operation moved by 1% of the time
where the time goes in v6:
time: 224 us; the launch traced here: 223 us
  blocking collectives  93.5 us (42%)
  starting transfers between devices  64.5 us (29%)
  waiting for transfers between devices  36.2 us (16%)
  Pallas kernels  21.7 us (10%)
  local copies, waits for them, and re-layouts  6.15 us (3%)
    all_to_all x6, blocking collectives, exchange(): return lax.all_to_all(x, axes, 0, 0, tiled=True)  93.5 us
    all_to_all x5, starting transfers between devices, exchange(): return lax.all_to_all(x, axes, 0, 0, tiled=True)  32.6 us
    all_to_all x5, waiting for transfers between devices, exchange(): return lax.all_to_all(x, axes, 0, 0, tiled=True)  25.1 us
    ppermute x3, starting transfers between devices, swap(): return lax.ppermute(x, axis, [(0, 1), (1, 0)])  22.6 us
    ppermute x3, starting transfers between devices, embeddings(): two = lax.ppermute(two, 'x', [(i, (i + d) % 4) for i in range(4)])  9.33 us
    ppermute x3, waiting for transfers between devices, swap(): return lax.ppermute(x, axis, [(0, 1), (1, 0)])  7.47 us
    pallas_call x3, Pallas kernels, utility_call(): pl.pallas_call(functools.partial(utility_kernel, k), in_specs=specs, out_...  6.84 us
    pallas_call x1, Pallas kernels, values_call(): pl.pallas_call(values_kernel, grid=(NGOOD // 256,), in_specs=[pl.BlockSpe...  6.35 us
  transfers between devices with their start and end apart: 11, of which 7 were waited for; matrix products, arithmetic and copies ran while one was open for 2% of the time, Pallas kernels for 1%

profile of v6, /device:TPU:1, one launch (start us, length us, event | category | flops | bytes accessed | tf_op | source)
XLA Modules:
  0.0 223.3 jit_solution(13673072132560269103)
XLA Ops:
  0.6 0.1 pad_add_fusion.place_ref
  0.7 0.0 copy-start
  0.7 0.9 copy-done
  1.6 0.0 copy-start.1
  1.6 0.9 copy-done.1
  2.5 2.1 shard_map.68
  4.6 16.2 %collective-permute-start = (bf16[4,80,128]{2,1,0:T(8,128)(2,1)S(1)}, bf16[4,80,128]{2,1,0:T(8,128)(2,1)S(1)}, u32[]{:S(2)}, u32[]{:S(2)}) collective-permute-start(bf16[4,80,128]{2,1,0:T(8,128)(2,1)S(1)} %get-tuple-element.22), channel_id=1, source_target_pairs={{0,2},{2,0},{1,3},{3,1},{4,6},{6,4},{5,7},{7,5},{8,10},{10,8},{9,1... | collective-permute-start | bytes 245768 | tf_op jit(solution)/shard_map/ppermute | solution.py:296
  20.9 7.8 %all-to-all-start = ((bf16[32,16,128]{2,1,0:T(8,128)(2,1)}), bf16[32,16,128]{2,1,0:T(8,128)(2,1)S(1)}, u32[]{:S(2)}, u32[]{:S(2)}) async-start(bf16[32,16,128]{2,1,0:T(8,128)(2,1)} %get-tuple-element.25), calls=%async_computation | async-start | bytes 262144 | tf_op jit(solution)/shard_map/all_to_all | solution.py:292
  28.7 1.0 copy.10
  29.6 0.1 reverse_select_fusion
  29.7 1.0 copy.13
  30.7 0.0 collective-permute-done.came_ref
  30.7 0.1 shard_map.69
  30.8 3.1 %collective-permute-start.1 = (bf16[4,80,128]{2,1,0:T(8,128)(2,1)S(1)}, bf16[4,80,128]{2,1,0:T(8,128)(2,1)S(1)}, u32[]{:S(2)}, u32[]{:S(2)}) collective-permute-start(bf16[4,80,128]{2,1,0:T(8,128)(2,1)S(1)} %get-tuple-element.24), channel_id=1, source_target_pairs={{0,1},{1,0},{2,3},{3,2},{4,5},{5,4},{6,7},{7,6},{8,9},{9,8},{10,11... | collective-permute-start | bytes 245768 | tf_op jit(solution)/shard_map/ppermute | solution.py:296
  34.0 0.9 collective-permute-done.1
  34.9 5.6 %all-to-all-done.got_ref = bf16[32,16,128]{2,1,0:T(8,128)(2,1)S(1)} async-done(((bf16[32,16,128]{2,1,0:T(8,128)(2,1)}), bf16[32,16,128]{2,1,0:T(8,128)(2,1)S(1)}, u32[]{:S(2)}, u32[]{:S(2)}) %all-to-all-start) | async-done | bytes 131104 | tf_op jit(solution)/shard_map/all_to_all | solution.py:292
  40.4 1.0 shard_map.71
  41.4 6.0 %all-to-all-start.1 = ((bf16[16,64,128]{2,1,0:T(8,128)(2,1)}), bf16[16,64,128]{2,1,0:T(8,128)(2,1)S(1)}, u32[]{:S(2)}, u32[]{:S(2)}) async-start(bf16[16,64,128]{2,1,0:T(8,128)(2,1)} %shard_map.71), calls=%async_computation.1 | async-start | bytes 524288 | tf_op jit(solution)/shard_map/all_to_all | solution.py:292
  47.4 4.4 %collective-permute-start.4 = (bf16[2,80,128]{2,1,0:T(8,128)(2,1)S(1)}, bf16[2,80,128]{2,1,0:T(8,128)(2,1)S(1)}, u32[]{:S(2)}, u32[]{:S(2)}) collective-permute-start(bf16[2,80,128]{2,1,0:T(8,128)(2,1)S(1)} %pad_maximum_fusion.2), channel_id=1, source_target_pairs={{0,12},{4,0},{8,4},{12,8},{1,13},{5,1},{9,5},{13,9},{2,14},{6,2},{... | collective-permute-start | bytes 122888 | tf_op jit(solution)/shard_map/ppermute | solution.py:310
  51.8 2.4 %collective-permute-start.3 = (bf16[2,80,128]{2,1,0:T(8,128)(2,1)S(1)}, bf16[2,80,128]{2,1,0:T(8,128)(2,1)S(1)}, u32[]{:S(2)}, u32[]{:S(2)}) collective-permute-start(bf16[2,80,128]{2,1,0:T(8,128)(2,1)S(1)} %pad_maximum_fusion.1), channel_id=1, source_target_pairs={{0,8},{4,12},{8,0},{12,4},{1,9},{5,13},{9,1},{13,5},{2,10},{6,14},... | collective-permute-start | bytes 122888 | tf_op jit(solution)/shard_map/ppermute | solution.py:310
  54.3 2.5 %collective-permute-start.2 = (bf16[2,80,128]{2,1,0:T(8,128)(2,1)S(1)}, bf16[2,80,128]{2,1,0:T(8,128)(2,1)S(1)}, u32[]{:S(2)}, u32[]{:S(2)}) collective-permute-start(bf16[2,80,128]{2,1,0:T(8,128)(2,1)S(1)} %pad_maximum_fusion), channel_id=1, source_target_pairs={{0,4},{4,8},{8,12},{12,0},{1,5},{5,9},{9,13},{13,1},{2,6},{6,10},{... | collective-permute-start | bytes 122888 | tf_op jit(solution)/shard_map/ppermute | solution.py:310
  56.8 0.0 collective-permute-done.4
  56.8 1.5 collective-permute-done.3
  58.4 2.2 collective-permute-done.2
  60.5 1.7 shard_map.70
  62.2 0.0 all-to-all-done.1
  62.2 9.9 %all-to-all-start.2 = ((bf16[32,80,128]{2,1,0:T(8,128)(2,1)}), bf16[32,80,128]{2,1,0:T(8,128)(2,1)S(1)}, u32[]{:S(2)}, u32[]{:S(2)}) async-start(bf16[32,80,128]{2,1,0:T(8,128)(2,1)} %shard_map.70), calls=%async_computation.2 | async-start | bytes 1310720 | tf_op jit(solution)/shard_map/all_to_all | solution.py:292
  72.1 0.8 reshape.41
  72.9 0.1 reshape.42
  73.0 11.9 %all-to-all-done.2 = bf16[32,80,128]{2,1,0:T(8,128)(2,1)S(1)} async-done(((bf16[32,80,128]{2,1,0:T(8,128)(2,1)}), bf16[32,80,128]{2,1,0:T(8,128)(2,1)S(1)}, u32[]{:S(2)}, u32[]{:S(2)}) %all-to-all-start.2) | async-done | bytes 655392 | tf_op jit(solution)/shard_map/all_to_all | solution.py:292
  85.0 6.4 %shard_map.72 = (bf16[1024,2560]{1,0:T(8,128)(2,1)S(1)}, f32[32,21,128]{2,1,0:T(8,128)S(1)}) custom-call(bf16[1024,128]{1,0:T(8,128)(2,1)S(1)} %bitcast.43, bf16[2560,128]{1,0:T(8,128)(2,1)S(1)} %bitcast.42, f32[1,128]{1,0:T(1,128)S(1)} %constant_dynamic-slice_fusion.money_ref), custom_call_target="tpu_custom_call" | custom-call | tf_op jit(solution)/shard_map/pallas_call | solution.py:167
  91.3 13.8 %all_to_all.55.got_ref = f32[32,21,128]{2,1,0:T(8,128)S(1)} all-to-all(f32[32,21,128]{2,1,0:T(8,128)S(1)} %get-tuple-element.28), channel_id=1, replica_groups=mesh['y'=4,'zl'=8,'x'=4,'zh'=2,'c'=2] {'y','x','c'}, dimensions={0} | all-to-all | bytes 688128 | tf_op jit(solution)/shard_map/all_to_all | solution.py:292
  105.1 1.5 shard_map.73
  106.6 21.7 %all_to_all.56.got_ref = f32[16,8,128]{2,1,0:T(8,128)S(1)} all-to-all(f32[16,8,128]{2,1,0:T(8,128)S(1)} %get-tuple-element.30), channel_id=1, replica_groups=mesh['y'=4,'zl'=8,'x'=4,'zh'=2,'c'=2] {'zh','zl'}, dimensions={0} | all-to-all | bytes 131072 | tf_op jit(solution)/shard_map/all_to_all | solution.py:292
  128.3 2.6 %shard_map.74 = (f32[32,4,640]{2,1,0:T(4,128)S(1)}, f32[8,128]{1,0:T(8,128)}, f32[1024,2560]{1,0:T(8,128)S(1)}) custom-call(f32[16,8,128]{2,1,0:T(8,128)S(1)} %all_to_all.56.got_ref, bf16[1024,2560]{1,0:T(8,128)(2,1)S(1)} %get-tuple-element.29.refs_0_), custom_call_target="tpu_custom_call" | custom-call | tf_op jit(solution)/shard_map/pallas_call | solution.py:207
  130.8 14.8 %all_to_all.57.got_ref = f32[32,4,640]{2,1,0:T(4,128)S(1)} all-to-all(f32[32,4,640]{2,1,0:T(4,128)S(1)} %get-tuple-element.31), channel_id=1, replica_groups=mesh['y'=4,'zl'=8,'x'=4,'zh'=2,'c'=2] {'y','x','c'}, dimensions={0} | all-to-all | bytes 655360 | tf_op jit(solution)/shard_map/all_to_all | solution.py:292
  145.6 1.1 shard_map.75
  146.7 14.3 %all_to_all.58.got_ref = f32[16,8,128]{2,1,0:T(8,128)S(1)} all-to-all(f32[16,8,128]{2,1,0:T(8,128)S(1)} %shard_map.75), channel_id=1, replica_groups=mesh['y'=4,'zl'=8,'x'=4,'zh'=2,'c'=2] {'zh','zl'}, dimensions={0} | all-to-all | bytes 131072 | tf_op jit(solution)/shard_map/all_to_all | solution.py:292
  161.0 2.1 shard_map.76
  163.1 14.7 %all_to_all.59.got_ref = f32[32,4,640]{2,1,0:T(4,128)S(1)} all-to-all(f32[32,4,640]{2,1,0:T(4,128)S(1)} %get-tuple-element.34), channel_id=1, replica_groups=mesh['y'=4,'zl'=8,'x'=4,'zh'=2,'c'=2] {'y','x','c'}, dimensions={0} | all-to-all | bytes 655360 | tf_op jit(solution)/shard_map/all_to_all | solution.py:292
  177.8 1.1 shard_map.77
  178.9 14.3 %all_to_all.60.got_ref = f32[16,8,128]{2,1,0:T(8,128)S(1)} all-to-all(f32[16,8,128]{2,1,0:T(8,128)S(1)} %shard_map.77), channel_id=1, replica_groups=mesh['y'=4,'zl'=8,'x'=4,'zh'=2,'c'=2] {'zh','zl'}, dimensions={0} | all-to-all | bytes 131072 | tf_op jit(solution)/shard_map/all_to_all | solution.py:292
  193.2 2.2 shard_map.78
  195.4 5.6 %all-to-all-start.9 = ((f32[32,5,128]{2,1,0:T(8,128)}), f32[32,5,128]{2,1,0:T(8,128)S(1)}, u32[]{:S(2)}, u32[]{:S(2)}) async-start(f32[32,5,128]{2,1,0:T(8,128)} %get-tuple-element.38), calls=%async_computation.9 | async-start | bytes 262144 | tf_op jit(solution)/shard_map/all_to_all | solution.py:292
  201.1 0.1 dynamic-slice_reduce_fusion
  201.2 7.6 %all-to-all-done.9 = f32[32,5,128]{2,1,0:T(8,128)S(1)} async-done(((f32[32,5,128]{2,1,0:T(8,128)}), f32[32,5,128]{2,1,0:T(8,128)S(1)}, u32[]{:S(2)}, u32[]{:S(2)}) %all-to-all-start.9) | async-done | bytes 81952 | tf_op jit(solution)/shard_map/all_to_all | solution.py:292
  208.8 3.2 %collective-permute-start.5 = (f32[5,128]{1,0:T(8,128)S(1)}, f32[5,128]{1,0:T(8,128)S(1)}, u32[]{:S(2)}, u32[]{:S(2)}) collective-permute-start(f32[5,128]{1,0:T(8,128)S(1)} %fusion), channel_id=1, source_target_pairs={{0,2},{2,0},{1,3},{3,1},{4,6},{6,4},{5,7},{7,5},{8,10},{10,8},{9,1... | collective-permute-start | bytes 7688 | tf_op jit(solution)/shard_map/ppermute | solution.py:296
  212.0 3.3 %all-to-all-start.10 = ((f32[4,4,128]{2,1,0:T(4,128)}), f32[4,4,128]{2,1,0:T(4,128)S(1)}, u32[]{:S(2)}, u32[]{:S(2)}) async-start(f32[4,4,128]{2,1,0:T(4,128)} %get-tuple-element.39), calls=%async_computation.10 | async-start | bytes 16384 | tf_op jit(solution)/shard_map/all_to_all | solution.py:292
  215.3 6.6 %collective-permute-done.5 = f32[5,128]{1,0:T(8,128)S(1)} collective-permute-done((f32[5,128]{1,0:T(8,128)S(1)}, f32[5,128]{1,0:T(8,128)S(1)}, u32[]{:S(2)}, u32[]{:S(2)}) %collective-permute-start.5) | collective-permute-done | bytes 2592 | tf_op jit(solution)/shard_map/ppermute | solution.py:296
  221.9 0.1 stack_reshape.6
  221.9 0.1 stack_reshape.7
  222.1 0.7 reshape.44
  222.7 0.0 all-to-all-done.10
  222.7 0.6 copy.15
  (15 shorter events, 0.2 us)
Async XLA Ops:
  0.7 0.9 copy-start
  1.6 0.9 copy-start.1
  4.6 26.1 %collective-permute-start = (bf16[4,80,128]{2,1,0:T(8,128)(2,1)S(1)}, bf16[4,80,128]{2,1,0:T(8,128)(2,1)S(1)}, u32[]{:S(2)}, u32[]{:S(2)}) collective-permute-start(bf16[4,80,128]{2,1,0:T(8,128)(2,1)S(1)} %get-tuple-element.22), channel_id=1, source_target_pairs={{0,2},{2,0},{1,3},{3,1},{4,6},{6,4},{5,7},{7,5},{8,10},{10,8},{9,1... | collective-permute-start | bytes 245768 | tf_op jit(solution)/shard_map/ppermute | solution.py:296
  20.9 19.6 %all-to-all-start = ((bf16[32,16,128]{2,1,0:T(8,128)(2,1)}), bf16[32,16,128]{2,1,0:T(8,128)(2,1)S(1)}, u32[]{:S(2)}, u32[]{:S(2)}) async-start(bf16[32,16,128]{2,1,0:T(8,128)(2,1)} %get-tuple-element.25), calls=%async_computation | async-start | bytes 262144 | tf_op jit(solution)/shard_map/all_to_all | solution.py:292
  30.8 4.1 %collective-permute-start.1 = (bf16[4,80,128]{2,1,0:T(8,128)(2,1)S(1)}, bf16[4,80,128]{2,1,0:T(8,128)(2,1)S(1)}, u32[]{:S(2)}, u32[]{:S(2)}) collective-permute-start(bf16[4,80,128]{2,1,0:T(8,128)(2,1)S(1)} %get-tuple-element.24), channel_id=1, source_target_pairs={{0,1},{1,0},{2,3},{3,2},{4,5},{5,4},{6,7},{7,6},{8,9},{9,8},{10,11... | collective-permute-start | bytes 245768 | tf_op jit(solution)/shard_map/ppermute | solution.py:296
  41.4 20.8 %all-to-all-start.1 = ((bf16[16,64,128]{2,1,0:T(8,128)(2,1)}), bf16[16,64,128]{2,1,0:T(8,128)(2,1)S(1)}, u32[]{:S(2)}, u32[]{:S(2)}) async-start(bf16[16,64,128]{2,1,0:T(8,128)(2,1)} %shard_map.71), calls=%async_computation.1 | async-start | bytes 524288 | tf_op jit(solution)/shard_map/all_to_all | solution.py:292
  47.4 9.4 %collective-permute-start.4 = (bf16[2,80,128]{2,1,0:T(8,128)(2,1)S(1)}, bf16[2,80,128]{2,1,0:T(8,128)(2,1)S(1)}, u32[]{:S(2)}, u32[]{:S(2)}) collective-permute-start(bf16[2,80,128]{2,1,0:T(8,128)(2,1)S(1)} %pad_maximum_fusion.2), channel_id=1, source_target_pairs={{0,12},{4,0},{8,4},{12,8},{1,13},{5,1},{9,5},{13,9},{2,14},{6,2},{... | collective-permute-start | bytes 122888 | tf_op jit(solution)/shard_map/ppermute | solution.py:310
  51.8 6.5 %collective-permute-start.3 = (bf16[2,80,128]{2,1,0:T(8,128)(2,1)S(1)}, bf16[2,80,128]{2,1,0:T(8,128)(2,1)S(1)}, u32[]{:S(2)}, u32[]{:S(2)}) collective-permute-start(bf16[2,80,128]{2,1,0:T(8,128)(2,1)S(1)} %pad_maximum_fusion.1), channel_id=1, source_target_pairs={{0,8},{4,12},{8,0},{12,4},{1,9},{5,13},{9,1},{13,5},{2,10},{6,14},... | collective-permute-start | bytes 122888 | tf_op jit(solution)/shard_map/ppermute | solution.py:310
  54.3 6.3 %collective-permute-start.2 = (bf16[2,80,128]{2,1,0:T(8,128)(2,1)S(1)}, bf16[2,80,128]{2,1,0:T(8,128)(2,1)S(1)}, u32[]{:S(2)}, u32[]{:S(2)}) collective-permute-start(bf16[2,80,128]{2,1,0:T(8,128)(2,1)S(1)} %pad_maximum_fusion), channel_id=1, source_target_pairs={{0,4},{4,8},{8,12},{12,0},{1,5},{5,9},{9,13},{13,1},{2,6},{6,10},{... | collective-permute-start | bytes 122888 | tf_op jit(solution)/shard_map/ppermute | solution.py:310
  62.2 22.8 %all-to-all-start.2 = ((bf16[32,80,128]{2,1,0:T(8,128)(2,1)}), bf16[32,80,128]{2,1,0:T(8,128)(2,1)S(1)}, u32[]{:S(2)}, u32[]{:S(2)}) async-start(bf16[32,80,128]{2,1,0:T(8,128)(2,1)} %shard_map.70), calls=%async_computation.2 | async-start | bytes 1310720 | tf_op jit(solution)/shard_map/all_to_all | solution.py:292
  195.4 13.4 %all-to-all-start.9 = ((f32[32,5,128]{2,1,0:T(8,128)}), f32[32,5,128]{2,1,0:T(8,128)S(1)}, u32[]{:S(2)}, u32[]{:S(2)}) async-start(f32[32,5,128]{2,1,0:T(8,128)} %get-tuple-element.38), calls=%async_computation.9 | async-start | bytes 262144 | tf_op jit(solution)/shard_map/all_to_all | solution.py:292
  208.8 13.1 %collective-permute-start.5 = (f32[5,128]{1,0:T(8,128)S(1)}, f32[5,128]{1,0:T(8,128)S(1)}, u32[]{:S(2)}, u32[]{:S(2)}) collective-permute-start(f32[5,128]{1,0:T(8,128)S(1)} %fusion), channel_id=1, source_target_pairs={{0,2},{2,0},{1,3},{3,1},{4,6},{6,4},{5,7},{7,5},{8,10},{10,8},{9,1... | collective-permute-start | bytes 7688 | tf_op jit(solution)/shard_map/ppermute | solution.py:296
  212.0 10.7 %all-to-all-start.10 = ((f32[4,4,128]{2,1,0:T(4,128)}), f32[4,4,128]{2,1,0:T(4,128)S(1)}, u32[]{:S(2)}, u32[]{:S(2)}) async-start(f32[4,4,128]{2,1,0:T(4,128)} %get-tuple-element.39), calls=%async_computation.10 | async-start | bytes 16384 | tf_op jit(solution)/shard_map/all_to_all | solution.py:292

commit v7 on v6

--- a/solution.py
+++ b/solution.py
@@ -217,7 +217,9 @@
     )(got, *blocks)
 
 
-def pack_kernel(place_ref, hidden_ref, goods_ref, keep_ref, go_ref, tiles_ref):
+def pack_kernel(place_ref, hidden_ref, goods_hbm, keep_ref, go_ref, tiles_ref, goods_ref, sem):
+    copy = pltpu.make_async_copy(goods_hbm, goods_ref, sem)
+    copy.start()
     x, zh, c = place_ref[0], place_ref[1], place_ref[2]
     rows = hidden_ref[...].astype(jnp.float32).T
 
@@ -240,6 +242,7 @@
             def _(at=at, part=part):
                 go_ref[at] = part
 
+    copy.wait()
     for t in range(16):
         top = goods_ref[0:16, 128 * t : 128 * t + 128].astype(jnp.float32)
         low = goods_ref[16:32, 128 * t : 128 * t + 128].astype(jnp.float32)
@@ -277,14 +280,16 @@
         out_ref[p] = emb
 
 
-def small_call(kernel, outs, *args, scratch=(), smem=0):
+def small_call(kernel, outs, *args, scratch=(), smem=0, hbm=0, params=PARAMS):
     return pl.pallas_call(
         kernel,
-        in_specs=[pl.BlockSpec(memory_space=pltpu.SMEM)] * smem + [VM] * (len(args) - smem),
+        in_specs=[pl.BlockSpec(memory_space=pltpu.SMEM)] * smem
+        + [VM] * (len(args) - smem - hbm)
+        + [pl.BlockSpec(memory_space=pl.ANY)] * hbm,
         out_specs=jax.tree.map(lambda _: VM, outs),
         out_shape=outs,
         scratch_shapes=list(scratch),
-        compiler_params=PARAMS,
+        compiler_params=params,
     )(*args)
 
 
@@ -300,7 +305,11 @@
     bf16 = jnp.bfloat16
     shape = jax.ShapeDtypeStruct
     outs = (shape((4, 80, 128), bf16), shape((4, 80, 128), bf16), shape((32, 16, 128), bf16))
-    keep, go, tiles = small_call(pack_kernel, outs, place, buyer_hidden.T, goods_hidden.T, smem=1)
+    keep, go, tiles = small_call(
+        pack_kernel, outs, place, buyer_hidden.T, goods_hidden.T,
+        scratch=(pltpu.VMEM((32, 2048), bf16), pltpu.SemaphoreType.DMA), smem=1, hbm=1,
+        params=pltpu.CompilerParams(vmem_limit_bytes=61 << 20),
+    )
     came = swap(go, "zh")
     here, across = small_call(pair_kernel, (shape((4, 80, 128), bf16),) * 2, keep, came)
     across = swap(across, "c")

time: 224 us -> 224 us (level)
  no operation moved by 1% of the time
where the time goes in v7:
time: 224 us; the launch traced here: 223 us
  blocking collectives  93.3 us (42%)
  starting transfers between devices  64.8 us (29%)
  waiting for transfers between devices  35.4 us (16%)
  Pallas kernels  22.1 us (10%)
  local copies, waits for them, and re-layouts  5.87 us (3%)
    all_to_all x6, blocking collectives, exchange(): return lax.all_to_all(x, axes, 0, 0, tiled=True)  93.3 us
    all_to_all x5, starting transfers between devices, exchange(): return lax.all_to_all(x, axes, 0, 0, tiled=True)  32.9 us
    all_to_all x5, waiting for transfers between devices, exchange(): return lax.all_to_all(x, axes, 0, 0, tiled=True)  24.2 us
    ppermute x3, starting transfers between devices, swap(): return lax.ppermute(x, axis, [(0, 1), (1, 0)])  22.6 us
    ppermute x3, starting transfers between devices, embeddings(): two = lax.ppermute(two, 'x', [(i, (i + d) % 4) for i in range(4)])  9.33 us
    ppermute x3, waiting for transfers between devices, swap(): return lax.ppermute(x, axis, [(0, 1), (1, 0)])  7.47 us
    pallas_call x3, Pallas kernels, utility_call(): pl.pallas_call(functools.partial(utility_kernel, k), in_specs=specs, out_...  6.8 us
    pallas_call x1, Pallas kernels, values_call(): pl.pallas_call(values_kernel, grid=(NGOOD // 256,), in_specs=[pl.BlockSpe...  6.35 us
  transfers between devices with their start and end apart: 11, of which 7 were waited for; matrix products, arithmetic and copies ran while one was open for 2% of the time, Pallas kernels for 1%

profile of v7, /device:TPU:1, one launch (start us, length us, event | category | flops | bytes accessed | tf_op | source)
XLA Modules:
  0.0 223.3 jit_solution(17896950452407026705)
XLA Ops:
  0.6 0.7 pad_add_fusion.place_ref
  1.3 2.6 %shard_map.68 = (bf16[4,80,128]{2,1,0:T(8,128)(2,1)}, bf16[4,80,128]{2,1,0:T(8,128)(2,1)}, bf16[32,16,128]{2,1,0:T(8,128)(2,1)}) custom-call(s32[3]{0:T(128)} %pad_add_fusion.place_ref, bf16[64,1280]{1,0:T(8,128)(2,1)} %bitcast.48, bf16[32,2048]{1,0:T(8,128)(2,1)} %bitcast.49), custom_call_target="tpu_custom_call" | custom-call | tf_op jit(solution)/shard_map/pallas_call | solution.py:284
  3.9 16.3 %collective-permute-start = (bf16[4,80,128]{2,1,0:T(8,128)(2,1)}, bf16[4,80,128]{2,1,0:T(8,128)(2,1)S(1)}, u32[]{:S(2)}, u32[]{:S(2)}) collective-permute-start(bf16[4,80,128]{2,1,0:T(8,128)(2,1)} %get-tuple-element.22), channel_id=1, source_target_pairs={{0,2},{2,0},{1,3},{3,1},{4,6},{6,4},{5,7},{7,5},{8,10},{10,8},{9,1... | collective-permute-start | bytes 245768 | tf_op jit(solution)/shard_map/ppermute | solution.py:301
  20.2 7.8 %all-to-all-start = ((bf16[32,16,128]{2,1,0:T(8,128)(2,1)}), bf16[32,16,128]{2,1,0:T(8,128)(2,1)S(1)}, u32[]{:S(2)}, u32[]{:S(2)}) async-start(bf16[32,16,128]{2,1,0:T(8,128)(2,1)} %get-tuple-element.25), calls=%async_computation | async-start | bytes 262144 | tf_op jit(solution)/shard_map/all_to_all | solution.py:297
  27.9 1.0 copy.10
  28.9 0.1 reverse_select_fusion
  29.0 1.0 copy.13
  30.0 0.0 collective-permute-done.came_ref
  30.0 0.0 copy-start
  30.0 0.9 copy-done
  30.9 0.1 shard_map.69
  31.0 3.1 %collective-permute-start.1 = (bf16[4,80,128]{2,1,0:T(8,128)(2,1)S(1)}, bf16[4,80,128]{2,1,0:T(8,128)(2,1)S(1)}, u32[]{:S(2)}, u32[]{:S(2)}) collective-permute-start(bf16[4,80,128]{2,1,0:T(8,128)(2,1)S(1)} %get-tuple-element.24), channel_id=1, source_target_pairs={{0,1},{1,0},{2,3},{3,2},{4,5},{5,4},{6,7},{7,6},{8,9},{9,8},{10,11... | collective-permute-start | bytes 245768 | tf_op jit(solution)/shard_map/ppermute | solution.py:301
  34.1 0.9 collective-permute-done.1
  35.0 4.7 %all-to-all-done.got_ref = bf16[32,16,128]{2,1,0:T(8,128)(2,1)S(1)} async-done(((bf16[32,16,128]{2,1,0:T(8,128)(2,1)}), bf16[32,16,128]{2,1,0:T(8,128)(2,1)S(1)}, u32[]{:S(2)}, u32[]{:S(2)}) %all-to-all-start) | async-done | bytes 131104 | tf_op jit(solution)/shard_map/all_to_all | solution.py:297
  39.7 1.0 shard_map.71
  40.7 6.0 %all-to-all-start.1 = ((bf16[16,64,128]{2,1,0:T(8,128)(2,1)}), bf16[16,64,128]{2,1,0:T(8,128)(2,1)S(1)}, u32[]{:S(2)}, u32[]{:S(2)}) async-start(bf16[16,64,128]{2,1,0:T(8,128)(2,1)} %shard_map.71), calls=%async_computation.1 | async-start | bytes 524288 | tf_op jit(solution)/shard_map/all_to_all | solution.py:297
  46.7 4.4 %collective-permute-start.4 = (bf16[2,80,128]{2,1,0:T(8,128)(2,1)S(1)}, bf16[2,80,128]{2,1,0:T(8,128)(2,1)S(1)}, u32[]{:S(2)}, u32[]{:S(2)}) collective-permute-start(bf16[2,80,128]{2,1,0:T(8,128)(2,1)S(1)} %pad_maximum_fusion.2), channel_id=1, source_target_pairs={{0,12},{4,0},{8,4},{12,8},{1,13},{5,1},{9,5},{13,9},{2,14},{6,2},{... | collective-permute-start | bytes 122888 | tf_op jit(solution)/shard_map/ppermute | solution.py:319
  51.1 2.4 %collective-permute-start.3 = (bf16[2,80,128]{2,1,0:T(8,128)(2,1)S(1)}, bf16[2,80,128]{2,1,0:T(8,128)(2,1)S(1)}, u32[]{:S(2)}, u32[]{:S(2)}) collective-permute-start(bf16[2,80,128]{2,1,0:T(8,128)(2,1)S(1)} %pad_maximum_fusion.1), channel_id=1, source_target_pairs={{0,8},{4,12},{8,0},{12,4},{1,9},{5,13},{9,1},{13,5},{2,10},{6,14},... | collective-permute-start | bytes 122888 | tf_op jit(solution)/shard_map/ppermute | solution.py:319
  53.6 2.5 %collective-permute-start.2 = (bf16[2,80,128]{2,1,0:T(8,128)(2,1)S(1)}, bf16[2,80,128]{2,1,0:T(8,128)(2,1)S(1)}, u32[]{:S(2)}, u32[]{:S(2)}) collective-permute-start(bf16[2,80,128]{2,1,0:T(8,128)(2,1)S(1)} %pad_maximum_fusion), channel_id=1, source_target_pairs={{0,4},{4,8},{8,12},{12,0},{1,5},{5,9},{9,13},{13,1},{2,6},{6,10},{... | collective-permute-start | bytes 122888 | tf_op jit(solution)/shard_map/ppermute | solution.py:319
  56.1 0.0 collective-permute-done.4
  56.1 1.5 collective-permute-done.3
  57.7 2.2 collective-permute-done.2
  59.8 0.0 copy-start.1
  59.8 0.7 copy-done.1
  60.5 1.7 shard_map.70
  62.2 0.0 all-to-all-done.1
  62.2 10.2 %all-to-all-start.2 = ((bf16[32,80,128]{2,1,0:T(8,128)(2,1)}), bf16[32,80,128]{2,1,0:T(8,128)(2,1)S(1)}, u32[]{:S(2)}, u32[]{:S(2)}) async-start(bf16[32,80,128]{2,1,0:T(8,128)(2,1)} %shard_map.70), calls=%async_computation.2 | async-start | bytes 1310720 | tf_op jit(solution)/shard_map/all_to_all | solution.py:297
  72.4 0.8 reshape.41
  73.2 0.1 reshape.42
  73.3 11.9 %all-to-all-done.2 = bf16[32,80,128]{2,1,0:T(8,128)(2,1)S(1)} async-done(((bf16[32,80,128]{2,1,0:T(8,128)(2,1)}), bf16[32,80,128]{2,1,0:T(8,128)(2,1)S(1)}, u32[]{:S(2)}, u32[]{:S(2)}) %all-to-all-start.2) | async-done | bytes 655392 | tf_op jit(solution)/shard_map/all_to_all | solution.py:297
  85.2 6.4 %shard_map.72 = (bf16[1024,2560]{1,0:T(8,128)(2,1)S(1)}, f32[32,21,128]{2,1,0:T(8,128)S(1)}) custom-call(bf16[1024,128]{1,0:T(8,128)(2,1)S(1)} %bitcast.43, bf16[2560,128]{1,0:T(8,128)(2,1)S(1)} %bitcast.42, f32[1,128]{1,0:T(1,128)S(1)} %constant_dynamic-slice_fusion.money_ref), custom_call_target="tpu_custom_call" | custom-call | tf_op jit(solution)/shard_map/pallas_call | solution.py:167
  91.5 13.8 %all_to_all.55.got_ref = f32[32,21,128]{2,1,0:T(8,128)S(1)} all-to-all(f32[32,21,128]{2,1,0:T(8,128)S(1)} %get-tuple-element.28), channel_id=1, replica_groups=mesh['y'=4,'zl'=8,'x'=4,'zh'=2,'c'=2] {'y','x','c'}, dimensions={0} | all-to-all | bytes 688128 | tf_op jit(solution)/shard_map/all_to_all | solution.py:297
  105.3 1.5 shard_map.73
  106.8 21.4 %all_to_all.56.got_ref = f32[16,8,128]{2,1,0:T(8,128)S(1)} all-to-all(f32[16,8,128]{2,1,0:T(8,128)S(1)} %get-tuple-element.30), channel_id=1, replica_groups=mesh['y'=4,'zl'=8,'x'=4,'zh'=2,'c'=2] {'zh','zl'}, dimensions={0} | all-to-all | bytes 131072 | tf_op jit(solution)/shard_map/all_to_all | solution.py:297
  128.2 2.5 %shard_map.74 = (f32[32,4,640]{2,1,0:T(4,128)S(1)}, f32[8,128]{1,0:T(8,128)}, f32[1024,2560]{1,0:T(8,128)S(1)}) custom-call(f32[16,8,128]{2,1,0:T(8,128)S(1)} %all_to_all.56.got_ref, bf16[1024,2560]{1,0:T(8,128)(2,1)S(1)} %get-tuple-element.29.refs_0_), custom_call_target="tpu_custom_call" | custom-call | tf_op jit(solution)/shard_map/pallas_call | solution.py:207
  130.8 14.8 %all_to_all.57.got_ref = f32[32,4,640]{2,1,0:T(4,128)S(1)} all-to-all(f32[32,4,640]{2,1,0:T(4,128)S(1)} %get-tuple-element.31), channel_id=1, replica_groups=mesh['y'=4,'zl'=8,'x'=4,'zh'=2,'c'=2] {'y','x','c'}, dimensions={0} | all-to-all | bytes 655360 | tf_op jit(solution)/shard_map/all_to_all | solution.py:297
  145.6 1.1 shard_map.75
  146.6 14.3 %all_to_all.58.got_ref = f32[16,8,128]{2,1,0:T(8,128)S(1)} all-to-all(f32[16,8,128]{2,1,0:T(8,128)S(1)} %shard_map.75), channel_id=1, replica_groups=mesh['y'=4,'zl'=8,'x'=4,'zh'=2,'c'=2] {'zh','zl'}, dimensions={0} | all-to-all | bytes 131072 | tf_op jit(solution)/shard_map/all_to_all | solution.py:297
  160.9 2.1 shard_map.76
  163.0 14.7 %all_to_all.59.got_ref = f32[32,4,640]{2,1,0:T(4,128)S(1)} all-to-all(f32[32,4,640]{2,1,0:T(4,128)S(1)} %get-tuple-element.34), channel_id=1, replica_groups=mesh['y'=4,'zl'=8,'x'=4,'zh'=2,'c'=2] {'y','x','c'}, dimensions={0} | all-to-all | bytes 655360 | tf_op jit(solution)/shard_map/all_to_all | solution.py:297
  177.7 1.1 shard_map.77
  178.8 14.3 %all_to_all.60.got_ref = f32[16,8,128]{2,1,0:T(8,128)S(1)} all-to-all(f32[16,8,128]{2,1,0:T(8,128)S(1)} %shard_map.77), channel_id=1, replica_groups=mesh['y'=4,'zl'=8,'x'=4,'zh'=2,'c'=2] {'zh','zl'}, dimensions={0} | all-to-all | bytes 131072 | tf_op jit(solution)/shard_map/all_to_all | solution.py:297
  193.1 2.2 shard_map.78
  195.3 5.6 %all-to-all-start.9 = ((f32[32,5,128]{2,1,0:T(8,128)}), f32[32,5,128]{2,1,0:T(8,128)S(1)}, u32[]{:S(2)}, u32[]{:S(2)}) async-start(f32[32,5,128]{2,1,0:T(8,128)} %get-tuple-element.38), calls=%async_computation.9 | async-start | bytes 262144 | tf_op jit(solution)/shard_map/all_to_all | solution.py:297
  201.0 0.1 dynamic-slice_reduce_fusion
  201.1 7.6 %all-to-all-done.9 = f32[32,5,128]{2,1,0:T(8,128)S(1)} async-done(((f32[32,5,128]{2,1,0:T(8,128)}), f32[32,5,128]{2,1,0:T(8,128)S(1)}, u32[]{:S(2)}, u32[]{:S(2)}) %all-to-all-start.9) | async-done | bytes 81952 | tf_op jit(solution)/shard_map/all_to_all | solution.py:297
  208.7 3.2 %collective-permute-start.5 = (f32[5,128]{1,0:T(8,128)S(1)}, f32[5,128]{1,0:T(8,128)S(1)}, u32[]{:S(2)}, u32[]{:S(2)}) collective-permute-start(f32[5,128]{1,0:T(8,128)S(1)} %fusion), channel_id=1, source_target_pairs={{0,2},{2,0},{1,3},{3,1},{4,6},{6,4},{5,7},{7,5},{8,10},{10,8},{9,1... | collective-permute-start | bytes 7688 | tf_op jit(solution)/shard_map/ppermute | solution.py:301
  211.9 3.3 %all-to-all-start.10 = ((f32[4,4,128]{2,1,0:T(4,128)}), f32[4,4,128]{2,1,0:T(4,128)S(1)}, u32[]{:S(2)}, u32[]{:S(2)}) async-start(f32[4,4,128]{2,1,0:T(4,128)} %get-tuple-element.39), calls=%async_computation.10 | async-start | bytes 16384 | tf_op jit(solution)/shard_map/all_to_all | solution.py:297
  215.2 6.6 %collective-permute-done.5 = f32[5,128]{1,0:T(8,128)S(1)} collective-permute-done((f32[5,128]{1,0:T(8,128)S(1)}, f32[5,128]{1,0:T(8,128)S(1)}, u32[]{:S(2)}, u32[]{:S(2)}) %collective-permute-start.5) | collective-permute-done | bytes 2592 | tf_op jit(solution)/shard_map/ppermute | solution.py:301
  221.8 0.1 stack_reshape.6
  221.9 0.1 stack_reshape.7
  222.0 0.7 reshape.44
  222.7 0.0 all-to-all-done.10
  222.7 0.6 copy.15
  (15 shorter events, 0.2 us)
Async XLA Ops:
  3.9 26.1 %collective-permute-start = (bf16[4,80,128]{2,1,0:T(8,128)(2,1)}, bf16[4,80,128]{2,1,0:T(8,128)(2,1)S(1)}, u32[]{:S(2)}, u32[]{:S(2)}) collective-permute-start(bf16[4,80,128]{2,1,0:T(8,128)(2,1)} %get-tuple-element.22), channel_id=1, source_target_pairs={{0,2},{2,0},{1,3},{3,1},{4,6},{6,4},{5,7},{7,5},{8,10},{10,8},{9,1... | collective-permute-start | bytes 245768 | tf_op jit(solution)/shard_map/ppermute | solution.py:301
  20.2 19.6 %all-to-all-start = ((bf16[32,16,128]{2,1,0:T(8,128)(2,1)}), bf16[32,16,128]{2,1,0:T(8,128)(2,1)S(1)}, u32[]{:S(2)}, u32[]{:S(2)}) async-start(bf16[32,16,128]{2,1,0:T(8,128)(2,1)} %get-tuple-element.25), calls=%async_computation | async-start | bytes 262144 | tf_op jit(solution)/shard_map/all_to_all | solution.py:297
  30.0 0.9 copy-start
  31.0 4.1 %collective-permute-start.1 = (bf16[4,80,128]{2,1,0:T(8,128)(2,1)S(1)}, bf16[4,80,128]{2,1,0:T(8,128)(2,1)S(1)}, u32[]{:S(2)}, u32[]{:S(2)}) collective-permute-start(bf16[4,80,128]{2,1,0:T(8,128)(2,1)S(1)} %get-tuple-element.24), channel_id=1, source_target_pairs={{0,1},{1,0},{2,3},{3,2},{4,5},{5,4},{6,7},{7,6},{8,9},{9,8},{10,11... | collective-permute-start | bytes 245768 | tf_op jit(solution)/shard_map/ppermute | solution.py:301
  40.7 21.5 %all-to-all-start.1 = ((bf16[16,64,128]{2,1,0:T(8,128)(2,1)}), bf16[16,64,128]{2,1,0:T(8,128)(2,1)S(1)}, u32[]{:S(2)}, u32[]{:S(2)}) async-start(bf16[16,64,128]{2,1,0:T(8,128)(2,1)} %shard_map.71), calls=%async_computation.1 | async-start | bytes 524288 | tf_op jit(solution)/shard_map/all_to_all | solution.py:297
  46.7 9.4 %collective-permute-start.4 = (bf16[2,80,128]{2,1,0:T(8,128)(2,1)S(1)}, bf16[2,80,128]{2,1,0:T(8,128)(2,1)S(1)}, u32[]{:S(2)}, u32[]{:S(2)}) collective-permute-start(bf16[2,80,128]{2,1,0:T(8,128)(2,1)S(1)} %pad_maximum_fusion.2), channel_id=1, source_target_pairs={{0,12},{4,0},{8,4},{12,8},{1,13},{5,1},{9,5},{13,9},{2,14},{6,2},{... | collective-permute-start | bytes 122888 | tf_op jit(solution)/shard_map/ppermute | solution.py:319
  51.1 6.5 %collective-permute-start.3 = (bf16[2,80,128]{2,1,0:T(8,128)(2,1)S(1)}, bf16[2,80,128]{2,1,0:T(8,128)(2,1)S(1)}, u32[]{:S(2)}, u32[]{:S(2)}) collective-permute-start(bf16[2,80,128]{2,1,0:T(8,128)(2,1)S(1)} %pad_maximum_fusion.1), channel_id=1, source_target_pairs={{0,8},{4,12},{8,0},{12,4},{1,9},{5,13},{9,1},{13,5},{2,10},{6,14},... | collective-permute-start | bytes 122888 | tf_op jit(solution)/shard_map/ppermute | solution.py:319
  53.6 6.3 %collective-permute-start.2 = (bf16[2,80,128]{2,1,0:T(8,128)(2,1)S(1)}, bf16[2,80,128]{2,1,0:T(8,128)(2,1)S(1)}, u32[]{:S(2)}, u32[]{:S(2)}) collective-permute-start(bf16[2,80,128]{2,1,0:T(8,128)(2,1)S(1)} %pad_maximum_fusion), channel_id=1, source_target_pairs={{0,4},{4,8},{8,12},{12,0},{1,5},{5,9},{9,13},{13,1},{2,6},{6,10},{... | collective-permute-start | bytes 122888 | tf_op jit(solution)/shard_map/ppermute | solution.py:319
  59.8 0.7 copy-start.1
  62.2 23.0 %all-to-all-start.2 = ((bf16[32,80,128]{2,1,0:T(8,128)(2,1)}), bf16[32,80,128]{2,1,0:T(8,128)(2,1)S(1)}, u32[]{:S(2)}, u32[]{:S(2)}) async-start(bf16[32,80,128]{2,1,0:T(8,128)(2,1)} %shard_map.70), calls=%async_computation.2 | async-start | bytes 1310720 | tf_op jit(solution)/shard_map/all_to_all | solution.py:297
  195.3 13.3 %all-to-all-start.9 = ((f32[32,5,128]{2,1,0:T(8,128)}), f32[32,5,128]{2,1,0:T(8,128)S(1)}, u32[]{:S(2)}, u32[]{:S(2)}) async-start(f32[32,5,128]{2,1,0:T(8,128)} %get-tuple-element.38), calls=%async_computation.9 | async-start | bytes 262144 | tf_op jit(solution)/shard_map/all_to_all | solution.py:297
  208.7 13.1 %collective-permute-start.5 = (f32[5,128]{1,0:T(8,128)S(1)}, f32[5,128]{1,0:T(8,128)S(1)}, u32[]{:S(2)}, u32[]{:S(2)}) collective-permute-start(f32[5,128]{1,0:T(8,128)S(1)} %fusion), channel_id=1, source_target_pairs={{0,2},{2,0},{1,3},{3,1},{4,6},{6,4},{5,7},{7,5},{8,10},{10,8},{9,1... | collective-permute-start | bytes 7688 | tf_op jit(solution)/shard_map/ppermute | solution.py:301
  211.9 10.7 %all-to-all-start.10 = ((f32[4,4,128]{2,1,0:T(4,128)}), f32[4,4,128]{2,1,0:T(4,128)S(1)}, u32[]{:S(2)}, u32[]{:S(2)}) async-start(f32[4,4,128]{2,1,0:T(4,128)} %get-tuple-element.39), calls=%async_computation.10 | async-start | bytes 16384 | tf_op jit(solution)/shard_map/all_to_all | solution.py:297

commit v8 on v6

--- a/solution.py
+++ b/solution.py
@@ -166,14 +166,14 @@
 def values_call(goods_emb, buyer_emb, money_row):
     return pl.pallas_call(
         values_kernel,
-        grid=(NGOOD // 256,),
+        grid=(NGOOD // 512,),
         in_specs=[
-            pl.BlockSpec((256, E), lambda i: (i, 0)),
+            pl.BlockSpec((512, E), lambda i: (i, 0)),
             pl.BlockSpec((NBUY, E), lambda i: (0, 0)),
             pl.BlockSpec((1, 128), lambda i: (0, 0)),
         ],
         out_specs=[
-            pl.BlockSpec((256, NBUY), lambda i: (i, 0)),
+            pl.BlockSpec((512, NBUY), lambda i: (i, 0)),
             pl.BlockSpec((32, LB + 1, 128), lambda i: (0, 0, 0)),
         ],
         out_shape=[

time: 224 us -> 224 us (level)
  no operation moved by 1% of the time
where the time goes in v8:
time: 224 us; the launch traced here: 223 us
  blocking collectives  93.5 us (42%)
  starting transfers between devices  64.5 us (29%)
  waiting for transfers between devices  36.2 us (16%)
  Pallas kernels  21.4 us (10%)
  local copies, waits for them, and re-layouts  6.15 us (3%)
    all_to_all x6, blocking collectives, exchange(): return lax.all_to_all(x, axes, 0, 0, tiled=True)  93.5 us
    all_to_all x5, starting transfers between devices, exchange(): return lax.all_to_all(x, axes, 0, 0, tiled=True)  32.6 us
    all_to_all x5, waiting for transfers between devices, exchange(): return lax.all_to_all(x, axes, 0, 0, tiled=True)  25.1 us
    ppermute x3, starting transfers between devices, swap(): return lax.ppermute(x, axis, [(0, 1), (1, 0)])  22.6 us
    ppermute x3, starting transfers between devices, embeddings(): two = lax.ppermute(two, 'x', [(i, (i + d) % 4) for i in range(4)])  9.33 us
    ppermute x3, waiting for transfers between devices, swap(): return lax.ppermute(x, axis, [(0, 1), (1, 0)])  7.47 us
    pallas_call x3, Pallas kernels, utility_call(): pl.pallas_call(functools.partial(utility_kernel, k), in_specs=specs, out_...  6.84 us
    pallas_call x1, Pallas kernels, values_call(): pl.pallas_call(values_kernel, grid=(NGOOD // 512,), in_specs=[pl.BlockSpe...  6.05 us
  transfers between devices with their start and end apart: 11, of which 7 were waited for; matrix products, arithmetic and copies ran while one was open for 2% of the time, Pallas kernels for 1%

profile of v8, /device:TPU:1, one launch (start us, length us, event | category | flops | bytes accessed | tf_op | source)
XLA Modules:
  0.0 223.0 jit_solution(11121966726484147963)
XLA Ops:
  0.6 0.1 pad_add_fusion.place_ref
  0.7 0.0 copy-start
  0.7 0.9 copy-done
  1.6 0.0 copy-start.1
  1.6 0.9 copy-done.1
  2.5 2.1 shard_map.68
  4.6 16.2 %collective-permute-start = (bf16[4,80,128]{2,1,0:T(8,128)(2,1)S(1)}, bf16[4,80,128]{2,1,0:T(8,128)(2,1)S(1)}, u32[]{:S(2)}, u32[]{:S(2)}) collective-permute-start(bf16[4,80,128]{2,1,0:T(8,128)(2,1)S(1)} %get-tuple-element.22), channel_id=1, source_target_pairs={{0,2},{2,0},{1,3},{3,1},{4,6},{6,4},{5,7},{7,5},{8,10},{10,8},{9,1... | collective-permute-start | bytes 245768 | tf_op jit(solution)/shard_map/ppermute | solution.py:296
  20.9 7.8 %all-to-all-start = ((bf16[32,16,128]{2,1,0:T(8,128)(2,1)}), bf16[32,16,128]{2,1,0:T(8,128)(2,1)S(1)}, u32[]{:S(2)}, u32[]{:S(2)}) async-start(bf16[32,16,128]{2,1,0:T(8,128)(2,1)} %get-tuple-element.25), calls=%async_computation | async-start | bytes 262144 | tf_op jit(solution)/shard_map/all_to_all | solution.py:292
  28.7 1.0 copy.10
  29.6 0.1 reverse_select_fusion
  29.7 1.0 copy.13
  30.7 0.0 collective-permute-done.came_ref
  30.7 0.1 shard_map.69
  30.8 3.1 %collective-permute-start.1 = (bf16[4,80,128]{2,1,0:T(8,128)(2,1)S(1)}, bf16[4,80,128]{2,1,0:T(8,128)(2,1)S(1)}, u32[]{:S(2)}, u32[]{:S(2)}) collective-permute-start(bf16[4,80,128]{2,1,0:T(8,128)(2,1)S(1)} %get-tuple-element.24), channel_id=1, source_target_pairs={{0,1},{1,0},{2,3},{3,2},{4,5},{5,4},{6,7},{7,6},{8,9},{9,8},{10,11... | collective-permute-start | bytes 245768 | tf_op jit(solution)/shard_map/ppermute | solution.py:296
  34.0 0.9 collective-permute-done.1
  34.9 5.6 %all-to-all-done.got_ref = bf16[32,16,128]{2,1,0:T(8,128)(2,1)S(1)} async-done(((bf16[32,16,128]{2,1,0:T(8,128)(2,1)}), bf16[32,16,128]{2,1,0:T(8,128)(2,1)S(1)}, u32[]{:S(2)}, u32[]{:S(2)}) %all-to-all-start) | async-done | bytes 131104 | tf_op jit(solution)/shard_map/all_to_all | solution.py:292
  40.4 1.0 shard_map.71
  41.4 6.0 %all-to-all-start.1 = ((bf16[16,64,128]{2,1,0:T(8,128)(2,1)}), bf16[16,64,128]{2,1,0:T(8,128)(2,1)S(1)}, u32[]{:S(2)}, u32[]{:S(2)}) async-start(bf16[16,64,128]{2,1,0:T(8,128)(2,1)} %shard_map.71), calls=%async_computation.1 | async-start | bytes 524288 | tf_op jit(solution)/shard_map/all_to_all | solution.py:292
  47.4 4.4 %collective-permute-start.4 = (bf16[2,80,128]{2,1,0:T(8,128)(2,1)S(1)}, bf16[2,80,128]{2,1,0:T(8,128)(2,1)S(1)}, u32[]{:S(2)}, u32[]{:S(2)}) collective-permute-start(bf16[2,80,128]{2,1,0:T(8,128)(2,1)S(1)} %pad_maximum_fusion.2), channel_id=1, source_target_pairs={{0,12},{4,0},{8,4},{12,8},{1,13},{5,1},{9,5},{13,9},{2,14},{6,2},{... | collective-permute-start | bytes 122888 | tf_op jit(solution)/shard_map/ppermute | solution.py:310
  51.8 2.4 %collective-permute-start.3 = (bf16[2,80,128]{2,1,0:T(8,128)(2,1)S(1)}, bf16[2,80,128]{2,1,0:T(8,128)(2,1)S(1)}, u32[]{:S(2)}, u32[]{:S(2)}) collective-permute-start(bf16[2,80,128]{2,1,0:T(8,128)(2,1)S(1)} %pad_maximum_fusion.1), channel_id=1, source_target_pairs={{0,8},{4,12},{8,0},{12,4},{1,9},{5,13},{9,1},{13,5},{2,10},{6,14},... | collective-permute-start | bytes 122888 | tf_op jit(solution)/shard_map/ppermute | solution.py:310
  54.3 2.5 %collective-permute-start.2 = (bf16[2,80,128]{2,1,0:T(8,128)(2,1)S(1)}, bf16[2,80,128]{2,1,0:T(8,128)(2,1)S(1)}, u32[]{:S(2)}, u32[]{:S(2)}) collective-permute-start(bf16[2,80,128]{2,1,0:T(8,128)(2,1)S(1)} %pad_maximum_fusion), channel_id=1, source_target_pairs={{0,4},{4,8},{8,12},{12,0},{1,5},{5,9},{9,13},{13,1},{2,6},{6,10},{... | collective-permute-start | bytes 122888 | tf_op jit(solution)/shard_map/ppermute | solution.py:310
  56.8 0.0 collective-permute-done.4
  56.8 1.5 collective-permute-done.3
  58.4 2.2 collective-permute-done.2
  60.5 1.7 shard_map.70
  62.2 0.0 all-to-all-done.1
  62.2 9.9 %all-to-all-start.2 = ((bf16[32,80,128]{2,1,0:T(8,128)(2,1)}), bf16[32,80,128]{2,1,0:T(8,128)(2,1)S(1)}, u32[]{:S(2)}, u32[]{:S(2)}) async-start(bf16[32,80,128]{2,1,0:T(8,128)(2,1)} %shard_map.70), calls=%async_computation.2 | async-start | bytes 1310720 | tf_op jit(solution)/shard_map/all_to_all | solution.py:292
  72.1 0.8 reshape.41
  72.9 0.1 reshape.42
  73.0 11.9 %all-to-all-done.2 = bf16[32,80,128]{2,1,0:T(8,128)(2,1)S(1)} async-done(((bf16[32,80,128]{2,1,0:T(8,128)(2,1)}), bf16[32,80,128]{2,1,0:T(8,128)(2,1)S(1)}, u32[]{:S(2)}, u32[]{:S(2)}) %all-to-all-start.2) | async-done | bytes 655392 | tf_op jit(solution)/shard_map/all_to_all | solution.py:292
  85.0 6.0 %shard_map.72 = (bf16[1024,2560]{1,0:T(8,128)(2,1)S(1)}, f32[32,21,128]{2,1,0:T(8,128)S(1)}) custom-call(bf16[1024,128]{1,0:T(8,128)(2,1)S(1)} %bitcast.43, bf16[2560,128]{1,0:T(8,128)(2,1)S(1)} %bitcast.42, f32[1,128]{1,0:T(1,128)S(1)} %constant_dynamic-slice_fusion.money_ref), custom_call_target="tpu_custom_call" | custom-call | tf_op jit(solution)/shard_map/pallas_call | solution.py:167
  91.0 13.8 %all_to_all.55.got_ref = f32[32,21,128]{2,1,0:T(8,128)S(1)} all-to-all(f32[32,21,128]{2,1,0:T(8,128)S(1)} %get-tuple-element.28), channel_id=1, replica_groups=mesh['y'=4,'zl'=8,'x'=4,'zh'=2,'c'=2] {'y','x','c'}, dimensions={0} | all-to-all | bytes 688128 | tf_op jit(solution)/shard_map/all_to_all | solution.py:292
  104.8 1.5 shard_map.73
  106.3 21.7 %all_to_all.56.got_ref = f32[16,8,128]{2,1,0:T(8,128)S(1)} all-to-all(f32[16,8,128]{2,1,0:T(8,128)S(1)} %get-tuple-element.30), channel_id=1, replica_groups=mesh['y'=4,'zl'=8,'x'=4,'zh'=2,'c'=2] {'zh','zl'}, dimensions={0} | all-to-all | bytes 131072 | tf_op jit(solution)/shard_map/all_to_all | solution.py:292
  127.9 2.6 %shard_map.74 = (f32[32,4,640]{2,1,0:T(4,128)S(1)}, f32[8,128]{1,0:T(8,128)}, f32[1024,2560]{1,0:T(8,128)S(1)}) custom-call(f32[16,8,128]{2,1,0:T(8,128)S(1)} %all_to_all.56.got_ref, bf16[1024,2560]{1,0:T(8,128)(2,1)S(1)} %get-tuple-element.29.refs_0_), custom_call_target="tpu_custom_call" | custom-call | tf_op jit(solution)/shard_map/pallas_call | solution.py:207
  130.5 14.8 %all_to_all.57.got_ref = f32[32,4,640]{2,1,0:T(4,128)S(1)} all-to-all(f32[32,4,640]{2,1,0:T(4,128)S(1)} %get-tuple-element.31), channel_id=1, replica_groups=mesh['y'=4,'zl'=8,'x'=4,'zh'=2,'c'=2] {'y','x','c'}, dimensions={0} | all-to-all | bytes 655360 | tf_op jit(solution)/shard_map/all_to_all | solution.py:292
  145.3 1.1 shard_map.75
  146.4 14.3 %all_to_all.58.got_ref = f32[16,8,128]{2,1,0:T(8,128)S(1)} all-to-all(f32[16,8,128]{2,1,0:T(8,128)S(1)} %shard_map.75), channel_id=1, replica_groups=mesh['y'=4,'zl'=8,'x'=4,'zh'=2,'c'=2] {'zh','zl'}, dimensions={0} | all-to-all | bytes 131072 | tf_op jit(solution)/shard_map/all_to_all | solution.py:292
  160.7 2.1 shard_map.76
  162.8 14.7 %all_to_all.59.got_ref = f32[32,4,640]{2,1,0:T(4,128)S(1)} all-to-all(f32[32,4,640]{2,1,0:T(4,128)S(1)} %get-tuple-element.34), channel_id=1, replica_groups=mesh['y'=4,'zl'=8,'x'=4,'zh'=2,'c'=2] {'y','x','c'}, dimensions={0} | all-to-all | bytes 655360 | tf_op jit(solution)/shard_map/all_to_all | solution.py:292
  177.5 1.1 shard_map.77
  178.6 14.3 %all_to_all.60.got_ref = f32[16,8,128]{2,1,0:T(8,128)S(1)} all-to-all(f32[16,8,128]{2,1,0:T(8,128)S(1)} %shard_map.77), channel_id=1, replica_groups=mesh['y'=4,'zl'=8,'x'=4,'zh'=2,'c'=2] {'zh','zl'}, dimensions={0} | all-to-all | bytes 131072 | tf_op jit(solution)/shard_map/all_to_all | solution.py:292
  192.9 2.2 shard_map.78
  195.1 5.6 %all-to-all-start.9 = ((f32[32,5,128]{2,1,0:T(8,128)}), f32[32,5,128]{2,1,0:T(8,128)S(1)}, u32[]{:S(2)}, u32[]{:S(2)}) async-start(f32[32,5,128]{2,1,0:T(8,128)} %get-tuple-element.38), calls=%async_computation.9 | async-start | bytes 262144 | tf_op jit(solution)/shard_map/all_to_all | solution.py:292
  200.8 0.1 dynamic-slice_reduce_fusion
  200.9 7.6 %all-to-all-done.9 = f32[32,5,128]{2,1,0:T(8,128)S(1)} async-done(((f32[32,5,128]{2,1,0:T(8,128)}), f32[32,5,128]{2,1,0:T(8,128)S(1)}, u32[]{:S(2)}, u32[]{:S(2)}) %all-to-all-start.9) | async-done | bytes 81952 | tf_op jit(solution)/shard_map/all_to_all | solution.py:292
  208.5 3.2 %collective-permute-start.5 = (f32[5,128]{1,0:T(8,128)S(1)}, f32[5,128]{1,0:T(8,128)S(1)}, u32[]{:S(2)}, u32[]{:S(2)}) collective-permute-start(f32[5,128]{1,0:T(8,128)S(1)} %fusion), channel_id=1, source_target_pairs={{0,2},{2,0},{1,3},{3,1},{4,6},{6,4},{5,7},{7,5},{8,10},{10,8},{9,1... | collective-permute-start | bytes 7688 | tf_op jit(solution)/shard_map/ppermute | solution.py:296
  211.7 3.3 %all-to-all-start.10 = ((f32[4,4,128]{2,1,0:T(4,128)}), f32[4,4,128]{2,1,0:T(4,128)S(1)}, u32[]{:S(2)}, u32[]{:S(2)}) async-start(f32[4,4,128]{2,1,0:T(4,128)} %get-tuple-element.39), calls=%async_computation.10 | async-start | bytes 16384 | tf_op jit(solution)/shard_map/all_to_all | solution.py:292
  215.0 6.6 %collective-permute-done.5 = f32[5,128]{1,0:T(8,128)S(1)} collective-permute-done((f32[5,128]{1,0:T(8,128)S(1)}, f32[5,128]{1,0:T(8,128)S(1)}, u32[]{:S(2)}, u32[]{:S(2)}) %collective-permute-start.5) | collective-permute-done | bytes 2592 | tf_op jit(solution)/shard_map/ppermute | solution.py:296
  221.6 0.1 stack_reshape.6
  221.6 0.1 stack_reshape.7
  221.7 0.7 reshape.44
  222.4 0.0 all-to-all-done.10
  222.4 0.6 copy.15
  (15 shorter events, 0.2 us)
Async XLA Ops:
  0.7 0.9 copy-start
  1.6 0.9 copy-start.1
  4.6 26.1 %collective-permute-start = (bf16[4,80,128]{2,1,0:T(8,128)(2,1)S(1)}, bf16[4,80,128]{2,1,0:T(8,128)(2,1)S(1)}, u32[]{:S(2)}, u32[]{:S(2)}) collective-permute-start(bf16[4,80,128]{2,1,0:T(8,128)(2,1)S(1)} %get-tuple-element.22), channel_id=1, source_target_pairs={{0,2},{2,0},{1,3},{3,1},{4,6},{6,4},{5,7},{7,5},{8,10},{10,8},{9,1... | collective-permute-start | bytes 245768 | tf_op jit(solution)/shard_map/ppermute | solution.py:296
  20.9 19.6 %all-to-all-start = ((bf16[32,16,128]{2,1,0:T(8,128)(2,1)}), bf16[32,16,128]{2,1,0:T(8,128)(2,1)S(1)}, u32[]{:S(2)}, u32[]{:S(2)}) async-start(bf16[32,16,128]{2,1,0:T(8,128)(2,1)} %get-tuple-element.25), calls=%async_computation | async-start | bytes 262144 | tf_op jit(solution)/shard_map/all_to_all | solution.py:292
  30.8 4.1 %collective-permute-start.1 = (bf16[4,80,128]{2,1,0:T(8,128)(2,1)S(1)}, bf16[4,80,128]{2,1,0:T(8,128)(2,1)S(1)}, u32[]{:S(2)}, u32[]{:S(2)}) collective-permute-start(bf16[4,80,128]{2,1,0:T(8,128)(2,1)S(1)} %get-tuple-element.24), channel_id=1, source_target_pairs={{0,1},{1,0},{2,3},{3,2},{4,5},{5,4},{6,7},{7,6},{8,9},{9,8},{10,11... | collective-permute-start | bytes 245768 | tf_op jit(solution)/shard_map/ppermute | solution.py:296
  41.4 20.8 %all-to-all-start.1 = ((bf16[16,64,128]{2,1,0:T(8,128)(2,1)}), bf16[16,64,128]{2,1,0:T(8,128)(2,1)S(1)}, u32[]{:S(2)}, u32[]{:S(2)}) async-start(bf16[16,64,128]{2,1,0:T(8,128)(2,1)} %shard_map.71), calls=%async_computation.1 | async-start | bytes 524288 | tf_op jit(solution)/shard_map/all_to_all | solution.py:292
  47.4 9.4 %collective-permute-start.4 = (bf16[2,80,128]{2,1,0:T(8,128)(2,1)S(1)}, bf16[2,80,128]{2,1,0:T(8,128)(2,1)S(1)}, u32[]{:S(2)}, u32[]{:S(2)}) collective-permute-start(bf16[2,80,128]{2,1,0:T(8,128)(2,1)S(1)} %pad_maximum_fusion.2), channel_id=1, source_target_pairs={{0,12},{4,0},{8,4},{12,8},{1,13},{5,1},{9,5},{13,9},{2,14},{6,2},{... | collective-permute-start | bytes 122888 | tf_op jit(solution)/shard_map/ppermute | solution.py:310
  51.8 6.5 %collective-permute-start.3 = (bf16[2,80,128]{2,1,0:T(8,128)(2,1)S(1)}, bf16[2,80,128]{2,1,0:T(8,128)(2,1)S(1)}, u32[]{:S(2)}, u32[]{:S(2)}) collective-permute-start(bf16[2,80,128]{2,1,0:T(8,128)(2,1)S(1)} %pad_maximum_fusion.1), channel_id=1, source_target_pairs={{0,8},{4,12},{8,0},{12,4},{1,9},{5,13},{9,1},{13,5},{2,10},{6,14},... | collective-permute-start | bytes 122888 | tf_op jit(solution)/shard_map/ppermute | solution.py:310
  54.3 6.3 %collective-permute-start.2 = (bf16[2,80,128]{2,1,0:T(8,128)(2,1)S(1)}, bf16[2,80,128]{2,1,0:T(8,128)(2,1)S(1)}, u32[]{:S(2)}, u32[]{:S(2)}) collective-permute-start(bf16[2,80,128]{2,1,0:T(8,128)(2,1)S(1)} %pad_maximum_fusion), channel_id=1, source_target_pairs={{0,4},{4,8},{8,12},{12,0},{1,5},{5,9},{9,13},{13,1},{2,6},{6,10},{... | collective-permute-start | bytes 122888 | tf_op jit(solution)/shard_map/ppermute | solution.py:310
  62.2 22.8 %all-to-all-start.2 = ((bf16[32,80,128]{2,1,0:T(8,128)(2,1)}), bf16[32,80,128]{2,1,0:T(8,128)(2,1)S(1)}, u32[]{:S(2)}, u32[]{:S(2)}) async-start(bf16[32,80,128]{2,1,0:T(8,128)(2,1)} %shard_map.70), calls=%async_computation.2 | async-start | bytes 1310720 | tf_op jit(solution)/shard_map/all_to_all | solution.py:292
  195.1 13.4 %all-to-all-start.9 = ((f32[32,5,128]{2,1,0:T(8,128)}), f32[32,5,128]{2,1,0:T(8,128)S(1)}, u32[]{:S(2)}, u32[]{:S(2)}) async-start(f32[32,5,128]{2,1,0:T(8,128)} %get-tuple-element.38), calls=%async_computation.9 | async-start | bytes 262144 | tf_op jit(solution)/shard_map/all_to_all | solution.py:292
  208.5 13.1 %collective-permute-start.5 = (f32[5,128]{1,0:T(8,128)S(1)}, f32[5,128]{1,0:T(8,128)S(1)}, u32[]{:S(2)}, u32[]{:S(2)}) collective-permute-start(f32[5,128]{1,0:T(8,128)S(1)} %fusion), channel_id=1, source_target_pairs={{0,2},{2,0},{1,3},{3,1},{4,6},{6,4},{5,7},{7,5},{8,10},{10,8},{9,1... | collective-permute-start | bytes 7688 | tf_op jit(solution)/shard_map/ppermute | solution.py:296
  211.7 10.7 %all-to-all-start.10 = ((f32[4,4,128]{2,1,0:T(4,128)}), f32[4,4,128]{2,1,0:T(4,128)S(1)}, u32[]{:S(2)}, u32[]{:S(2)}) async-start(f32[4,4,128]{2,1,0:T(4,128)} %get-tuple-element.39), calls=%async_computation.10 | async-start | bytes 16384 | tf_op jit(solution)/shard_map/all_to_all | solution.py:292
